TPU v7x, 32 devices: a whole 2x2x4 slice. The times are simulated.
32 devices in a mesh: branch: 2 (over core), dp: 16 (over z, y, x).
Axes of the slice: x: 2, y: 2, z: 4, core: 2. Of those that a mesh axis runs over, the one named last changes fastest.
Arguments:
- small_tokens: bfloat16 [2, 128, 145, 192], P('branch', 'dp'), may hold values from -6 to 6
- large_tokens: bfloat16 [2, 128, 197, 384], P('branch', 'dp'), may hold values from -6 to 6
- small_cot: bfloat16 [2, 128, 145, 192], P('branch', 'dp'), may hold values from -6 to 6
- large_cot: bfloat16 [2, 128, 197, 384], P('branch', 'dp'), may hold values from -6 to 6
- live_counts: int32 [2, 16], P(None, 'dp'), may hold values from 1 to 8, as said below
- master: float32 [3257856], P(('branch', 'dp'))
- first_moment: float32 [3257856], P(('branch', 'dp')), may hold values from -0.0034179688 to 0.0034179688
- second_moment: float32 [3257856], P(('branch', 'dp')), may hold values from 3.0695034e-07 to 1.2278014e-06
Outputs:
- small_out: bfloat16 [2, 128, 145, 192], P('branch', 'dp')
- large_out: bfloat16 [2, 128, 197, 384], P('branch', 'dp')
- small_grad: bfloat16 [2, 128, 145, 192], P('branch', 'dp')
- large_grad: bfloat16 [2, 128, 197, 384], P('branch', 'dp')
- grad_norm: float32 [], replicated
- new_first: float32 [3257856], P(('branch', 'dp'))
- new_second: float32 [3257856], P(('branch', 'dp'))
- new_master: float32 [3257856], P(('branch', 'dp'))
- new_master16: bfloat16 [3257856], P(('branch', 'dp'))
Inputs may be any that keep to these rules, and one draw needn't show every extreme that they name: `live_counts`: 8 is reached in every draw.
All inputs are finite; a program needn't handle non-finite values.
Results may differ from a plain program's by a relative error of at most 0.014.
The roundings to bfloat16 on the way count: a program that leaves them out, or rounds other values in their place, can miss the bound.
Values may be sent and summed in bfloat16 or wider, within the bound.
No kernel may reach another device: no remote copies, remote signals or barrier semaphores. Data moves between devices by JAX's collectives and lax.ppermute only.
A program may use at most 192 MiB of HBM per device.

v0:
```python
import functools
import math

import jax
import jax.numpy as jnp
import numpy as np
from jax import lax
from jax.experimental import pallas as pl
from jax.experimental.pallas import tpu as pltpu
from jax.experimental.layout import Layout, with_layout_constraint
from jax.sharding import PartitionSpec as P

DS = 192
DL = 384
MS = 768
ML = 1536
HEADS = 6

norm_eps = 1e-06
clip_norm = 1.0
beta_one = 0.5
beta_two = 0.5
adam_eps = 1e-08
rate = 0.05
decay = 0.05
bias_one = 1.0 - 0.5**5
bias_two = 1.0 - 0.5**5

f32 = jnp.float32
bf16 = jnp.bfloat16
LANES = 128


def layout():
    shapes = []
    for label, width, hidden in (("s", DS, MS), ("l", DL, ML)):
        shapes += [
            (label + "_ln1", (2, width)),
            (label + "_qkv_w", (width, 3 * width)),
            (label + "_qkv_b", (3 * width,)),
            (label + "_proj_w", (width, width)),
            (label + "_proj_b", (width,)),
            (label + "_ln2", (2, width)),
            (label + "_fc1_w", (width, hidden)),
            (label + "_fc1_b", (hidden,)),
            (label + "_fc2_w", (hidden, width)),
            (label + "_fc2_b", (width,)),
        ]
    for label, owner, other in (("s", DS, DL), ("l", DL, DS)):
        shapes += [
            (label + "_to_ln", (2, owner)),
            (label + "_to_w", (owner, other)),
            (label + "_to_b", (other,)),
            (label + "_ca_ln", (2, other)),
            (label + "_ca_q_w", (other, other)),
            (label + "_ca_q_b", (other,)),
            (label + "_ca_k_w", (other, other)),
            (label + "_ca_v_w", (other, other)),
            (label + "_ca_v_b", (other,)),
            (label + "_ca_o_w", (other, other)),
            (label + "_ca_o_b", (other,)),
            (label + "_back_ln", (2, other)),
            (label + "_back_w", (other, owner)),
            (label + "_back_b", (owner,)),
        ]
    return shapes


def round_up(value, unit):
    return -(-value // unit) * unit


def grid_plan(shards):
    names = []
    regions = []
    offset = 0
    for label, shape in layout():
        count = math.prod(shape)
        phase = offset % LANES
        if not regions or regions[-1][2] != phase:
            regions.append([offset, offset, phase])
        names.append((label, shape, offset, len(regions) - 1))
        offset += count
        regions[-1][1] = offset
    total = offset
    starts = []
    row = 0
    for first, last, phase in regions:
        starts.append(row)
        row += -(-(last - first) // LANES)
    rows = row
    places = {}
    for label, shape, place, region in names:
        places[label] = (starts[region] + (place - regions[region][0]) // LANES, shape)
    size = total // shards
    bases = []
    pieces = []
    for device in range(shards):
        low, high = device * size, (device + 1) * size
        own = []
        base = None
        for (first, last, phase), start in zip(regions, starts):
            left, right = max(low, first), min(high, last)
            if left >= right:
                continue
            if base is None:
                base = (start + (left - first) // LANES) // 16 * 16
            delta = start * LANES - first + low - base * LANES
            own.append((left - low, right - low, delta))
        bases.append(base)
        pieces.append(own)
    most = max(len(own) for own in pieces)
    table = np.zeros((shards, most * 3), np.int32)
    need = 0
    for device, own in enumerate(pieces):
        for number, (left, right, delta) in enumerate(own):
            table[device, 3 * number : 3 * number + 3] = (left, right, delta)
            need = max(need, right + delta)
    span = round_up(-(-need // LANES), 32)
    overlap = 16
    for device in range(1, shards):
        overlap = max(overlap, bases[device - 1] + span - bases[device])
    half = shards // 2
    edge = half * size
    sides = [[], []]
    for label, shape, place, region in names:
        if place < edge:
            sides[0].append((label, shape))
        if place + math.prod(shape) > edge:
            sides[1].append((label, shape))
    origins = [0, min(bases[half], places[sides[1][0][0]][0]) // 16 * 16]
    heights = []
    for side in range(2):
        last = bases[half * (side + 1) - 1] + span
        for label, shape in sides[side]:
            last = max(last, places[label][0] + -(-math.prod(shape) // LANES))
        heights.append(round_up(last - origins[side] + overlap, 16))
    groups = []
    for first, last in ((0, half // 2), (half // 2, half), (half, shards)):
        held = [
            (label, shape)
            for label, shape, place, region in names
            if place < last * size and place + math.prod(shape) > first * size
        ]
        origin = min([bases[first]] + [places[label][0] for label, shape in held]) // 16 * 16
        stop = max(
            [bases[last - 1] + span]
            + [places[label][0] + -(-math.prod(shape) // LANES) for label, shape in held]
        )
        groups.append((first, last - first, held, origin, round_up(stop - origin + overlap, 16)))
    return dict(
        places=places,
        groups=groups,
        rows=rows,
        half=half,
        sides=sides,
        origins=origins,
        heights=heights,
        size=size,
        bases=bases,
        table=table,
        most=most,
        span=span,
        overlap=overlap,
        shard_rows=round_up(-(-size // LANES), 16),
    )


def mm(left, right):
    return lax.dot_general(left, right, (((1,), (0,)), ((), ())), preferred_element_type=f32)


def mm_t(left, right):
    return lax.dot_general(left, right, (((1,), (1,)), ((), ())), preferred_element_type=f32)


def t_mm(left, right):
    return lax.dot_general(left, right, (((0,), (0,)), ((), ())), preferred_element_type=f32)


def vmem_spec(shape, index):
    return pl.BlockSpec(shape, index)


def whole(shape):
    rank = len(shape)
    return pl.BlockSpec(shape, lambda *_: (0,) * rank, pipeline_mode=pl.Buffered(1))


def estimate(flops, moved):
    return pl.CostEstimate(flops=int(flops), bytes_accessed=int(moved), transcendentals=0)


def shift_rows(ref, amount, rows, margin):
    down = amount // LANES
    across = amount - down * LANES
    here = ref[pl.ds(margin - down, rows), :]
    above = ref[pl.ds(margin - down - 1, rows), :]
    here = pltpu.roll(here, across, 1)
    above = pltpu.roll(above, across, 1)
    lane = lax.broadcasted_iota(jnp.int32, here.shape, 1)
    return jnp.where(lane < across, above, here)


def align_kernel(most, rows, span, margin, core_ref, table_ref, shard_ref, keep_ref, send_ref, padded):
    padded[...] = jnp.zeros_like(padded)
    padded[margin : margin + rows, :] = shard_ref[...]
    place = lax.broadcasted_iota(jnp.int32, (span, LANES), 0) * LANES
    place = place + lax.broadcasted_iota(jnp.int32, (span, LANES), 1)
    total = jnp.zeros((span, LANES), f32)
    for number in range(most):
        left = table_ref[3 * number]
        right = table_ref[3 * number + 1]
        delta = table_ref[3 * number + 2]
        moved = shift_rows(padded, delta, span, margin)
        total = jnp.where((place >= left + delta) & (place < right + delta), moved, total)
    total = total.astype(bf16)
    first = core_ref[0] == 0
    upper, lower = total[: span // 2], total[span // 2 :]
    keep_ref[...] = jnp.where(first, upper, lower)
    send_ref[...] = jnp.where(first, lower, upper)


def unalign_kernel(
    most, rows, span, margin, core_ref, table_ref, own_ref, got_ref, out_ref, norm_ref, padded
):
    first = core_ref[0] == 0
    padded[span:, :] = jnp.zeros((padded.shape[0] - span, LANES), f32)
    padded[0 : span // 2, :] = jnp.where(first, own_ref[...], got_ref[...])
    padded[span // 2 : span, :] = jnp.where(first, got_ref[...], own_ref[...])
    place = lax.broadcasted_iota(jnp.int32, (rows, LANES), 0) * LANES
    place = place + lax.broadcasted_iota(jnp.int32, (rows, LANES), 1)
    total = jnp.zeros((rows, LANES), f32)
    lane = lax.broadcasted_iota(jnp.int32, (rows, LANES), 1)
    for number in range(most):
        left = table_ref[3 * number]
        right = table_ref[3 * number + 1]
        delta = table_ref[3 * number + 2]
        down = delta // LANES
        across = delta - down * LANES
        back = lax.rem(LANES - across, LANES)
        here = pltpu.roll(padded[pl.ds(down, rows), :], back, 1)
        below = pltpu.roll(padded[pl.ds(down + 1, rows), :], back, 1)
        moved = jnp.where(lane < LANES - across, here, below)
        total = jnp.where((place >= left) & (place < right), moved, total)
    out_ref[...] = total
    norm_ref[...] = jnp.broadcast_to(jnp.sum(total * total).reshape(1, 1), (8, LANES))


def align(core, table, shard, plan):
    rows, span, most = plan["shard_rows"], plan["span"], plan["most"]
    margin = 8 + round_up(int(plan["table"].max(initial=0, where=pick_delta(plan))) // LANES + 1, 8)
    tall = margin + max(rows, span) + 8
    vmem = pl.BlockSpec(memory_space=pltpu.VMEM)
    smem = pl.BlockSpec(memory_space=pltpu.SMEM)
    part = jax.ShapeDtypeStruct((span // 2, LANES), bf16)
    return pl.pallas_call(
        functools.partial(align_kernel, most, rows, span, margin),
        out_shape=(part, part),
        in_specs=[smem, smem, vmem],
        out_specs=(vmem, vmem),
        scratch_shapes=[pltpu.VMEM((tall, LANES), f32)],
        cost_estimate=estimate(1_000_000, 1_000_000),
        name="align",
    )(core, table, shard)


def unalign(core, table, own, got, plan):
    rows, span, most = plan["shard_rows"], plan["span"], plan["most"]
    margin = 16 + round_up(int(plan["table"].max(initial=0, where=pick_delta(plan))) // LANES + 1, 8)
    tall = max(rows, span) + margin
    vmem = pl.BlockSpec(memory_space=pltpu.VMEM)
    smem = pl.BlockSpec(memory_space=pltpu.SMEM)
    return pl.pallas_call(
        functools.partial(unalign_kernel, most, rows, span, margin),
        out_shape=(
            jax.ShapeDtypeStruct((rows, LANES), f32),
            jax.ShapeDtypeStruct((8, LANES), f32),
        ),
        in_specs=[smem, smem, vmem, vmem],
        out_specs=(vmem, vmem),
        scratch_shapes=[pltpu.VMEM((tall, LANES), f32)],
        cost_estimate=estimate(1_000_000, 1_000_000),
        name="unalign",
    )(core, table, own, got)


def pick_delta(plan):
    mask = np.zeros(plan["table"].shape, bool)
    mask[:, 2::3] = True
    return mask


def two_dim(shape):
    return shape if len(shape) == 2 else (1, shape[0])


def is_matrix(label):
    return label[-2:] == "_w"


def strided(start, count, step):
    return pl.ds(start, count) if step == 1 or count == 1 else pl.ds(start, count, stride=step)


def half_swap(value):
    return pltpu.roll(value, LANES // 2, 1)


def read_param(flat, row, shape, out_ref, pair_ref):
    depth, width = two_dim(shape)
    dtype = out_ref.dtype
    if width % LANES == 0:
        step = width // LANES
        for col in range(step):
            out_ref[:, col * LANES : (col + 1) * LANES] = flat[
                strided(row + col, depth, step), :
            ].astype(dtype)
        return
    half = LANES // 2
    lead = width // LANES
    if depth == 1:
        for col in range(lead):
            out_ref[:, col * LANES : (col + 1) * LANES] = flat[row + col : row + col + 1, :].astype(
                dtype
            )
        out_ref[:, lead * LANES :] = flat[row + lead : row + lead + 1, 0:half].astype(dtype)
        return
    step = 2 * width // LANES
    pairs = depth // 2
    lane = lax.broadcasted_iota(jnp.int32, (pairs, LANES), 1)
    blocks = [flat[strided(row + col, pairs, step), :] for col in range(step)]
    turned = [half_swap(block) for block in blocks[lead:]]
    for col in range(lead):
        pair_ref[col, strided(0, pairs, 2), :] = blocks[col]
        pair_ref[col, strided(1, pairs, 2), :] = jnp.where(lane < half, turned[col], turned[col + 1])
    pair_ref[lead, strided(0, pairs, 2), :] = blocks[lead]
    pair_ref[lead, strided(1, pairs, 2), :] = turned[lead]
    for col in range(lead):
        out_ref[:, col * LANES : (col + 1) * LANES] = pair_ref[col, 0:depth, :].astype(dtype)
    out_ref[:, lead * LANES :] = pair_ref[lead, 0:depth, 0:half].astype(dtype)


def write_param(flat, row, shape, in_ref, pair_ref, window):
    depth, width = two_dim(shape)
    if width % LANES == 0:
        step = width // LANES
        first = max(0, (window[0] - row) // step) // 8 * 8
        last = min(depth, round_up(max(0, -(-(window[1] - row) // step)), 8))
        for col in range(step):
            flat[strided(row + first * step + col, last - first, step), :] = in_ref[
                first:last, col * LANES : (col + 1) * LANES
            ]
        return
    half = LANES // 2
    lead = width // LANES
    if depth == 1:
        for col in range(lead):
            flat[row + col : row + col + 1, :] = in_ref[:, col * LANES : (col + 1) * LANES]
        tail = jnp.concatenate([in_ref[:, lead * LANES :], jnp.zeros((1, half), f32)], 1)
        flat[row + lead : row + lead + 1, :] = tail
        return
    step = 2 * width // LANES
    pairs = depth // 2
    lane = lax.broadcasted_iota(jnp.int32, (pairs, LANES), 1)
    for col in range(lead):
        pair_ref[col, 0:depth, :] = in_ref[:, col * LANES : (col + 1) * LANES]
    pair_ref[lead, 0:depth, 0:half] = in_ref[:, lead * LANES :]
    even = [pair_ref[col, strided(0, pairs, 2), :] for col in range(lead + 1)]
    odd = [half_swap(pair_ref[col, strided(1, pairs, 2), :]) for col in range(lead + 1)]
    for col in range(lead):
        flat[strided(row + col, pairs, step), :] = even[col]
    flat[strided(row + lead, pairs, step), :] = jnp.where(lane < half, even[lead], odd[0])
    for col in range(lead):
        flat[strided(row + lead + 1 + col, pairs, step), :] = jnp.where(
            lane < half, odd[col], odd[col + 1]
        )


def decode(number, core, bits):
    first = (number >> (bits - 1)) & 1
    second = (number >> (bits - 2)) & 1
    found = (first << core) | (second << (1 - core))
    for place in range(2, bits):
        found = found | (((number >> (bits - 1 - place)) & 1) << place)
    return found


def unflatten_kernel(plan, side, bits, where_ref, base_ref, *refs):
    pieces, refs = refs[:4], refs[4:]
    carried, refs = (refs[:1], refs[1:]) if side else ((), refs)
    outs, (flat, pair_ref) = refs[:-2], refs[-2:]
    span, overlap, half = plan["span"], plan["overlap"], plan["half"]
    origin = plan["origins"][side]
    core, mine = where_ref[0], where_ref[1]
    lead = plan["bases"][side * half] - origin
    if lead:
        flat[0:lead, :] = jnp.zeros((lead, LANES), f32)
    last = plan["bases"][side * half + half - 1] - origin + span
    if flat.shape[0] > last:
        flat[last:, :] = jnp.zeros((flat.shape[0] - last, LANES), f32)

    def base_of(owner):
        return pl.multiple_of(base_ref[side * half + owner] - origin, 16)

    def clear(owner, carry):
        base = base_of(owner)
        flat[pl.ds(base, overlap), :] = jnp.zeros((overlap, LANES), f32)
        flat[pl.ds(base + span - overlap, overlap), :] = jnp.zeros((overlap, LANES), f32)
        return carry

    lax.fori_loop(0, half, clear, 0)
    middle = span // 2
    for number, piece in enumerate(pieces):
        theirs = number // 2
        owner_core = core if theirs == 0 else 1 - core
        upper = number % 2 * (half // 2)
        for part in range(2):

            @pl.when(owner_core == part)
            def _(part=part, piece=piece, upper=upper):
                def place(entry, carry):
                    base = base_of(decode(entry + upper, part, bits) ^ mine)
                    value = piece[entry].astype(f32)
                    if part == 0:
                        flat[pl.ds(base, overlap), :] += value[:overlap]
                        flat[pl.ds(base + overlap, middle - overlap), :] = value[overlap:]
                    else:
                        flat[pl.ds(base + middle, middle - overlap), :] = value[: middle - overlap]
                        flat[pl.ds(base + span - overlap, overlap), :] += value[middle - overlap :]
                    return carry

                lax.fori_loop(0, half // 2, place, 0)

    for number, ((label, shape), out_ref) in enumerate(zip(plan["sides"][side], outs)):
        read_param(flat, plan["places"][label][0] - origin, shape, out_ref, pair_ref)
        if side and number == 0:
            out_ref[...] += carried[0][...]


def unflatten(where, pieces, plan, side, bits, carried=()):
    outs = []
    for label, shape in plan["sides"][side]:
        outs.append(jax.ShapeDtypeStruct(two_dim(shape), bf16 if is_matrix(label) else f32))
    vmem = pl.BlockSpec(memory_space=pltpu.VMEM)
    smem = pl.BlockSpec(memory_space=pltpu.SMEM)
    values = pl.pallas_call(
        functools.partial(unflatten_kernel, plan, side, bits),
        out_shape=outs,
        in_specs=[smem, smem] + [vmem] * (len(pieces) + len(carried)),
        out_specs=[vmem] * len(outs),
        scratch_shapes=[
            pltpu.VMEM((plan["heights"][side], LANES), f32),
            pltpu.VMEM((5, MS, LANES), f32),
        ],
        cost_estimate=estimate(1_000_000, 8_000_000),
        name="unflatten" + str(side),
    )(where, jnp.asarray(plan["bases"], jnp.int32), *pieces, *carried)
    return {label: value for (label, shape), value in zip(plan["sides"][side], values)}


def flatten_kernel(plan, group, bits, where_ref, base_ref, *refs):
    begin, owners, held, origin, height = plan["groups"][group]
    count = len(held)
    grads, (low_ref, high_ref, send_ref, flat, pair_ref) = refs[:count], refs[count:]
    span = plan["span"]
    core, mine = where_ref[0], where_ref[1]
    first, last = None, 0
    for label, shape in held:
        row = plan["places"][label][0] - origin
        first = row if first is None else first
        last = row + -(-math.prod(shape) // LANES)
    if first:
        flat[0:first, :] = jnp.zeros((first, LANES), f32)
    flat[last // 8 * 8 :, :] = jnp.zeros((height - last // 8 * 8, LANES), f32)
    window = (plan["bases"][begin] - origin, plan["bases"][begin + owners - 1] + span - origin)
    for (label, shape), ref in zip(held, grads):
        write_param(flat, plan["places"][label][0] - origin, shape, ref, pair_ref, window)

    def rows_of(entry, part):
        owner = (decode(entry, part, bits) ^ mine) & (owners - 1)
        base = base_ref[begin + owner] - origin + part * (span // 2)
        return flat[pl.ds(pl.multiple_of(base, 16), span // 2), :].astype(bf16)

    def place(entry, carry):
        low_ref[entry] = rows_of(entry, core)
        high_ref[entry] = rows_of(entry + owners // 2, core)
        send_ref[entry] = rows_of(entry, 1 - core)
        send_ref[entry + owners // 2] = rows_of(entry + owners // 2, 1 - core)
        return carry

    lax.fori_loop(0, owners // 2, place, 0)


def flatten(where, grads, plan, group):
    vmem = pl.BlockSpec(memory_space=pltpu.VMEM)
    smem = pl.BlockSpec(memory_space=pltpu.SMEM)
    begin, owners, held, origin, height = plan["groups"][group]
    rows = plan["span"] // 2
    values = [grads[label] for label, shape in held]
    return pl.pallas_call(
        functools.partial(flatten_kernel, plan, group, owners.bit_length() - 1),
        out_shape=(
            jax.ShapeDtypeStruct((owners // 2, rows, LANES), bf16),
            jax.ShapeDtypeStruct((owners // 2, rows, LANES), bf16),
            jax.ShapeDtypeStruct((owners, rows, LANES), bf16),
        ),
        in_specs=[smem, smem] + [vmem] * len(values),
        out_specs=(vmem, vmem, vmem),
        scratch_shapes=[
            pltpu.VMEM((height, LANES), f32),
            pltpu.VMEM((5, MS, LANES), f32),
        ],
        cost_estimate=estimate(1_000_000, 10_000_000),
        name="flatten" + str(group),
    )(where, jnp.asarray(plan["bases"], jnp.int32), *values)


def ln_parts(value):
    mean = jnp.mean(value, -1, keepdims=True)
    centred = value - mean
    variance = jnp.mean(centred * centred, -1, keepdims=True)
    inverse = lax.rsqrt(variance + norm_eps)
    return centred * inverse, inverse


def ln_back(grad, hat, inverse, gain):
    scaled = grad * gain
    first = jnp.mean(scaled, -1, keepdims=True)
    second = jnp.mean(scaled * hat, -1, keepdims=True)
    return inverse * (scaled - first - hat * second)


def gelu_parts(value):
    cdf = 0.5 + 0.5 * lax.erf(value * (2.0**-0.5))
    density = jnp.exp(value * value * -0.5) * (1.0 / math.sqrt(2.0 * math.pi))
    return value * cdf, cdf + value * density


def col_sum(value):
    return jnp.sum(value, 0, keepdims=True)


def groups(width):
    size = width // HEADS
    found = []
    for start in range(0, width, LANES):
        stop = min(start + LANES, width)
        found.append((start, stop, (stop - start) // size))
    return found, size


def stack_heads(value, count, size):
    lane = lax.broadcasted_iota(jnp.int32, value.shape, 1)
    zero = jnp.zeros_like(value)
    return jnp.concatenate(
        [
            jnp.where((lane >= head * size) & (lane < (head + 1) * size), value, zero)
            for head in range(count)
        ],
        0,
    )


def merge_heads(value, count, size):
    rows = value.shape[0] // count
    lane = lax.broadcasted_iota(jnp.int32, (rows, value.shape[1]), 1)
    merged = value[0:rows]
    for head in range(1, count):
        merged = jnp.where(lane >= head * size, value[head * rows : (head + 1) * rows], merged)
    return merged


def attention_forward(pair, length, tall, tokens, weights, keeps):
    ln1_ref, qkv_w, qkv_b, proj_w, proj_b, ln2_ref = weights
    a1_ref, qkv_ref, probs_ref, att_ref, mid_ref, n2_ref = keeps
    width = tokens.shape[-1]
    found, size = groups(width)
    scale = size ** (-0.5)
    hat, _ = ln_parts(tokens)
    a1 = (hat * ln1_ref[0:1, :] + ln1_ref[1:2, :]).astype(bf16)
    a1_ref[...] = a1
    qkv_ref[...] = (mm(a1, qkv_w[...]) + qkv_b[...]).astype(bf16)
    key_lane = lax.broadcasted_iota(jnp.int32, (1, tall), 1)
    bias = jnp.where(key_lane < length, 0.0, -1e30).astype(f32)
    for crop in range(pair):
        here = slice(crop * tall, (crop + 1) * tall)
        for start, stop, count in found:
            query = stack_heads(qkv_ref[here, start:stop], count, size)
            key = qkv_ref[here, width + start : width + stop]
            value = qkv_ref[here, 2 * width + start : 2 * width + stop]
            scores = mm_t(query, key) * scale + bias
            summit = jnp.max(scores, -1, keepdims=True)
            weights = jnp.exp(scores - summit)
            probs = (weights / jnp.sum(weights, -1, keepdims=True)).astype(bf16)
            first = start // size
            for head in range(count):
                probs_ref[crop, first + head] = probs[head * tall : (head + 1) * tall]
            att_ref[here, start:stop] = merge_heads(mm(probs, value), count, size).astype(bf16)
    mid = tokens + mm(att_ref[...], proj_w[...]) + proj_b[...]
    mid_ref[...] = mid
    hat, _ = ln_parts(mid)
    n2_ref[...] = (hat * ln2_ref[0:1, :] + ln2_ref[1:2, :]).astype(bf16)


def mlp_forward(chunk, mid_ref, n2_ref, weights, keeps):
    fc1_w, fc1_b, fc2_w, fc2_b = weights
    z_ref, slope_ref, y_ref = keeps
    y_ref[...] = mid_ref[...] + fc2_b[...]
    for number in range(fc1_w.shape[1] // chunk):
        cols = slice(number * chunk, (number + 1) * chunk)
        inner = mm(n2_ref[...], fc1_w[:, cols]) + fc1_b[:, cols]
        active, slope = gelu_parts(inner)
        z_ref[:, cols] = active.astype(bf16)
        slope_ref[:, cols] = slope.astype(bf16)
        y_ref[...] += mm(z_ref[:, cols], fc2_w[cols, :])


def keep_heads(pair, tall, y_ref, head_ref):
    for crop in range(pair):
        slot = pl.program_id(0) * pair + crop
        head_ref[pl.ds(slot, 1), :] = y_ref[crop * tall : crop * tall + 1, :]


def carry(value, norm, weight, bias):
    hat, _ = ln_parts(value)
    active, _ = gelu_parts(hat * norm[0:1, :] + norm[1:2, :])
    return (mm(active.astype(bf16), weight[...]) + bias[...]).astype(bf16)


def attention_kernel(pair, length, tall, tok_ref, *refs):
    tokens = tok_ref[...].reshape(pair * tall, tok_ref.shape[-1]).astype(f32)
    attention_forward(pair, length, tall, tokens, refs[:6], refs[6:])


def block_kernel(pair, length, tall, chunk, tok_ref, *refs):
    tokens = tok_ref[...].reshape(pair * tall, tok_ref.shape[-1]).astype(f32)
    attention_forward(pair, length, tall, tokens, refs[:6], refs[10:16])
    mlp_forward(chunk, refs[14], refs[15], refs[6:10], refs[16:19])
    keep_heads(pair, tall, refs[18], refs[19])


def mlp_kernel(pair, tall, chunk, mid_ref, n2_ref, *refs):
    weights, heads, (far_head, *far), near = refs[:4], None, refs[4:8], refs[8:11]
    z_ref, slope_ref, y_ref, head_ref, near_ref, far_ref = refs[11:]
    mlp_forward(chunk, mid_ref, n2_ref, weights, (z_ref, slope_ref, y_ref))
    keep_heads(pair, tall, y_ref, head_ref)

    @pl.when(pl.program_id(0) == pl.num_programs(0) - 1)
    def _():
        near_ref[...] = carry(head_ref[...], *near)
        far_ref[...] = carry(far_head[...], *far)


ATTENTION = ("ln1", "qkv_w", "qkv_b", "proj_w", "proj_b", "ln2")
MLP = ("fc1_w", "fc1_b", "fc2_w", "fc2_b")
TO = ("to_ln", "to_w", "to_b")


def pick(params, label, names):
    return [params[label + "_" + name] for name in names]


def row_spec(rows, cols):
    return pl.BlockSpec((rows, cols), lambda i: (i, 0))


def fixed_spec(shape):
    rank = len(shape)
    return pl.BlockSpec(shape, lambda i: (0,) * rank)


def kept_outs(crops, tall, width, hidden, pair):
    rows, flat = pair * tall, crops * tall

    def entry(cols, dtype):
        return row_spec(rows, cols), jax.ShapeDtypeStruct((flat, cols), dtype)

    attention = [
        entry(width, bf16),
        entry(3 * width, bf16),
        (
            pl.BlockSpec((pair, HEADS, tall, tall), lambda i: (i, 0, 0, 0)),
            jax.ShapeDtypeStruct((crops, HEADS, tall, tall), bf16),
        ),
        entry(width, bf16),
        entry(width, f32),
        entry(width, bf16),
    ]
    mlp = [
        entry(hidden, bf16),
        entry(hidden, bf16),
        entry(width, f32),
        (fixed_spec((crops, width)), jax.ShapeDtypeStruct((crops, width), f32)),
    ]
    return attention, mlp


def block_forward(tokens, params, label, length, pair):
    crops, tall, width = tokens.shape
    hidden = params[label + "_fc1_w"].shape[1]
    weights = pick(params, label, ATTENTION + MLP)
    attention, mlp = kept_outs(crops, tall, width, hidden, pair)
    outs = attention + mlp
    flops = 2 * crops * tall * (4 * width * width + 2 * width * hidden)
    return pl.pallas_call(
        functools.partial(block_kernel, pair, length, tall, 384),
        grid=(crops // pair,),
        out_shape=[shape for spec, shape in outs],
        in_specs=[pl.BlockSpec((pair, tall, width), lambda i: (i, 0, 0))]
        + [whole(value.shape) for value in weights],
        out_specs=[spec for spec, shape in outs],
        cost_estimate=estimate(8 * flops, 10_000_000),
        name="block_" + label,
    )(tokens, *weights)


def attention_only(tokens, params, label, length, pair):
    crops, tall, width = tokens.shape
    weights = pick(params, label, ATTENTION)
    outs, _ = kept_outs(crops, tall, width, width, pair)
    flops = 2 * crops * tall * 4 * width * width
    return pl.pallas_call(
        functools.partial(attention_kernel, pair, length, tall),
        grid=(crops // pair,),
        out_shape=[shape for spec, shape in outs],
        in_specs=[pl.BlockSpec((pair, tall, width), lambda i: (i, 0, 0))]
        + [whole(value.shape) for value in weights],
        out_specs=[spec for spec, shape in outs],
        cost_estimate=estimate(8 * flops, 20_000_000),
        name="attention_" + label,
    )(tokens, *weights)


def mlp_only(mid, n2, far_head, params, label, far, crops, pair):
    flat, width = mid.shape
    tall = flat // crops
    rows = pair * tall
    hidden = params[label + "_fc1_w"].shape[1]
    weights = pick(params, label, MLP)
    extra = [far_head] + pick(params, far, TO) + pick(params, label, TO)
    _, outs = kept_outs(crops, tall, width, hidden, pair)
    for name in (label, far):
        shape = (crops, params[name + "_to_w"].shape[1])
        outs.append((fixed_spec(shape), jax.ShapeDtypeStruct(shape, bf16)))
    flops = 2 * flat * 2 * width * hidden
    return pl.pallas_call(
        functools.partial(mlp_kernel, pair, tall, 384),
        grid=(crops // pair,),
        out_shape=[shape for spec, shape in outs],
        in_specs=[row_spec(rows, width), row_spec(rows, width)]
        + [whole(value.shape) for value in weights + extra],
        out_specs=[spec for spec, shape in outs],
        cost_estimate=estimate(8 * flops, 20_000_000),
        name="mlp_" + label,
    )(mid, n2, *weights, *extra)


def cross_kernel(
    length,
    tall,
    crops,
    sent_ref,
    y_ref,
    gret_ref,
    ca_ln,
    q_w,
    q_b,
    k_w,
    v_w,
    v_b,
    o_w,
    o_b,
    back_ln,
    back_w,
    back_b,
    returned_ref,
    gsent_ref,
    gj_ref,
    d_ca_ln,
    d_q_w,
    d_q_b,
    d_k_w,
    d_v_w,
    d_v_b,
    d_o_w,
    d_o_b,
    d_back_ln,
    d_back_w,
    d_back_b,
    sent_f,
    n_all,
    score_all,
    mates_all,
    pairs_all,
    gn_head,
    gj_head,
):
    width = y_ref.shape[1]
    size = width // HEADS
    scale = size ** (-0.5)
    stacked = crops * 8
    lane = lax.broadcasted_iota(jnp.int32, (8, width), 1)
    head = lax.broadcasted_iota(jnp.int32, (8, width), 0)
    own_head = (lane >= head * size) & (lane < (head + 1) * size)
    row = lax.broadcasted_iota(jnp.int32, (tall, 1), 0)
    key_lane = lax.broadcasted_iota(jnp.int32, (1, tall), 1)
    bias = jnp.where(key_lane < length, 0.0, -1e30).astype(f32)
    gain, shift = ca_ln[0:1, :], ca_ln[1:2, :]
    sent_f[...] = sent_ref[...].astype(f32)
    hat, _ = ln_parts(sent_f[...])
    n_head = (hat * gain + shift).astype(bf16)

    def spread(value):
        return jnp.concatenate(
            [jnp.where(own_head, value[crop : crop + 1], 0.0) for crop in range(crops)], 0
        )

    def gathered(value):
        return jnp.concatenate(
            [
                col_sum(jnp.where(own_head, value[crop * 8 : crop * 8 + 8], 0.0))
                for crop in range(crops)
            ],
            0,
        )

    def normed_of(crop):
        return n_all[crop * tall : (crop + 1) * tall, :]

    def against(value):
        return jnp.concatenate(
            [
                mm_t(value[crop * 8 : crop * 8 + 8].astype(bf16), normed_of(crop))
                for crop in range(crops)
            ],
            0,
        )

    def mixed(value):
        return jnp.concatenate(
            [
                mm(value[crop * 8 : crop * 8 + 8].astype(bf16), normed_of(crop))
                for crop in range(crops)
            ],
            0,
        )

    query = spread((mm(n_head, q_w[...]) + q_b[...]).astype(bf16).astype(f32)).astype(bf16)
    keyed = mm_t(query, k_w[...]) * scale
    blank = jnp.zeros((8, width), f32)
    for crop in range(crops):
        mates_all[crop] = jnp.concatenate([keyed[crop * 8 : crop * 8 + 8], blank], 0).astype(bf16)

    def joined(crop):
        here = pl.ds(pl.multiple_of(crop * tall, 16), tall)
        return here, jnp.where(row == 0, sent_f[pl.ds(crop, 1), :], y_ref[here, :])

    def ahead(crop, carry):
        here, value = joined(crop)
        hat, _ = ln_parts(value)
        normed = (hat * gain + shift).astype(bf16)
        n_all[here, :] = normed
        score_all[pl.ds(crop, 1)] = mm_t(mates_all[crop], normed)[None, 0:8]
        return carry

    lax.fori_loop(0, crops, ahead, 0)
    scores = score_all[...].reshape(stacked, tall) + bias
    summit = jnp.max(scores, -1, keepdims=True)
    weights = jnp.exp(scores - summit)
    probs = weights / jnp.sum(weights, -1, keepdims=True)
    rounded = probs.astype(bf16).astype(f32)
    total = jnp.sum(rounded, -1, keepdims=True)
    mean_n = mixed(rounded).astype(bf16)
    attended = gathered(mm(mean_n, v_w[...]) + total * v_b[...]).astype(bf16)
    merged = sent_f[...] + mm(attended, o_w[...]) + o_b[...]
    hat, inverse = ln_parts(merged)
    active, slope = gelu_parts(hat * back_ln[0:1, :] + back_ln[1:2, :])
    active = active.astype(bf16)
    returned_ref[...] = (mm(active, back_w[...]) + back_b[...]).astype(bf16)
    gret = gret_ref[...]
    d_back_w[...] = t_mm(active, gret)
    d_back_b[...] = col_sum(gret.astype(f32))
    gact = mm_t(gret, back_w[...]) * slope
    d_back_ln[0:1, :] = col_sum(gact * hat)
    d_back_ln[1:2, :] = col_sum(gact)
    gfused = ln_back(gact, hat, inverse, back_ln[0:1, :])
    gfo = gfused.astype(bf16)
    d_o_w[...] = t_mm(attended, gfo)
    d_o_b[...] = col_sum(gfo.astype(f32))
    gatt = spread(mm_t(gfo, o_w[...]).astype(bf16).astype(f32))
    d_v_b[...] = col_sum(total * gatt)
    gbias = jnp.sum(gatt * v_b[...], -1, keepdims=True)
    gatt = gatt.astype(bf16)
    d_v_w[...] = t_mm(mean_n, gatt)
    valued = mm_t(gatt, v_w[...])
    gprobs = against(valued) + gbias
    inner = gprobs - jnp.sum(gprobs * probs, -1, keepdims=True)
    gscores = (probs * inner).astype(bf16).astype(f32)
    for crop in range(crops):
        part = slice(crop * 8, crop * 8 + 8)
        mates_all[crop] = jnp.concatenate([keyed[part], valued[part]], 0).astype(bf16)
        pairs_all[crop] = jnp.concatenate([gscores[part], rounded[part]], 0).astype(bf16)
    slid = (mixed(gscores) * scale).astype(bf16)
    d_k_w[...] = t_mm(slid, query)
    gq = gathered(mm(slid, k_w[...])).astype(bf16)
    d_q_w[...] = t_mm(n_head, gq)
    d_q_b[...] = col_sum(gq.astype(f32))
    gn_head[...] = mm_t(gq, q_w[...])
    d_ca_ln[...] = jnp.zeros_like(d_ca_ln)

    def finish(crop, carry):
        here, value = joined(crop)
        hat, inverse = ln_parts(value)
        gn = t_mm(pairs_all[crop], mates_all[crop])
        gn = gn + jnp.where(row == 0, gn_head[pl.ds(crop, 1), :], 0.0)
        d_ca_ln[0:1, :] += col_sum(gn * hat)
        d_ca_ln[1:2, :] += col_sum(gn)
        gj = ln_back(gn, hat, inverse, gain)
        gj_ref[here, :] = gj
        gj_head[pl.ds(crop, 1), :] = gj[0:1, :]
        return carry

    lax.fori_loop(0, crops, finish, 0)
    gsent_ref[...] = (gj_head[...] + gfused).astype(bf16)


def cross(sent, hosted, gret, params, label, length, tall):
    crops, width = sent.shape
    own = gret.shape[1]
    flat = crops * tall
    names = ("ca_ln", "ca_q_w", "ca_q_b", "ca_k_w", "ca_v_w", "ca_v_b", "ca_o_w", "ca_o_b")
    names = names + ("back_ln", "back_w", "back_b")
    weights = [params[label + "_" + name] for name in names]
    outs = [
        jax.ShapeDtypeStruct((crops, own), bf16),
        jax.ShapeDtypeStruct((crops, width), bf16),
        jax.ShapeDtypeStruct((flat, width), f32),
    ] + [jax.ShapeDtypeStruct(value.shape, f32) for value in weights]
    vmem = pl.BlockSpec(memory_space=pltpu.VMEM)
    small = pltpu.VMEM((crops, width), f32)
    values = pl.pallas_call(
        functools.partial(cross_kernel, length, tall, crops),
        out_shape=outs,
        in_specs=[vmem] * (3 + len(weights)),
        out_specs=[vmem] * len(outs),
        scratch_shapes=[
            small,
            pltpu.VMEM((flat, width), bf16),
            pltpu.VMEM((crops, 8, tall), f32),
            pltpu.VMEM((crops, 16, width), bf16),
            pltpu.VMEM((crops, 16, tall), bf16),
            small,
            small,
        ],
        cost_estimate=estimate(2 * flat * width * width * 2, 8_000_000),
        name="cross_" + label,
    )(sent, hosted, gret, *weights)
    grads = {label + "_" + name: value for name, value in zip(names, values[3:])}
    return values[0], values[1], values[2], grads


def head_backward(headrow_ref, gsent_ref, to_ln, to_w, d_to_ln, d_to_w, d_to_b, ghead_ref):
    hat, inverse = ln_parts(headrow_ref[...])
    active, slope = gelu_parts(hat * to_ln[0:1, :] + to_ln[1:2, :])
    gsent = gsent_ref[...]
    d_to_w[...] = t_mm(active.astype(bf16), gsent)
    d_to_b[...] = col_sum(gsent.astype(f32))
    gact = mm_t(gsent, to_w[...]) * slope
    d_to_ln[0:1, :] = col_sum(gact * hat)
    d_to_ln[1:2, :] = col_sum(gact)
    ghead_ref[...] = ln_back(gact, hat, inverse, to_ln[0:1, :])


def clear_all(refs):
    for ref in refs:
        ref[...] = jnp.zeros_like(ref)


def mlp_backward(pair, tall, chunk, live_ref, acts, weights, grads, out_ref, gy, gnormed):
    cot_ref, y_ref, gj_ref, mid_ref, n2_ref, z_ref, slope_ref, ghead, returned_ref = acts
    ln2_ref, fc1_w, fc2_w = weights
    d_ln2, d_fc1_w, d_fc1_b, d_fc2_w, d_fc2_b = grads
    length = out_ref.shape[2]
    row = lax.broadcasted_iota(jnp.int32, (tall, 1), 0)
    for crop in range(pair):
        here = slice(crop * tall, (crop + 1) * tall)
        slot = pl.program_id(0) * pair + crop
        live = jnp.where(slot < live_ref[0], 1.0, 0.0).astype(f32)
        seed = cot_ref[crop].astype(f32) * live + gj_ref[here, :]
        gy[here, :] = jnp.where(row == 0, ghead[pl.ds(slot, 1), :], seed)
        home = returned_ref[pl.ds(slot, 1), :]
        final = jnp.where(row == 0, home, y_ref[here, :])
        out_ref[0, crop] = final[0:length].astype(bf16)
    gm = gy[...].astype(bf16)
    d_fc2_b[...] += col_sum(gm.astype(f32))
    for number in range(fc1_w.shape[1] // chunk):
        cols = slice(number * chunk, (number + 1) * chunk)
        d_fc2_w[cols, :] += t_mm(z_ref[:, cols], gm)
        gu = slope_ref[:, cols].astype(f32) * mm_t(gm, fc2_w[cols, :])
        gu = gu.astype(bf16)
        d_fc1_w[:, cols] += t_mm(n2_ref[...], gu)
        d_fc1_b[:, cols] += col_sum(gu.astype(f32))
        part = mm_t(gu, fc1_w[:, cols])
        gnormed[...] = part if number == 0 else gnormed[...] + part
    hat, inverse = ln_parts(mid_ref[...])
    gn = gnormed[...]
    d_ln2[0:1, :] += col_sum(gn * hat)
    d_ln2[1:2, :] += col_sum(gn)
    gy[...] += ln_back(gn, hat, inverse, ln2_ref[0:1, :])


def attention_backward(pair, tall, acts, weights, grads, gtok_ref, gmid_ref, gqkv, gatt_ref):
    tok_ref, a1_ref, qkv_ref, probs_ref, att_ref = acts
    ln1_ref, qkv_w, proj_w = weights
    d_ln1, d_qkv_w, d_qkv_b, d_proj_w, d_proj_b = grads
    width = tok_ref.shape[-1]
    length = gtok_ref.shape[2]
    found, size = groups(width)
    scale = size ** (-0.5)
    gp = gmid_ref[...].astype(bf16)
    d_proj_w[...] += t_mm(att_ref[...], gp)
    d_proj_b[...] += col_sum(gp.astype(f32))
    gatt_ref[...] = mm_t(gp, proj_w[...]).astype(bf16)

    def one(crop, carry):
        here = pl.ds(crop * tall, tall)
        if not isinstance(crop, int):
            here = pl.ds(pl.multiple_of(crop * tall, 16), tall)
        for start, stop, count in found:
            first = start // size
            query = stack_heads(qkv_ref[here, start:stop], count, size)
            key = qkv_ref[here, width + start : width + stop]
            value = qkv_ref[here, 2 * width + start : 2 * width + stop]
            gatt = stack_heads(gatt_ref[here, start:stop], count, size)
            probs_low = jnp.concatenate([probs_ref[crop, first + head] for head in range(count)], 0)
            probs = probs_low.astype(f32)
            gprobs = mm_t(gatt, value)
            inner = gprobs - jnp.sum(gprobs * probs, -1, keepdims=True)
            gscores = (probs * inner).astype(bf16)
            gq = merge_heads(mm(gscores, key), count, size) * scale
            gk = t_mm(gscores, query) * scale
            gv = t_mm(probs_low, gatt)
            gqkv[here, start:stop] = gq.astype(bf16)
            gqkv[here, width + start : width + stop] = gk.astype(bf16)
            gqkv[here, 2 * width + start : 2 * width + stop] = gv.astype(bf16)
        return carry

    if len(found) > 2:
        lax.fori_loop(0, pair, one, 0)
    else:
        for crop in range(pair):
            one(crop, 0)
    grad = gqkv[...]
    d_qkv_w[...] += t_mm(a1_ref[...], grad)
    d_qkv_b[...] += col_sum(grad.astype(f32))
    gn = mm_t(grad, qkv_w[...])
    hat, inverse = ln_parts(tok_ref[...].reshape(pair * tall, width).astype(f32))
    d_ln1[0:1, :] += col_sum(gn * hat)
    d_ln1[1:2, :] += col_sum(gn)
    gtok = gmid_ref[...] + ln_back(gn, hat, inverse, ln1_ref[0:1, :])
    for crop in range(pair):
        gtok_ref[0, crop] = gtok[crop * tall : crop * tall + length].astype(bf16)


GRAD_MLP = ("ln2", "fc1_w", "fc1_b", "fc2_w", "fc2_b")
GRAD_ATTENTION = ("ln1", "qkv_w", "qkv_b", "proj_w", "proj_b")


def mlp_back_kernel(pair, tall, chunk, live_ref, *refs):
    cot_ref, y_ref, gj_ref, mid_ref, n2_ref, z_ref, slope_ref, returned_ref = refs[:8]
    weights = refs[8:11]
    near, far = refs[11:15], refs[15:19]
    out_ref, gmid_ref, ghead_far = refs[19:22]
    grads, near_grads, far_grads = refs[22:27], refs[27:30], refs[30:33]
    ghead, gnormed, home = refs[33:]

    @pl.when(pl.program_id(0) == 0)
    def _():
        head_backward(*near, *near_grads, ghead)
        head_backward(*far, *far_grads, ghead_far)
        clear_all(grads)
        home[...] = returned_ref[...].astype(f32)

    acts = (cot_ref, y_ref, gj_ref, mid_ref, n2_ref, z_ref, slope_ref, ghead, home)
    mlp_backward(pair, tall, chunk, live_ref, acts, weights, grads, out_ref, gmid_ref, gnormed)


def attention_back_kernel(pair, tall, gmid_ref, *refs):
    acts, weights, gtok_ref, grads = refs[:5], refs[5:8], refs[8], refs[9:14]

    @pl.when(pl.program_id(0) == 0)
    def _():
        clear_all(grads)

    attention_backward(pair, tall, acts, weights, grads, gtok_ref, gmid_ref, *refs[14:])


def block_back_kernel(pair, tall, chunk, live_ref, *refs):
    mlp_acts, acts = refs[:9], refs[9:14]
    weights, mlp_weights = refs[14:17], refs[17:20]
    out_ref, gtok_ref = refs[20:22]
    mlp_grads, grads = refs[22:27], refs[27:32]
    gy, gnormed, gqkv, gatt_ref, home = refs[32:]

    @pl.when(pl.program_id(0) == 0)
    def _():
        clear_all(mlp_grads + grads)
        home[...] = mlp_acts[8][...].astype(f32)

    mlp_backward(
        pair, tall, chunk, live_ref, (*mlp_acts[:8], home), mlp_weights, mlp_grads, out_ref, gy, gnormed
    )
    attention_backward(pair, tall, acts, weights, grads, gtok_ref, gy, gqkv, gatt_ref)


def named(label, names, values):
    return {label + "_" + name: value for name, value in zip(names, values)}


def grad_outs(params, label, names):
    return [
        (fixed_spec(value.shape), jax.ShapeDtypeStruct(value.shape, f32))
        for value in pick(params, label, names)
    ]


def token_out(crops, length, width, pair):
    return (
        pl.BlockSpec((1, pair, length, width), lambda i: (0, i, 0, 0)),
        jax.ShapeDtypeStruct((1, crops, length, width), bf16),
    )


def mlp_back(cot, live, kept, gj, near, far, returned, params, label, other, length, pair):
    crops, tall, width = cot.shape
    mid, n2, z, slope, y = kept
    hidden = z.shape[1]
    rows, flat = pair * tall, crops * tall
    weights = pick(params, label, ("ln2", "fc1_w", "fc2_w"))
    near = list(near) + pick(params, label, ("to_ln", "to_w"))
    far = list(far) + pick(params, other, ("to_ln", "to_w"))
    smem = pl.BlockSpec(memory_space=pltpu.SMEM)
    outs = [
        token_out(crops, length, width, pair),
        (row_spec(rows, width), jax.ShapeDtypeStruct((flat, width), f32)),
        (fixed_spec(far[0].shape), jax.ShapeDtypeStruct(far[0].shape, f32)),
    ]
    outs += grad_outs(params, label, GRAD_MLP)
    outs += grad_outs(params, label, TO) + grad_outs(params, other, TO)
    values = pl.pallas_call(
        functools.partial(mlp_back_kernel, pair, tall, 384),
        grid=(crops // pair,),
        out_shape=[shape for spec, shape in outs],
        in_specs=[smem, pl.BlockSpec((pair, tall, width), lambda i: (i, 0, 0))]
        + [row_spec(rows, width)] * 4
        + [row_spec(rows, hidden)] * 2
        + [whole(value.shape) for value in [returned] + weights + near + far],
        out_specs=[spec for spec, shape in outs],
        scratch_shapes=[
            pltpu.VMEM((crops, width), f32),
            pltpu.VMEM((rows, width), f32),
            pltpu.VMEM((crops, width), f32),
        ],
        cost_estimate=estimate(8 * 8 * flat * width * hidden, 20_000_000),
        name="mlp_back_" + label,
    )(live, cot, y, gj, mid, n2, z, slope, returned, *weights, *near, *far)
    grads = named(label, GRAD_MLP, values[3:8])
    grads.update(named(label, TO, values[8:11]))
    grads.update(named(other, TO, values[11:14]))
    return values[0], values[1], values[2], grads


def attention_back(tokens, gmid, kept, params, label, length, pair):
    crops, tall, width = tokens.shape
    a1, qkv, probs, att = kept
    rows, flat = pair * tall, crops * tall
    weights = pick(params, label, ("ln1", "qkv_w", "proj_w"))
    outs = [token_out(crops, length, width, pair)] + grad_outs(params, label, GRAD_ATTENTION)
    values = pl.pallas_call(
        functools.partial(attention_back_kernel, pair, tall),
        grid=(crops // pair,),
        out_shape=[shape for spec, shape in outs],
        in_specs=[
            row_spec(rows, width),
            pl.BlockSpec((pair, tall, width), lambda i: (i, 0, 0)),
            row_spec(rows, width),
            row_spec(rows, 3 * width),
            pl.BlockSpec((pair, HEADS, tall, tall), lambda i: (i, 0, 0, 0)),
            row_spec(rows, width),
        ]
        + [whole(value.shape) for value in weights],
        out_specs=[spec for spec, shape in outs],
        scratch_shapes=[pltpu.VMEM((rows, 3 * width), bf16), pltpu.VMEM((rows, width), bf16)],
        cost_estimate=estimate(8 * 16 * flat * width * width, 20_000_000),
        name="attention_back_" + label,
    )(gmid, tokens, a1, qkv, probs, att, *weights)
    return values[0], named(label, GRAD_ATTENTION, values[1:])


def block_back(tokens, cot, live, kept, gj, ghead, returned, params, label, length, pair):
    crops, tall, width = tokens.shape
    a1, qkv, probs, att, mid, n2, z, slope, y = kept
    hidden = z.shape[1]
    rows, flat = pair * tall, crops * tall
    weights = pick(params, label, ("ln1", "qkv_w", "proj_w", "ln2", "fc1_w", "fc2_w"))
    smem = pl.BlockSpec(memory_space=pltpu.SMEM)
    token_spec = pl.BlockSpec((pair, tall, width), lambda i: (i, 0, 0))
    outs = [token_out(crops, length, width, pair)] * 2
    outs += grad_outs(params, label, GRAD_MLP) + grad_outs(params, label, GRAD_ATTENTION)
    values = pl.pallas_call(
        functools.partial(block_back_kernel, pair, tall, 384),
        grid=(crops // pair,),
        out_shape=[shape for spec, shape in outs],
        in_specs=[smem, token_spec]
        + [row_spec(rows, width)] * 4
        + [row_spec(rows, hidden)] * 2
        + [whole(ghead.shape), whole(returned.shape)]
        + [
            token_spec,
            row_spec(rows, width),
            row_spec(rows, 3 * width),
            pl.BlockSpec((pair, HEADS, tall, tall), lambda i: (i, 0, 0, 0)),
            row_spec(rows, width),
        ]
        + [whole(value.shape) for value in weights],
        out_specs=[spec for spec, shape in outs],
        scratch_shapes=[
            pltpu.VMEM((rows, width), f32),
            pltpu.VMEM((rows, width), f32),
            pltpu.VMEM((rows, 3 * width), bf16),
            pltpu.VMEM((rows, width), bf16),
            pltpu.VMEM((crops, width), f32),
        ],
        cost_estimate=estimate(8 * 4 * flat * (4 * width * width + 2 * width * hidden), 20_000_000),
        name="block_back_" + label,
    )(live, cot, y, gj, mid, n2, z, slope, ghead, returned, tokens, a1, qkv, probs, att, *weights)
    grads = named(label, GRAD_MLP, values[2:7])
    grads.update(named(label, GRAD_ATTENTION, values[7:12]))
    return values[0], values[1], grads


def swap(value):
    return lax.ppermute(value, "branch", [(0, 1), (1, 0)])


def partner(value, bit):
    count = lax.axis_size("dp")
    return lax.ppermute(value, "dp", [(i, i ^ bit) for i in range(count)])


def side_partner(value, place):
    count = lax.axis_size("dp")
    pairs = []
    for core in range(2):
        bit = 1 << (place ^ core)
        pairs += [(core * count + i, core * count + (i ^ bit)) for i in range(count)]
    return lax.ppermute(value, ("branch", "dp"), pairs)


def tie(value, *others):
    return lax.optimization_barrier((value, *others))[0] if others else value


def gather_lines(held, first, last, jobs=()):
    for number, place in enumerate(range(first, last, -1)):
        got = partner(held, 1 << place)
        if number < len(jobs):
            got = tie(got, *jobs[number](held))
        held = jnp.concatenate([held, got], 0)
    return held


def gather_middle(held):
    return jnp.concatenate([held, side_partner(held, 1)], 0)


def add_low(*values):
    total = values[0].astype(f32)
    for value in values[1:]:
        total = total + value.astype(f32)
    return total.astype(bf16)


def reduce_start(low, high, got):
    half = low.shape[0]
    sent = add_low(high, got[half:])
    return sent, [low, got[:half], side_partner(sent, 0)]


def reduce_middle(parts):
    quarter = parts[0].shape[0] // 2
    sent = add_low(*[part[quarter:] for part in parts])
    return sent, [part[:quarter] for part in parts] + [side_partner(sent, 1)]


def reduce_line(parts, place):
    count = parts[0].shape[0] // 2
    sent = add_low(*[part[count:] for part in parts])
    return [part[:count] for part in parts] + [partner(sent, 1 << place)]


def reduce_lines(parts, first, last):
    for place in range(first, last):
        parts = reduce_line(parts, place)
    return parts


def add_up(parts):
    total = parts[0][0].astype(f32)
    for part in parts[1:]:
        total = total + part[0].astype(f32)
    return total


def shards(
    small_tokens,
    large_tokens,
    small_cot,
    large_cot,
    live_counts,
    master,
    first_moment,
    second_moment,
):
    count = lax.axis_size("branch") * lax.axis_size("dp")
    bits = lax.axis_size("dp").bit_length() - 1
    plan = grid_plan(count)
    core, mine = lax.axis_index("branch"), lax.axis_index("dp")
    where = jnp.stack([core, mine]).astype(jnp.int32)
    index = lax.axis_index(("branch", "dp"))
    size = master.shape[0]
    rows = plan["shard_rows"]
    table = lax.dynamic_index_in_dim(jnp.asarray(plan["table"]), index, 0, False)
    padded = jnp.pad(master, (0, rows * LANES - size)).reshape(rows, LANES)
    keep, send = align(where, table, padded, plan)
    got = swap(send)
    counts = live_counts[:, 0]
    own_count = lax.dynamic_slice_in_dim(counts, core, 1)
    far_count = lax.dynamic_slice_in_dim(counts, 1 - core, 1)
    crops, length_s = small_tokens.shape[1], small_tokens.shape[2]
    length_l = large_tokens.shape[2]
    tall_s, tall_l = round_up(length_s, 16), round_up(length_l, 16)
    pair = 2

    def inward(value):
        return jnp.transpose(value[0], (1, 0, 2))

    def settled(value):
        return with_layout_constraint(inward(value), Layout(major_to_minor=(0, 1, 2)))

    def outward(value):
        return jnp.transpose(value, (1, 0, 2))[None]

    def taller(value, length, tall):
        return jnp.pad(value[0], ((0, 0), (0, tall - length), (0, 0)))

    early = []

    def pad_tokens(held):
        early.append(taller(tie(small_tokens, held), length_s, tall_s))
        early.append(taller(tie(large_tokens, held), length_l, tall_l))
        return early[0:2]

    def pad_seeds(held):
        slots = jnp.arange(crops, dtype=jnp.int32)[:, None]
        small_held, large_held = tie(small_cot, held), tie(large_cot, held)
        early.append(taller(small_held, length_s, tall_s))
        early.append(taller(large_held, length_l, tall_l))
        early.append(jnp.where(slots < own_count, small_held[0, :, 0], 0))
        early.append(jnp.where(slots < far_count, large_held[0, :, 0], 0))
        return early[2:6]

    held = jnp.where(core == 0, keep, got)[None]
    near = gather_lines(held, bits - 1, 1, (pad_tokens, pad_seeds))
    small, large, small_seed, large_seed, ret_small, ret_large = early
    far = tie(jnp.where(core == 0, got, keep)[None], near)
    middle = (bits + 1) // 2
    far = gather_lines(far, bits - 1, middle)
    near = tie(gather_middle(near), far)
    near_end = side_partner(near, 0)
    far = gather_lines(far, middle, 1)
    near_end = tie(near_end, far)
    near_pieces = (near, near_end, swap(near), swap(near_end))
    ret_small, ret_large = swap(ret_small), swap(ret_large)

    params = unflatten(where, near_pieces, plan, 0, bits)
    straddling = params.pop(plan["sides"][1][0][0])
    far = tie(far, near_end)
    far = jnp.concatenate([far, tie(side_partner(far, 1), params["s_ln1"])], 0)
    *kept_s, head_s = block_forward(tie(small, far), params, "s", length_s, pair)
    far_end = side_partner(far, 0)
    kept_l = attention_only(tie(large, far_end), params, "l", length_l, 1)
    far_pieces = (far, far_end, swap(far), swap(far_end))
    params.update(unflatten(where, far_pieces, plan, 1, bits, (straddling,)))
    z_l, slope_l, y_l, head_l, sent_l, sent_s = mlp_only(
        kept_l[4], kept_l[5], head_s, params, "l", "s", crops, pair
    )
    got_s, got_l = swap(sent_s), swap(sent_l)
    grads = {}
    back_s, gsent_s, gj_l, part = cross(got_s, y_l, ret_small, params, "s", length_l, tall_l)
    grads.update(part)
    home_s, own_s = swap(back_s), swap(gsent_s)
    back_l, gsent_l, gj_s, part = cross(got_l, kept_s[8], ret_large, params, "l", length_s, tall_s)
    grads.update(part)
    home_l, own_l = swap(back_l), swap(gsent_l)
    large_out, gmid, ghead_s, part = mlp_back(
        large_seed,
        far_count,
        (kept_l[4], kept_l[5], z_l, slope_l, y_l),
        gj_l,
        (head_l, own_l),
        (head_s, own_s),
        home_l,
        params,
        "l",
        "s",
        length_l,
        pair,
    )
    grads.update(part)
    far_parts = flatten(where, grads, plan, 2)
    far_got = swap(far_parts[2])
    large_grad, part = attention_back(large, gmid, kept_l[:4], params, "l", length_l, pair)
    grads.update(part)
    grads["l_ln1"], far_got = lax.optimization_barrier((grads["l_ln1"], far_got))
    upper_parts = flatten(where, grads, plan, 1)
    upper_got = swap(upper_parts[2])
    sent_far, far_side = reduce_start(*far_parts[:2], far_got)
    sent_upper, upper = reduce_start(*upper_parts[:2], tie(upper_got, sent_far))
    ghead_s = tie(ghead_s, sent_far, sent_upper, gmid)
    small_out, small_grad, part = block_back(
        small, small_seed, own_count, kept_s, gj_s, ghead_s, home_s, params, "s", length_s, pair
    )
    grads.update(part)
    grads["s_ln1"] = tie(grads["s_ln1"], far_side[-1], upper[-1])
    lower_parts = flatten(where, grads, plan, 0)
    lower_got = swap(lower_parts[2])
    sent, far_side = reduce_middle(far_side)
    sent, upper = reduce_middle(upper)
    sent, lower = reduce_start(*lower_parts[:2], lower_got)
    lower[-1], large_out, large_grad = lax.optimization_barrier(
        (lower[-1], settled(tie(large_out, sent)), settled(tie(large_grad, sent)))
    )
    far_side[-1], upper[-1] = tie(far_side[-1], sent), tie(upper[-1], sent)
    far_side = reduce_line(far_side, 2)
    upper = reduce_lines(upper, 2, bits - 1)
    sent, lower = reduce_middle(lower)
    lower[-1], small_out, small_grad = lax.optimization_barrier(
        (lower[-1], settled(tie(small_out, sent)), settled(tie(small_grad, sent)))
    )
    lower = add_up(reduce_lines(lower, 2, bits - 1))
    far_total = add_up(reduce_lines(far_side, 3, bits))
    upper = add_up(upper)
    top = (mine >> (bits - 1)) & 1
    last_sent = jnp.where(top == 1, lower, upper).astype(bf16)
    near_total = jnp.where(top == 1, upper, lower)
    near_total = near_total + partner(last_sent, 1 << (bits - 1)).astype(f32)
    own = jnp.where(core == 0, near_total, far_total)
    got = swap(jnp.where(core == 0, far_total, near_total))
    summed, square = unalign(where, table, own, got, plan)
    square = square + swap(square)
    for place in range(bits):
        square = square + partner(square, 1 << place)
    grad_norm = jnp.sqrt(square[0, 0])
    own_grad = summed.reshape(-1)[:size]
    clipped = own_grad * jnp.minimum(1.0, clip_norm / grad_norm)
    new_first = beta_one * first_moment + (1.0 - beta_one) * clipped
    new_second = beta_two * second_moment + (1.0 - beta_two) * clipped * clipped
    new_master = master - rate * (
        new_first / bias_one / (jnp.sqrt(new_second / bias_two) + adam_eps) + decay * master
    )
    return (
        outward(small_out),
        outward(large_out),
        outward(small_grad),
        outward(large_grad),
        grad_norm,
        new_first,
        new_second,
        new_master,
        new_master.astype(bf16),
    )


def solution(mesh):
    return jax.shard_map(
        shards,
        mesh=mesh,
        in_specs=(
            P("branch", "dp", None, None),
            P("branch", "dp", None, None),
            P("branch", "dp", None, None),
            P("branch", "dp", None, None),
            P(None, "dp"),
            P(("branch", "dp")),
            P(("branch", "dp")),
            P(("branch", "dp")),
        ),
        out_specs=(
            P("branch", "dp", None, None),
            P("branch", "dp", None, None),
            P("branch", "dp", None, None),
            P("branch", "dp", None, None),
            P(),
            P(("branch", "dp")),
            P(("branch", "dp")),
            P(("branch", "dp")),
            P(("branch", "dp")),
        ),
        check_vma=False,
    )
```

profile of v0, /device:TPU:0, one launch (start us, length us, event | category | flops | bytes accessed | tf_op | source)
XLA Modules:
  0.0 304.6 jit_solution(15459684497016632876)
XLA Ops:
  4.4 2.3 align.1
  10.1 3.6 %collective-permute-start.1 = (bf16[1,416,128]{2,1,0:T(8,128)(2,1)S(1)}, bf16[1,416,128]{2,1,0:T(8,128)(2,1)S(1)}, u32[]{:S(2)}, u32[]{:S(2)}) collective-permute-start(bf16[1,416,128]{2,1,0:T(8,128)(2,1)S(1)} %get-tuple-element.367), channel_id=1, source_target_pairs={{0,8},{1,9},{2,10},{3,11},{4,12},{5,13},{6,14},{7,15},{8,0},{9,1},... | collective-permute-start | bytes 319496 | tf_op jit(solution)/shard_map/ppermute | solution.py:1249
  23.1 3.7 %collective-permute-done.2 = bf16[2,416,128]{2,1,0:T(8,128)(2,1)S(1)} collective-permute-done((bf16[2,416,128]{2,1,0:T(8,128)(2,1)S(1)}, bf16[2,416,128]{2,1,0:T(8,128)(2,1)S(1)}, u32[]{:S(2)}, u32[]{:S(2)}) %collective-permute-start.2) | collective-permute-done | bytes 213024 | tf_op jit(solution)/shard_map/ppermute | solution.py:1249
  28.3 2.7 collective-permute-start.3
  31.7 3.9 %collective-permute-done.3 = bf16[1,416,128]{2,1,0:T(8,128)(2,1)S(1)} collective-permute-done((bf16[1,416,128]{2,1,0:T(8,128)(2,1)S(1)}, bf16[1,416,128]{2,1,0:T(8,128)(2,1)S(1)}, u32[]{:S(2)}, u32[]{:S(2)}) %collective-permute-start.3) | collective-permute-done | bytes 106528 | tf_op jit(solution)/shard_map/ppermute | solution.py:1249
  38.2 5.9 %collective-permute-done.4 = bf16[2,416,128]{2,1,0:T(8,128)(2,1)S(1)} collective-permute-done((bf16[2,416,128]{2,1,0:T(8,128)(2,1)S(1)}, bf16[2,416,128]{2,1,0:T(8,128)(2,1)S(1)}, u32[]{:S(2)}, u32[]{:S(2)}) %collective-permute-start.4) | collective-permute-done | bytes 213024 | tf_op jit(solution)/shard_map/ppermute | solution.py:1249
  44.8 4.4 %collective-permute-done.6.refs_1_ = bf16[8,416,128]{2,1,0:T(8,128)(2,1)S(1)} collective-permute-done((bf16[8,416,128]{2,1,0:T(8,128)(2,1)S(1)}, bf16[8,416,128]{2,1,0:T(8,128)(2,1)S(1)}, u32[]{:S(2)}, u32[]{:S(2)}) %collective-permute-start.6) | collective-permute-done | bytes 852000 | tf_op jit(solution)/shard_map/ppermute | solution.py:1258
  52.6 4.9 %unflatten0.1 = (f32[2,192]{1,0:T(2,128)}, bf16[192,576]{1,0:T(8,128)(2,1)}, f32[1,576]{1,0:T(1,128)}, bf16[192,192]{1,0:T(8,128)(2,1)}, f32[1,192]{1,0:T(1,128)...) custom-call(s32[2]{0:T(128)} %pad_add_fusion.core_ref.where_ref, ...), custom_call_target="tpu_custom_call" | custom-call | flops 1000000 | bytes 8000000 | tf_op jit(solution)/shard_map/unflatten0/pallas_call | solution.py:447
  60.1 14.5 %block_s.1 = (bf16[1280,192]{1,0:T(8,128)(2,1)}, bf16[1280,576]{1,0:T(8,128)(2,1)}, bf16[8,6,160,160]{3,2,1,0:T(8,128)(2,1)}, bf16[1280,192]{1,0:T(8,128)(2,1)},...) custom-call(bf16[8,160,192]{2,1,0:T(8,128)(2,1)} %pad.19.tok_ref.ref, ...), custom_call_target="tpu_custom_call" | custom-call | flops 9059696640 | bytes 10000000 | tf_op jit(solution)/shard_map/block_s/pallas_call | solution.py:706
  74.8 17.3 %attention_l.1 = (bf16[1664,384]{1,0:T(8,128)(2,1)}, bf16[1664,1152]{1,0:T(8,128)(2,1)}, bf16[8,6,208,208]{3,2,1,0:T(8,128)(2,1)}, bf16[1664,384]{1,0:T(8,128)(2...) custom-call(bf16[8,208,384]{2,1,0:T(8,128)(2,1)} %pad.20.tok_ref.refs_0_, ...), custom_call_target="tpu_custom_call" | custom-call | flops 15703474176 | bytes 20000000 | tf_op jit(solution)/shard_map/attention_l/pallas_call | solution.py:723
  93.3 5.1 %unflatten1.1 = (f32[1,1536]{1,0:T(1,128)}, bf16[1536,384]{1,0:T(8,128)(2,1)}, f32[1,384]{1,0:T(1,128)}, f32[2,192]{1,0:T(2,128)}, bf16[192,384]{1,0:T(8,128)(2,...) custom-call(s32[2]{0:T(128)} %pad_add_fusion.core_ref.where_ref, ...), custom_call_target="tpu_custom_call" | custom-call | flops 1000000 | bytes 8000000 | tf_op jit(solution)/shard_map/unflatten1/pallas_call | solution.py:447
  98.4 15.7 %mlp_l.1 = (bf16[1664,1536]{1,0:T(8,128)(2,1)}, bf16[1664,1536]{1,0:T(8,128)(2,1)}, f32[1664,384]{1,0:T(8,128)}, f32[8,384]{1,0:T(8,128)}, bf16[8,192]{1,0:T(8,128)(2,1)}, /*index=5*/bf16[8,384]{1,0:T(8,128)(2,1)}) custom-call(f32[1664,384]{1,0:T(8,128)} %get-tuple-element.215.mid_ref.refs_3_, bf16[1664,384]{1,0:T(8,128)(2,1)} %get-tuple-element.216.n2_ref.refs_4_, ...), custom_call_target="tpu_custom_call" | custom-call | flops 31406948352 | bytes 20000000 | tf_op jit(solution)/shard_map/mlp_l/pallas_call | solution.py:747
  116.2 10.6 %cross_l.1 = (bf16[8,384]{1,0:T(8,128)(2,1)}, bf16[8,192]{1,0:T(8,128)(2,1)}, f32[1280,192]{1,0:T(8,128)}, f32[2,192]{1,0:T(2,128)}, f32[192,192]{1,0:T(8,128)},...) custom-call(bf16[8,192]{1,0:T(8,128)(2,1)} %copy-done.29, ...), custom_call_target="tpu_custom_call" | custom-call | flops 188743680 | bytes 8000000 | tf_op jit(solution)/shard_map/cross_l/pallas_call | solution.py:942
  127.8 13.8 %cross_s.1 = (bf16[8,192]{1,0:T(8,128)(2,1)}, bf16[8,384]{1,0:T(8,128)(2,1)}, f32[1664,384]{1,0:T(8,128)}, f32[2,384]{1,0:T(2,128)}, f32[384,384]{1,0:T(8,128)},...) custom-call(bf16[8,384]{1,0:T(8,128)(2,1)} %copy-done.28, ...), custom_call_target="tpu_custom_call" | custom-call | flops 981467136 | bytes 8000000 | tf_op jit(solution)/shard_map/cross_s/pallas_call | solution.py:942
  143.7 24.5 %mlp_back_l.1 = (bf16[1,8,197,384]{3,2,1,0:T(8,128)(2,1)}, f32[1664,384]{1,0:T(8,128)}, f32[8,192]{1,0:T(8,128)}, f32[2,384]{1,0:T(2,128)}, f32[384,1536]{1,0:T(...) custom-call(s32[1]{0:T(128)} %bitcast.15.live_ref, ...), custom_call_target="tpu_custom_call" | custom-call | flops 62813896704 | bytes 20000000 | tf_op jit(solution)/shard_map/mlp_back_l/pallas_call | solution.py:1151
  168.2 5.9 %flatten2.1 = (bf16[8,416,128]{2,1,0:T(8,128)(2,1)}, bf16[8,416,128]{2,1,0:T(8,128)(2,1)}, bf16[16,416,128]{2,1,0:T(8,128)(2,1)}) custom-call(s32[2]{0:T(128)} %pad_add_fusion.core_ref.where_ref, s32[32]{0:T(128)} %constant.48.clone.base_ref, f32[1,1536]{1,0:T(1,128)} %get-tuple-element.267.refs_0_.refs_6_, f32[1536,384]{1,0:T(8,128)} %get-tuple-element.268.refs_1_, ...), custom_call_target="tpu_custom_call" | custom-call | flops 1000000 | bytes 10000000 | tf_op jit(solution)/shard_map/flatten2/pallas_call | solution.py:501
  174.4 24.4 %attention_back_l.1 = (bf16[1,8,197,384]{3,2,1,0:T(8,128)(2,1)}, f32[2,384]{1,0:T(2,128)}, f32[384,1152]{1,0:T(8,128)}, f32[1,1152]{1,0:T(1,128)}, f32[384,384]{1,0:T(8,128)}, /*index=5*/f32[1,384]{1,0:T(1,128)}) custom-call(f32[1664,384]{1,0:T(8,128)} %get-tuple-element.299.gmid_ref, bf16[8,208,384]{2,1,0:T(8,128)(2,1)} %pad.20.tok_ref.refs_0_, ...), custom_call_target="tpu_custom_call" | custom-call | flops 31406948352 | bytes 20000000 | tf_op jit(solution)/shard_map/attention_back_l/pallas_call | solution.py:1180
  198.8 4.0 %flatten1.1 = (bf16[4,416,128]{2,1,0:T(8,128)(2,1)}, bf16[4,416,128]{2,1,0:T(8,128)(2,1)}, bf16[8,416,128]{2,1,0:T(8,128)(2,1)}) custom-call(s32[2]{0:T(128)} %pad_add_fusion.core_ref.where_ref, s32[32]{0:T(128)} %constant.48.clone.base_ref, f32[384,1152]{1,0:T(8,128)} %get-tuple-element.307.refs_0_.refs_11_, f32[1,1152]{1,0:T(1,128)} %get-tuple-element.308.refs_1_, ...), custom_call_target="tpu_custom_call" | custom-call | flops 1000000 | bytes 10000000 | tf_op jit(solution)/shard_map/flatten1/pallas_call | solution.py:501
  208.9 21.6 %block_back_s.1 = (bf16[1,8,145,192]{3,2,1,0:T(8,128)(2,1)}, bf16[1,8,145,192]{3,2,1,0:T(8,128)(2,1)}, f32[2,192]{1,0:T(2,128)}, f32[192,768]{1,0:T(8,128)}, f32...) custom-call(s32[1]{0:T(128)} %bitcast.2.live_ref, ...), custom_call_target="tpu_custom_call" | custom-call | flops 18119393280 | bytes 20000000 | tf_op jit(solution)/shard_map/block_back_s/pallas_call | solution.py:1211
  231.5 4.4 %flatten0.1 = (bf16[4,416,128]{2,1,0:T(8,128)(2,1)}, bf16[4,416,128]{2,1,0:T(8,128)(2,1)}, bf16[8,416,128]{2,1,0:T(8,128)(2,1)}) custom-call(s32[2]{0:T(128)} %pad_add_fusion.core_ref.where_ref, s32[32]{0:T(128)} %constant.48.clone.base_ref, f32[2,192]{1,0:T(2,128)} %get-tuple-element.323.refs_0_, f32[192,576]{1,0:T(8,128)} %get-tuple-element.324.refs_1_, ...), custom_call_target="tpu_custom_call" | custom-call | flops 1000000 | bytes 10000000 | tf_op jit(solution)/shard_map/flatten0/pallas_call | solution.py:501
  244.2 7.9 %collective-permute-done.32 = bf16[4,416,128]{2,1,0:T(8,128)(2,1)S(1)} collective-permute-done((bf16[4,416,128]{2,1,0:T(8,128)(2,1)S(1)}, bf16[4,416,128]{2,1,0:T(8,128)(2,1)S(1)}, u32[]{:S(2)}, u32[]{:S(2)}) %collective-permute-start.32) | collective-permute-done | bytes 426016 | tf_op jit(solution)/shard_map/ppermute | solution.py:1258
  259.3 2.2 collective-permute-done.27
  264.0 2.6 collective-permute-start.34
  268.4 4.1 %collective-permute-start.31 = (bf16[416,128]{1,0:T(8,128)(2,1)S(1)}, bf16[416,128]{1,0:T(8,128)(2,1)S(1)}, u32[]{:S(2)}, u32[]{:S(2)}) collective-permute-start(bf16[416,128]{1,0:T(8,128)(2,1)S(1)} %get-tuple-element.361), channel_id=1, source_target_pairs={{0,8},{1,9},{2,10},{3,11},{4,12},{5,13},{6,14},{7,15},{8,0},{9,1},... | collective-permute-start | bytes 319496 | tf_op jit(solution)/shard_map/ppermute | solution.py:1249
  273.0 2.9 collective-permute-done.31
  279.8 2.6 unalign.1
  285.2 2.9 collective-permute-done.37
  288.8 2.8 collective-permute-done.38
  291.7 3.6 %collective-permute-done.39 = f32[8,128]{1,0:T(8,128)S(1)} collective-permute-done((f32[8,128]{1,0:T(8,128)S(1)}, f32[8,128]{1,0:T(8,128)S(1)}, u32[]{:S(2)}, u32[]{:S(2)}) %collective-permute-start.39) | collective-permute-done | bytes 4128 | tf_op jit(solution)/shard_map/ppermute | solution.py:1249
  295.3 2.1 collective-permute-start.40
  297.4 2.4 collective-permute-done.40
  301.1 2.4 fusion.3
  (186 shorter events, 69.7 us)
Async XLA Ops:
  10.1 9.6 %collective-permute-start.1 = (bf16[1,416,128]{2,1,0:T(8,128)(2,1)S(1)}, bf16[1,416,128]{2,1,0:T(8,128)(2,1)S(1)}, u32[]{:S(2)}, u32[]{:S(2)}) collective-permute-start(bf16[1,416,128]{2,1,0:T(8,128)(2,1)S(1)} %get-tuple-element.367), channel_id=1, source_target_pairs={{0,8},{1,9},{2,10},{3,11},{4,12},{5,13},{6,14},{7,15},{8,0},{9,1},... | collective-permute-start | bytes 319496 | tf_op jit(solution)/shard_map/ppermute | solution.py:1249
  19.7 7.2 %collective-permute-start.2 = (bf16[2,416,128]{2,1,0:T(8,128)(2,1)S(1)}, bf16[2,416,128]{2,1,0:T(8,128)(2,1)S(1)}, u32[]{:S(2)}, u32[]{:S(2)}) collective-permute-start(bf16[2,416,128]{2,1,0:T(8,128)(2,1)S(1)} %pad_maximum_fusion.2), channel_id=1, source_target_pairs={{0,4},{1,5},{2,6},{3,7},{4,0},{5,1},{6,2},{7,3},{8,12},{9,13},{10,... | collective-permute-start | bytes 638984 | tf_op jit(solution)/shard_map/ppermute | solution.py:1249
  26.9 9.4 %collective-permute-start.5 = (bf16[4,416,128]{2,1,0:T(8,128)(2,1)S(1)}, bf16[4,416,128]{2,1,0:T(8,128)(2,1)S(1)}, u32[]{:S(2)}, u32[]{:S(2)}) collective-permute-start(bf16[4,416,128]{2,1,0:T(8,128)(2,1)S(1)} %pad_maximum_fusion.1), channel_id=1, source_target_pairs={{0,2},{1,3},{2,0},{3,1},{4,6},{5,7},{6,4},{7,5},{8,10},{9,11},{10,... | collective-permute-start | bytes 1277960 | tf_op jit(solution)/shard_map/ppermute | solution.py:1258
  28.3 7.3 %collective-permute-start.3 = (bf16[1,416,128]{2,1,0:T(8,128)(2,1)S(1)}, bf16[1,416,128]{2,1,0:T(8,128)(2,1)S(1)}, u32[]{:S(2)}, u32[]{:S(2)}) collective-permute-start(bf16[1,416,128]{2,1,0:T(8,128)(2,1)S(1)} %get-tuple-element.191), channel_id=1, source_target_pairs={{0,8},{1,9},{2,10},{3,11},{4,12},{5,13},{6,14},{7,15},{8,0},{9,1},... | collective-permute-start | bytes 319496 | tf_op jit(solution)/shard_map/ppermute | solution.py:1249
  36.4 12.8 %collective-permute-start.6 = (bf16[8,416,128]{2,1,0:T(8,128)(2,1)S(1)}, bf16[8,416,128]{2,1,0:T(8,128)(2,1)S(1)}, u32[]{:S(2)}, u32[]{:S(2)}) collective-permute-start(bf16[8,416,128]{2,1,0:T(8,128)(2,1)S(1)} %pad_maximum_fusion.refs_0_), channel_id=1, source_target_pairs={{0,1},{1,0},{2,3},{3,2},{4,5},{5,4},{6,7},{7,6},{8,9},{9,8},{10,11... | collective-permute-start | bytes 2555912 | tf_op jit(solution)/shard_map/ppermute | solution.py:1258
  37.3 6.7 %collective-permute-start.4 = (bf16[2,416,128]{2,1,0:T(8,128)(2,1)S(1)}, bf16[2,416,128]{2,1,0:T(8,128)(2,1)S(1)}, u32[]{:S(2)}, u32[]{:S(2)}) collective-permute-start(bf16[2,416,128]{2,1,0:T(8,128)(2,1)S(1)} %get-tuple-element.368), channel_id=1, source_target_pairs={{0,4},{1,5},{2,6},{3,7},{4,0},{5,1},{6,2},{7,3},{8,12},{9,13},{10,... | collective-permute-start | bytes 638984 | tf_op jit(solution)/shard_map/ppermute | solution.py:1249
  44.8 7.0 %collective-permute-start.8 = (bf16[8,416,128]{2,1,0:T(8,128)(2,1)S(1)}, bf16[8,416,128]{2,1,0:T(8,128)(2,1)S(1)}, u32[]{:S(2)}, u32[]{:S(2)}) collective-permute-start(bf16[8,416,128]{2,1,0:T(8,128)(2,1)S(1)} %pad_maximum_fusion.refs_0_), channel_id=1, source_target_pairs={{0,16},{16,0},{1,17},{17,1},{2,18},{18,2},{3,19},{19,3},{4,20},{20... | collective-permute-start | bytes 2555912 | tf_op jit(solution)/shard_map/ppermute | solution.py:1244
  49.1 8.4 %collective-permute-start.7 = (bf16[4,416,128]{2,1,0:T(8,128)(2,1)}, bf16[4,416,128]{2,1,0:T(8,128)(2,1)}, u32[]{:S(2)}, u32[]{:S(2)}) collective-permute-start(bf16[4,416,128]{2,1,0:T(8,128)(2,1)} %constant_dynamic-update-slice_fusion.2), channel_id=1, source_target_pairs={{0,2},{1,3},{2,0},{3,1},{4,6},{5,7},{6,4},{7,5},{8,10},{9,11},{10,... | collective-permute-start | bytes 1277960 | tf_op jit(solution)/shard_map/ppermute | solution.py:1258
  58.7 16.0 %collective-permute-start.10 = (bf16[8,416,128]{2,1,0:T(8,128)(2,1)S(1)}, bf16[8,416,128]{2,1,0:T(8,128)(2,1)S(1)}, u32[]{:S(2)}, u32[]{:S(2)}) collective-permute-start(bf16[8,416,128]{2,1,0:T(8,128)(2,1)S(1)} %constant_dynamic-update-slice_fusion.5.refs_0_), channel_id=1, source_target_pairs={{0,1},{1,0},{2,3},{3,2},{4,5},{5,4},{6,7},{7,6},{8,9},{9,8},{10,11... | collective-permute-start | bytes 2555912 | tf_op jit(solution)/shard_map/ppermute | solution.py:1258
  59.6 55.4 %collective-permute-start.14 = (bf16[8,384]{1,0:T(8,128)(2,1)S(1)}, bf16[8,384]{1,0:T(8,128)(2,1)S(1)}, u32[]{:S(2)}, u32[]{:S(2)}) collective-permute-start(bf16[8,384]{1,0:T(8,128)(2,1)S(1)} %bitcast_select_fusion.2), channel_id=1, source_target_pairs={{0,16},{16,0},{1,17},{17,1},{2,18},{18,2},{3,19},{19,3},{4,20},{20... | collective-permute-start | bytes 18440 | tf_op jit(solution)/shard_map/ppermute | solution.py:1244
  59.6 32.5 %collective-permute-start.11 = (bf16[8,416,128]{2,1,0:T(8,128)(2,1)S(1)}, bf16[8,416,128]{2,1,0:T(8,128)(2,1)S(1)}, u32[]{:S(2)}, u32[]{:S(2)}) collective-permute-start(bf16[8,416,128]{2,1,0:T(8,128)(2,1)S(1)} %constant_dynamic-update-slice_fusion.5.refs_0_), channel_id=1, source_target_pairs={{0,16},{16,0},{1,17},{17,1},{2,18},{18,2},{3,19},{19,3},{4,20},{20... | collective-permute-start | bytes 2555912 | tf_op jit(solution)/shard_map/ppermute | solution.py:1244
  74.7 17.4 %collective-permute-start.12 = (bf16[8,416,128]{2,1,0:T(8,128)(2,1)S(1)}, bf16[8,416,128]{2,1,0:T(8,128)(2,1)S(1)}, u32[]{:S(2)}, u32[]{:S(2)}) collective-permute-start(bf16[8,416,128]{2,1,0:T(8,128)(2,1)S(1)} %collective-permute-done.10.refs_1_), channel_id=1, source_target_pairs={{0,16},{16,0},{1,17},{17,1},{2,18},{18,2},{3,19},{19,3},{4,20},{20... | collective-permute-start | bytes 2555912 | tf_op jit(solution)/shard_map/ppermute | solution.py:1244
  114.5 12.7 %collective-permute-start.16 = (bf16[8,192]{1,0:T(8,128)(2,1)S(1)}, bf16[8,192]{1,0:T(8,128)(2,1)S(1)}, u32[]{:S(2)}, u32[]{:S(2)}) collective-permute-start(bf16[8,192]{1,0:T(8,128)(2,1)S(1)} %bitcast_select_fusion.3), channel_id=1, source_target_pairs={{0,16},{16,0},{1,17},{17,1},{2,18},{18,2},{3,19},{19,3},{4,20},{20... | collective-permute-start | bytes 9224 | tf_op jit(solution)/shard_map/ppermute | solution.py:1244
  114.7 12.5 %collective-permute-start.15 = (bf16[8,384]{1,0:T(8,128)(2,1)}, bf16[8,384]{1,0:T(8,128)(2,1)S(1)}, u32[]{:S(2)}, u32[]{:S(2)}) collective-permute-start(bf16[8,384]{1,0:T(8,128)(2,1)} %get-tuple-element.247), channel_id=1, source_target_pairs={{0,16},{16,0},{1,17},{17,1},{2,18},{18,2},{3,19},{19,3},{4,20},{20... | collective-permute-start | bytes 18440 | tf_op jit(solution)/shard_map/ppermute | solution.py:1244
  126.8 16.3 %collective-permute-start.17 = (bf16[8,384]{1,0:T(8,128)(2,1)}, bf16[8,384]{1,0:T(8,128)(2,1)S(1)}, u32[]{:S(2)}, u32[]{:S(2)}) collective-permute-start(bf16[8,384]{1,0:T(8,128)(2,1)} %get-tuple-element.262), channel_id=1, source_target_pairs={{0,16},{16,0},{1,17},{17,1},{2,18},{18,2},{3,19},{19,3},{4,20},{20... | collective-permute-start | bytes 18440 | tf_op jit(solution)/shard_map/ppermute | solution.py:1244
  174.1 29.3 %collective-permute-start.20 = (bf16[16,416,128]{2,1,0:T(8,128)(2,1)}, bf16[16,416,128]{2,1,0:T(8,128)(2,1)S(1)}, u32[]{:S(2)}, u32[]{:S(2)}) collective-permute-start(bf16[16,416,128]{2,1,0:T(8,128)(2,1)} %get-tuple-element.305), channel_id=1, source_target_pairs={{0,16},{16,0},{1,17},{17,1},{2,18},{18,2},{3,19},{19,3},{4,20},{20... | collective-permute-start | bytes 5111816 | tf_op jit(solution)/shard_map/ppermute | solution.py:1244
  203.1 5.3 %collective-permute-start.22 = (bf16[8,192]{1,0:T(8,128)(2,1)S(1)}, bf16[8,192]{1,0:T(8,128)(2,1)S(1)}, u32[]{:S(2)}, u32[]{:S(2)}) collective-permute-start(bf16[8,192]{1,0:T(8,128)(2,1)S(1)} %copy-done.33), channel_id=1, source_target_pairs={{0,16},{16,0},{1,17},{17,1},{2,18},{18,2},{3,19},{19,3},{4,20},{20... | collective-permute-start | bytes 9224 | tf_op jit(solution)/shard_map/ppermute | solution.py:1244
  203.6 26.9 %collective-permute-start.23 = (bf16[8,416,128]{2,1,0:T(8,128)(2,1)S(1)}, bf16[8,416,128]{2,1,0:T(8,128)(2,1)S(1)}, u32[]{:S(2)}, u32[]{:S(2)}) collective-permute-start(bf16[8,416,128]{2,1,0:T(8,128)(2,1)S(1)} %add_convert_fusion), channel_id=1, source_target_pairs={{0,1},{1,0},{2,3},{3,2},{4,5},{5,4},{6,7},{7,6},{8,9},{9,8},{10,11... | collective-permute-start | bytes 2555912 | tf_op jit(solution)/shard_map/ppermute | solution.py:1258
  207.2 23.3 %collective-permute-start.24 = (bf16[4,416,128]{2,1,0:T(8,128)(2,1)}, bf16[4,416,128]{2,1,0:T(8,128)(2,1)}, u32[]{:S(2)}, u32[]{:S(2)}) collective-permute-start(bf16[4,416,128]{2,1,0:T(8,128)(2,1)} %add_convert_fusion.3), channel_id=1, source_target_pairs={{0,1},{1,0},{2,3},{3,2},{4,5},{5,4},{6,7},{7,6},{8,9},{9,8},{10,11... | collective-permute-start | bytes 1277960 | tf_op jit(solution)/shard_map/ppermute | solution.py:1258
  235.8 4.7 %collective-permute-start.25 = (bf16[8,416,128]{2,1,0:T(8,128)(2,1)}, bf16[8,416,128]{2,1,0:T(8,128)(2,1)}, u32[]{:S(2)}, u32[]{:S(2)}) collective-permute-start(bf16[8,416,128]{2,1,0:T(8,128)(2,1)} %get-tuple-element.335), channel_id=1, source_target_pairs={{0,16},{16,0},{1,17},{17,1},{2,18},{18,2},{3,19},{19,3},{4,20},{20... | collective-permute-start | bytes 2555912 | tf_op jit(solution)/shard_map/ppermute | solution.py:1244
  237.0 6.2 %collective-permute-start.28 = (bf16[2,416,128]{2,1,0:T(8,128)(2,1)S(1)}, bf16[2,416,128]{2,1,0:T(8,128)(2,1)S(1)}, u32[]{:S(2)}, u32[]{:S(2)}) collective-permute-start(bf16[2,416,128]{2,1,0:T(8,128)(2,1)S(1)} %add_convert_fusion.5), channel_id=1, source_target_pairs={{0,2},{1,3},{2,0},{3,1},{4,6},{5,7},{6,4},{7,5},{8,10},{9,11},{10,... | collective-permute-start | bytes 638984 | tf_op jit(solution)/shard_map/ppermute | solution.py:1258
  240.0 12.1 %collective-permute-start.32 = (bf16[4,416,128]{2,1,0:T(8,128)(2,1)S(1)}, bf16[4,416,128]{2,1,0:T(8,128)(2,1)S(1)}, u32[]{:S(2)}, u32[]{:S(2)}) collective-permute-start(bf16[4,416,128]{2,1,0:T(8,128)(2,1)S(1)} %add_convert_fusion.1), channel_id=1, source_target_pairs={{0,2},{1,3},{2,0},{3,1},{4,6},{5,7},{6,4},{7,5},{8,10},{9,11},{10,... | collective-permute-start | bytes 1277960 | tf_op jit(solution)/shard_map/ppermute | solution.py:1258
  241.7 12.8 %collective-permute-start.26 = (bf16[4,416,128]{2,1,0:T(8,128)(2,1)S(1)}, bf16[4,416,128]{2,1,0:T(8,128)(2,1)S(1)}, u32[]{:S(2)}, u32[]{:S(2)}) collective-permute-start(bf16[4,416,128]{2,1,0:T(8,128)(2,1)S(1)} %add_convert_fusion.2), channel_id=1, source_target_pairs={{0,1},{1,0},{2,3},{3,2},{4,5},{5,4},{6,7},{7,6},{8,9},{9,8},{10,11... | collective-permute-start | bytes 1277960 | tf_op jit(solution)/shard_map/ppermute | solution.py:1258
  252.1 14.5 %collective-permute-start.29 = (bf16[1,416,128]{2,1,0:T(8,128)(2,1)S(1)}, bf16[1,416,128]{2,1,0:T(8,128)(2,1)S(1)}, u32[]{:S(2)}, u32[]{:S(2)}) collective-permute-start(bf16[1,416,128]{2,1,0:T(8,128)(2,1)S(1)} %add_convert_fusion.9), channel_id=1, source_target_pairs={{0,4},{1,5},{2,6},{3,7},{4,0},{5,1},{6,2},{7,3},{8,12},{9,13},{10,... | collective-permute-start | bytes 319496 | tf_op jit(solution)/shard_map/ppermute | solution.py:1249
  255.6 5.9 %collective-permute-start.27 = (bf16[2,416,128]{2,1,0:T(8,128)(2,1)S(1)}, bf16[2,416,128]{2,1,0:T(8,128)(2,1)S(1)}, u32[]{:S(2)}, u32[]{:S(2)}) collective-permute-start(bf16[2,416,128]{2,1,0:T(8,128)(2,1)S(1)} %add_convert_fusion.6), channel_id=1, source_target_pairs={{0,2},{1,3},{2,0},{3,1},{4,6},{5,7},{6,4},{7,5},{8,10},{9,11},{10,... | collective-permute-start | bytes 638984 | tf_op jit(solution)/shard_map/ppermute | solution.py:1258
  256.1 7.8 %collective-permute-start.33 = (bf16[2,416,128]{2,1,0:T(8,128)(2,1)S(1)}, bf16[2,416,128]{2,1,0:T(8,128)(2,1)S(1)}, u32[]{:S(2)}, u32[]{:S(2)}) collective-permute-start(bf16[2,416,128]{2,1,0:T(8,128)(2,1)S(1)} %add_convert_fusion.4), channel_id=1, source_target_pairs={{0,4},{1,5},{2,6},{3,7},{4,0},{5,1},{6,2},{7,3},{8,12},{9,13},{10,... | collective-permute-start | bytes 638984 | tf_op jit(solution)/shard_map/ppermute | solution.py:1249
  262.5 4.8 %collective-permute-start.30 = (bf16[1,416,128]{2,1,0:T(8,128)(2,1)S(1)}, bf16[1,416,128]{2,1,0:T(8,128)(2,1)S(1)}, u32[]{:S(2)}, u32[]{:S(2)}) collective-permute-start(bf16[1,416,128]{2,1,0:T(8,128)(2,1)S(1)} %add_convert_fusion.8), channel_id=1, source_target_pairs={{0,4},{1,5},{2,6},{3,7},{4,0},{5,1},{6,2},{7,3},{8,12},{9,13},{10,... | collective-permute-start | bytes 319496 | tf_op jit(solution)/shard_map/ppermute | solution.py:1249
  264.0 9.0 %collective-permute-start.34 = (bf16[1,416,128]{2,1,0:T(8,128)(2,1)S(1)}, bf16[1,416,128]{2,1,0:T(8,128)(2,1)S(1)}, u32[]{:S(2)}, u32[]{:S(2)}) collective-permute-start(bf16[1,416,128]{2,1,0:T(8,128)(2,1)S(1)} %add_convert_fusion.7), channel_id=1, source_target_pairs={{0,8},{1,9},{2,10},{3,11},{4,12},{5,13},{6,14},{7,15},{8,0},{9,1},... | collective-permute-start | bytes 319496 | tf_op jit(solution)/shard_map/ppermute | solution.py:1249
  268.4 7.6 %collective-permute-start.31 = (bf16[416,128]{1,0:T(8,128)(2,1)S(1)}, bf16[416,128]{1,0:T(8,128)(2,1)S(1)}, u32[]{:S(2)}, u32[]{:S(2)}) collective-permute-start(bf16[416,128]{1,0:T(8,128)(2,1)S(1)} %get-tuple-element.361), channel_id=1, source_target_pairs={{0,8},{1,9},{2,10},{3,11},{4,12},{5,13},{6,14},{7,15},{8,0},{9,1},... | collective-permute-start | bytes 319496 | tf_op jit(solution)/shard_map/ppermute | solution.py:1249
  284.4 3.6 %collective-permute-start.37 = (f32[8,128]{1,0:T(8,128)S(1)}, f32[8,128]{1,0:T(8,128)S(1)}, u32[]{:S(2)}, u32[]{:S(2)}) collective-permute-start(f32[8,128]{1,0:T(8,128)S(1)} %add.220), channel_id=1, source_target_pairs={{0,1},{1,0},{2,3},{3,2},{4,5},{5,4},{6,7},{7,6},{8,9},{9,8},{10,11... | collective-permute-start | bytes 12296 | tf_op jit(solution)/shard_map/ppermute | solution.py:1249
  291.7 3.6 %collective-permute-start.39 = (f32[8,128]{1,0:T(8,128)S(1)}, f32[8,128]{1,0:T(8,128)S(1)}, u32[]{:S(2)}, u32[]{:S(2)}) collective-permute-start(f32[8,128]{1,0:T(8,128)S(1)} %add.222), channel_id=1, source_target_pairs={{0,4},{1,5},{2,6},{3,7},{4,0},{5,1},{6,2},{7,3},{8,12},{9,13},{10,... | collective-permute-start | bytes 12296 | tf_op jit(solution)/shard_map/ppermute | solution.py:1249
  295.3 4.5 %collective-permute-start.40 = (f32[8,128]{1,0:T(8,128)S(1)}, f32[8,128]{1,0:T(8,128)S(1)}, u32[]{:S(2)}, u32[]{:S(2)}) collective-permute-start(f32[8,128]{1,0:T(8,128)S(1)} %add.223), channel_id=1, source_target_pairs={{0,8},{1,9},{2,10},{3,11},{4,12},{5,13},{6,14},{7,15},{8,0},{9,1},... | collective-permute-start | bytes 12296 | tf_op jit(solution)/shard_map/ppermute | solution.py:1249
  (46 other events, 266.0 us)
where the time goes:
time: 305 us
  Pallas kernels  172 us (56%)
  waiting for transfers between devices  50.6 us (17%)
  starting transfers between devices  36.8 us (12%)
  local copies, waits for them, and re-layouts  25.6 us (8%)
  other arithmetic  17 us (6%)
    ppermute x13, waiting for transfers between devices, partner(): return lax.ppermute(value, 'dp', [(i, i ^ bit) for i in range(count)])  31.2 us
    pallas_call x1, Pallas kernels, mlp_back(): pl.pallas_call(functools.partial(mlp_back_kernel, pair, tall, 384), grid=...  24.5 us
    pallas_call x2, Pallas kernels, cross(): pl.pallas_call(functools.partial(cross_kernel, length, tall, crops), out_...  24.5 us
    pallas_call x1, Pallas kernels, attention_back(): pl.pallas_call(functools.partial(attention_back_kernel, pair, tall), grid...  24.4 us
    ppermute x13, starting transfers between devices, partner(): return lax.ppermute(value, 'dp', [(i, i ^ bit) for i in range(count)])  21.9 us
    pallas_call x1, Pallas kernels, block_back(): pl.pallas_call(functools.partial(block_back_kernel, pair, tall, 384), gri...  21.6 us
    pallas_call x1, Pallas kernels, attention_only(): pl.pallas_call(functools.partial(attention_kernel, pair, length, tall), g...  17.3 us
    pallas_call x1, Pallas kernels, mlp_only(): pl.pallas_call(functools.partial(mlp_kernel, pair, tall, 384), grid=(crop...  15.7 us
  transfers between devices with their start and end apart: 41, of which 19 were waited for; matrix products, arithmetic and copies ran while one was open for 8% of the time, Pallas kernels for 43%

commit v1 on v0

--- a/solution.py
+++ b/solution.py
@@ -222,7 +222,7 @@
 
 
 def unalign_kernel(
-    most, rows, span, margin, core_ref, table_ref, own_ref, got_ref, out_ref, norm_ref, padded
+    most, rows, span, margin, core_ref, table_ref, own_ref, got_ref, out_ref, padded
 ):
     first = core_ref[0] == 0
     padded[span:, :] = jnp.zeros((padded.shape[0] - span, LANES), f32)
@@ -244,7 +244,47 @@
         moved = jnp.where(lane < LANES - across, here, below)
         total = jnp.where((place >= left) & (place < right), moved, total)
     out_ref[...] = total
-    norm_ref[...] = jnp.broadcast_to(jnp.sum(total * total).reshape(1, 1), (8, LANES))
+
+
+def settle_kernel(most, where_ref, table_ref, keep_ref, last_ref, *refs):
+    *far_refs, own_ref, send_ref, norm_ref = refs
+    core = where_ref[0]
+    near = keep_ref[...] + last_ref[...].astype(f32)
+    far = far_refs[0][0].astype(f32)
+    for ref in far_refs[1:]:
+        far = far + ref[0].astype(f32)
+    rows = near.shape[0]
+    place = (lax.broadcasted_iota(jnp.int32, near.shape, 0) + core * rows) * LANES
+    place = place + lax.broadcasted_iota(jnp.int32, near.shape, 1)
+
+    def squares(total, entry):
+        found = jnp.zeros_like(total)
+        for number in range(most):
+            at = 3 * (entry * most + number)
+            left, right, delta = table_ref[at], table_ref[at + 1], table_ref[at + 2]
+            inside = (place >= left + delta) & (place < right + delta)
+            found = jnp.where(inside, total * total, found)
+        return found
+
+    both = squares(near, 0) + squares(far, 1)
+    norm_ref[...] = jnp.broadcast_to(jnp.sum(both).reshape(1, 1), (8, LANES))
+    own_ref[...] = jnp.where(core == 0, near, far)
+    send_ref[...] = jnp.where(core == 0, far, near)
+
+
+def settle(where, tables, keep, last, far_parts, plan):
+    smem = pl.BlockSpec(memory_space=pltpu.SMEM)
+    part = jax.ShapeDtypeStruct(keep.shape, f32)
+    return pl.pallas_call(
+        functools.partial(settle_kernel, plan["most"]),
+        grid=(1,),
+        out_shape=(part, part, jax.ShapeDtypeStruct((8, LANES), f32)),
+        in_specs=[smem, smem, fixed_spec(keep.shape), fixed_spec(keep.shape)]
+        + [pl.BlockSpec((1, *keep.shape), lambda i: (0, 0, 0))] * len(far_parts),
+        out_specs=(fixed_spec(keep.shape), fixed_spec(keep.shape), fixed_spec((8, LANES))),
+        cost_estimate=estimate(1_000_000, 2_000_000),
+        name="settle",
+    )(where, tables, keep, last, *far_parts)
 
 
 def align(core, table, shard, plan):
@@ -273,12 +313,9 @@
     smem = pl.BlockSpec(memory_space=pltpu.SMEM)
     return pl.pallas_call(
         functools.partial(unalign_kernel, most, rows, span, margin),
-        out_shape=(
-            jax.ShapeDtypeStruct((rows, LANES), f32),
-            jax.ShapeDtypeStruct((8, LANES), f32),
-        ),
+        out_shape=jax.ShapeDtypeStruct((rows, LANES), f32),
         in_specs=[smem, smem, vmem, vmem],
-        out_specs=(vmem, vmem),
+        out_specs=vmem,
         scratch_shapes=[pltpu.VMEM((tall, LANES), f32)],
         cost_estimate=estimate(1_000_000, 1_000_000),
         name="unalign",
@@ -994,15 +1031,34 @@
         out_ref[0, crop] = final[0:length].astype(bf16)
     gm = gy[...].astype(bf16)
     d_fc2_b[...] += col_sum(gm.astype(f32))
-    for number in range(fc1_w.shape[1] // chunk):
-        cols = slice(number * chunk, (number + 1) * chunk)
+
+    def one(number, first):
+        start = number * chunk
+        if not isinstance(number, int):
+            start = pl.multiple_of(start, LANES)
+        cols = pl.ds(start, chunk)
         d_fc2_w[cols, :] += t_mm(z_ref[:, cols], gm)
         gu = slope_ref[:, cols].astype(f32) * mm_t(gm, fc2_w[cols, :])
         gu = gu.astype(bf16)
         d_fc1_w[:, cols] += t_mm(n2_ref[...], gu)
         d_fc1_b[:, cols] += col_sum(gu.astype(f32))
         part = mm_t(gu, fc1_w[:, cols])
-        gnormed[...] = part if number == 0 else gnormed[...] + part
+        gnormed[...] = part if first else gnormed[...] + part
+
+    def two(number, carry):
+        one(2 * number, False)
+        one(2 * number + 1, False)
+        return carry
+
+    chunks = fc1_w.shape[1] // chunk
+    if chunks > 2:
+        gnormed[...] = jnp.zeros_like(gnormed)
+        lax.fori_loop(0, chunks // 2, two, 0)
+        for number in range(chunks // 2 * 2, chunks):
+            one(number, False)
+    else:
+        for number in range(chunks):
+            one(number, number == 0)
     hat, inverse = ln_parts(mid_ref[...])
     gn = gnormed[...]
     d_ln2[0:1, :] += col_sum(gn * hat)
@@ -1282,28 +1338,26 @@
     return total.astype(bf16)
 
 
+def reduce_step(parts, count, send):
+    count = count // 2
+    sent = add_low(*[part[count : 2 * count] for part in parts])
+    return sent, parts + [send(sent)], count
+
+
 def reduce_start(low, high, got):
     half = low.shape[0]
     sent = add_low(high, got[half:])
-    return sent, [low, got[:half], side_partner(sent, 0)]
-
-
-def reduce_middle(parts):
-    quarter = parts[0].shape[0] // 2
-    sent = add_low(*[part[quarter:] for part in parts])
-    return sent, [part[:quarter] for part in parts] + [side_partner(sent, 1)]
-
-
-def reduce_line(parts, place):
-    count = parts[0].shape[0] // 2
-    sent = add_low(*[part[count:] for part in parts])
-    return [part[:count] for part in parts] + [partner(sent, 1 << place)]
-
-
-def reduce_lines(parts, first, last):
+    return sent, [low, got, side_partner(sent, 0)], half
+
+
+def reduce_middle(parts, count):
+    return reduce_step(parts, count, lambda sent: side_partner(sent, 1))
+
+
+def reduce_lines(parts, count, first, last):
     for place in range(first, last):
-        parts = reduce_line(parts, place)
-    return parts
+        _, parts, count = reduce_step(parts, count, lambda sent: partner(sent, 1 << place))
+    return parts, count
 
 
 def add_up(parts):
@@ -1390,7 +1444,7 @@
     far = jnp.concatenate([far, tie(side_partner(far, 1), params["s_ln1"])], 0)
     *kept_s, head_s = block_forward(tie(small, far), params, "s", length_s, pair)
     far_end = side_partner(far, 0)
-    kept_l = attention_only(tie(large, far_end), params, "l", length_l, 1)
+    kept_l = attention_only(tie(large, far_end), params, "l", length_l, pair)
     far_pieces = (far, far_end, swap(far), swap(far_end))
     params.update(unflatten(where, far_pieces, plan, 1, bits, (straddling,)))
     z_l, slope_l, y_l, head_l, sent_l, sent_s = mlp_only(
@@ -1426,8 +1480,8 @@
     grads["l_ln1"], far_got = lax.optimization_barrier((grads["l_ln1"], far_got))
     upper_parts = flatten(where, grads, plan, 1)
     upper_got = swap(upper_parts[2])
-    sent_far, far_side = reduce_start(*far_parts[:2], far_got)
-    sent_upper, upper = reduce_start(*upper_parts[:2], tie(upper_got, sent_far))
+    sent_far, far_side, far_left = reduce_start(*far_parts[:2], far_got)
+    sent_upper, upper, upper_left = reduce_start(*upper_parts[:2], tie(upper_got, sent_far))
     ghead_s = tie(ghead_s, sent_far, sent_upper, gmid)
     small_out, small_grad, part = block_back(
         small, small_seed, own_count, kept_s, gj_s, ghead_s, home_s, params, "s", length_s, pair
@@ -1436,32 +1490,39 @@
     grads["s_ln1"] = tie(grads["s_ln1"], far_side[-1], upper[-1])
     lower_parts = flatten(where, grads, plan, 0)
     lower_got = swap(lower_parts[2])
-    sent, far_side = reduce_middle(far_side)
-    sent, upper = reduce_middle(upper)
-    sent, lower = reduce_start(*lower_parts[:2], lower_got)
+    _, far_side, far_left = reduce_middle(far_side, far_left)
+    _, upper, upper_left = reduce_middle(upper, upper_left)
+    sent, lower, lower_left = reduce_start(*lower_parts[:2], lower_got)
     lower[-1], large_out, large_grad = lax.optimization_barrier(
         (lower[-1], settled(tie(large_out, sent)), settled(tie(large_grad, sent)))
     )
     far_side[-1], upper[-1] = tie(far_side[-1], sent), tie(upper[-1], sent)
-    far_side = reduce_line(far_side, 2)
-    upper = reduce_lines(upper, 2, bits - 1)
-    sent, lower = reduce_middle(lower)
+    far_side, far_left = reduce_lines(far_side, far_left, 2, 3)
+    upper, _ = reduce_lines(upper, upper_left, 2, bits - 1)
+    sent, lower, lower_left = reduce_middle(lower, lower_left)
     lower[-1], small_out, small_grad = lax.optimization_barrier(
         (lower[-1], settled(tie(small_out, sent)), settled(tie(small_grad, sent)))
     )
-    lower = add_up(reduce_lines(lower, 2, bits - 1))
-    far_total = add_up(reduce_lines(far_side, 3, bits))
+    lower = add_up(reduce_lines(lower, lower_left, 2, bits - 1)[0])
+    far_side, _ = reduce_lines(far_side, far_left, 3, bits)
     upper = add_up(upper)
     top = (mine >> (bits - 1)) & 1
     last_sent = jnp.where(top == 1, lower, upper).astype(bf16)
     near_total = jnp.where(top == 1, upper, lower)
-    near_total = near_total + partner(last_sent, 1 << (bits - 1)).astype(f32)
-    own = jnp.where(core == 0, near_total, far_total)
-    got = swap(jnp.where(core == 0, far_total, near_total))
-    summed, square = unalign(where, table, own, got, plan)
+    last_got = partner(last_sent, 1 << (bits - 1))
+    everyone = jnp.asarray(plan["table"])
+    tables = [
+        lax.dynamic_index_in_dim(everyone, mine + begin, 0, False) for begin in (0, plan["half"])
+    ]
+    own, send, square = settle(
+        where, jnp.concatenate(tables), near_total, last_got, far_side, plan
+    )
+    got = swap(send)
     square = square + swap(square)
+    summed = unalign(where, table, own, tie(got, square), plan)
     for place in range(bits):
-        square = square + partner(square, 1 << place)
+        there = partner(square, 1 << place)
+        square = square + (tie(there, summed) if place == 0 else there)
     grad_norm = jnp.sqrt(square[0, 0])
     own_grad = summed.reshape(-1)[:size]
     clipped = own_grad * jnp.minimum(1.0, clip_norm / grad_norm)

time: 305 us -> 304 us (level)
  waiting for transfers between devices: 50.6 us -> 46.7 us
    pallas_call x1, Pallas kernels: 17.3 us -> 14.2 us  [attention_only(): pl.pallas_call(functools.partial(attention_kernel, pair, length, tall), g...]
    unnamed x76 -> x92, local copies, waits for them, and re-layouts: 8.69 us -> 9.26 us
  transfers between devices with their start and end apart: 41 -> 41, of which waited for: 19 -> 17; matrix products, arithmetic and copies ran while one was open for 8% -> 9% of each run, Pallas kernels for 43% -> 44%
where the time goes in v1:
time: 304 us; the launch traced here: 303 us
  Pallas kernels  174 us (57%)
  waiting for transfers between devices  46.7 us (15%)
  starting transfers between devices  36.8 us (12%)
  local copies, waits for them, and re-layouts  26.4 us (9%)
  other arithmetic  15.8 us (5%)
    ppermute x13, waiting for transfers between devices, partner(): return lax.ppermute(value, 'dp', [(i, i ^ bit) for i in range(count)])  29.3 us
    pallas_call x1, Pallas kernels, mlp_back(): pl.pallas_call(functools.partial(mlp_back_kernel, pair, tall, 384), grid=...  27.1 us
    pallas_call x1, Pallas kernels, attention_back(): pl.pallas_call(functools.partial(attention_back_kernel, pair, tall), grid...  24.6 us
    pallas_call x2, Pallas kernels, cross(): pl.pallas_call(functools.partial(cross_kernel, length, tall, crops), out_...  24.5 us
    pallas_call x1, Pallas kernels, block_back(): pl.pallas_call(functools.partial(block_back_kernel, pair, tall, 384), gri...  21.7 us
    ppermute x13, starting transfers between devices, partner(): return lax.ppermute(value, 'dp', [(i, i ^ bit) for i in range(count)])  20.9 us
    pallas_call x1, Pallas kernels, mlp_only(): pl.pallas_call(functools.partial(mlp_kernel, pair, tall, 384), grid=(crop...  15.5 us
    ppermute x10, waiting for transfers between devices, side_partner(): return lax.ppermute(value, ('branch', 'dp'), pairs)  14.7 us
  transfers between devices with their start and end apart: 41, of which 17 were waited for; matrix products, arithmetic and copies ran while one was open for 9% of the time, Pallas kernels for 44%

profile of v1, /device:TPU:0, one launch (start us, length us, event | category | flops | bytes accessed | tf_op | source)
XLA Modules:
  0.0 302.8 jit_solution(11528108392115604259)
XLA Ops:
  0.7 1.9 pad_bitcast_fusion.shard_ref
  4.5 2.3 align.1
  10.2 3.6 %collective-permute-start.1 = (bf16[1,416,128]{2,1,0:T(8,128)(2,1)S(1)}, bf16[1,416,128]{2,1,0:T(8,128)(2,1)S(1)}, u32[]{:S(2)}, u32[]{:S(2)}) collective-permute-start(bf16[1,416,128]{2,1,0:T(8,128)(2,1)S(1)} %get-tuple-element.370), channel_id=1, source_target_pairs={{0,8},{1,9},{2,10},{3,11},{4,12},{5,13},{6,14},{7,15},{8,0},{9,1},... | collective-permute-start | bytes 319496 | tf_op jit(solution)/shard_map/ppermute | solution.py:1305
  23.3 3.7 %collective-permute-done.2 = bf16[2,416,128]{2,1,0:T(8,128)(2,1)S(1)} collective-permute-done((bf16[2,416,128]{2,1,0:T(8,128)(2,1)S(1)}, bf16[2,416,128]{2,1,0:T(8,128)(2,1)S(1)}, u32[]{:S(2)}, u32[]{:S(2)}) %collective-permute-start.2) | collective-permute-done | bytes 213024 | tf_op jit(solution)/shard_map/ppermute | solution.py:1305
  28.4 2.7 collective-permute-start.3
  31.8 3.9 %collective-permute-done.3 = bf16[1,416,128]{2,1,0:T(8,128)(2,1)S(1)} collective-permute-done((bf16[1,416,128]{2,1,0:T(8,128)(2,1)S(1)}, bf16[1,416,128]{2,1,0:T(8,128)(2,1)S(1)}, u32[]{:S(2)}, u32[]{:S(2)}) %collective-permute-start.3) | collective-permute-done | bytes 106528 | tf_op jit(solution)/shard_map/ppermute | solution.py:1305
  38.3 5.9 %collective-permute-done.4 = bf16[2,416,128]{2,1,0:T(8,128)(2,1)S(1)} collective-permute-done((bf16[2,416,128]{2,1,0:T(8,128)(2,1)S(1)}, bf16[2,416,128]{2,1,0:T(8,128)(2,1)S(1)}, u32[]{:S(2)}, u32[]{:S(2)}) %collective-permute-start.4) | collective-permute-done | bytes 213024 | tf_op jit(solution)/shard_map/ppermute | solution.py:1305
  44.9 4.4 %collective-permute-done.6.refs_1_ = bf16[8,416,128]{2,1,0:T(8,128)(2,1)S(1)} collective-permute-done((bf16[8,416,128]{2,1,0:T(8,128)(2,1)S(1)}, bf16[8,416,128]{2,1,0:T(8,128)(2,1)S(1)}, u32[]{:S(2)}, u32[]{:S(2)}) %collective-permute-start.6) | collective-permute-done | bytes 852000 | tf_op jit(solution)/shard_map/ppermute | solution.py:1314
  52.8 4.9 %unflatten0.1 = (f32[2,192]{1,0:T(2,128)}, bf16[192,576]{1,0:T(8,128)(2,1)}, f32[1,576]{1,0:T(1,128)}, bf16[192,192]{1,0:T(8,128)(2,1)}, f32[1,192]{1,0:T(1,128)...) custom-call(s32[2]{0:T(128)} %pad_add_fusion.core_ref.where_ref, ...), custom_call_target="tpu_custom_call" | custom-call | flops 1000000 | bytes 8000000 | tf_op jit(solution)/shard_map/unflatten0/pallas_call | solution.py:484
  60.3 14.6 %block_s.1 = (bf16[1280,192]{1,0:T(8,128)(2,1)}, bf16[1280,576]{1,0:T(8,128)(2,1)}, bf16[8,6,160,160]{3,2,1,0:T(8,128)(2,1)}, bf16[1280,192]{1,0:T(8,128)(2,1)},...) custom-call(bf16[8,160,192]{2,1,0:T(8,128)(2,1)} %pad.19.tok_ref.ref, ...), custom_call_target="tpu_custom_call" | custom-call | flops 9059696640 | bytes 10000000 | tf_op jit(solution)/shard_map/block_s/pallas_call | solution.py:743
  74.9 14.2 %attention_l.1 = (bf16[1664,384]{1,0:T(8,128)(2,1)}, bf16[1664,1152]{1,0:T(8,128)(2,1)}, bf16[8,6,208,208]{3,2,1,0:T(8,128)(2,1)}, bf16[1664,384]{1,0:T(8,128)(2...) custom-call(bf16[8,208,384]{2,1,0:T(8,128)(2,1)} %pad.20.tok_ref.refs_0_, ...), custom_call_target="tpu_custom_call" | custom-call | flops 15703474176 | bytes 20000000 | tf_op jit(solution)/shard_map/attention_l/pallas_call | solution.py:760
  90.4 5.3 %unflatten1.1 = (f32[1,1536]{1,0:T(1,128)}, bf16[1536,384]{1,0:T(8,128)(2,1)}, f32[1,384]{1,0:T(1,128)}, f32[2,192]{1,0:T(2,128)}, bf16[192,384]{1,0:T(8,128)(2,...) custom-call(s32[2]{0:T(128)} %pad_add_fusion.core_ref.where_ref, ...), custom_call_target="tpu_custom_call" | custom-call | flops 1000000 | bytes 8000000 | tf_op jit(solution)/shard_map/unflatten1/pallas_call | solution.py:484
  95.7 15.5 %mlp_l.1 = (bf16[1664,1536]{1,0:T(8,128)(2,1)}, bf16[1664,1536]{1,0:T(8,128)(2,1)}, f32[1664,384]{1,0:T(8,128)}, f32[8,384]{1,0:T(8,128)}, bf16[8,192]{1,0:T(8,128)(2,1)}, /*index=5*/bf16[8,384]{1,0:T(8,128)(2,1)}) custom-call(f32[1664,384]{1,0:T(8,128)} %get-tuple-element.218.mid_ref.refs_3_, bf16[1664,384]{1,0:T(8,128)(2,1)} %get-tuple-element.219.n2_ref.refs_4_, ...), custom_call_target="tpu_custom_call" | custom-call | flops 31406948352 | bytes 20000000 | tf_op jit(solution)/shard_map/mlp_l/pallas_call | solution.py:784
  113.3 10.7 %cross_l.1 = (bf16[8,384]{1,0:T(8,128)(2,1)}, bf16[8,192]{1,0:T(8,128)(2,1)}, f32[1280,192]{1,0:T(8,128)}, f32[2,192]{1,0:T(2,128)}, f32[192,192]{1,0:T(8,128)},...) custom-call(bf16[8,192]{1,0:T(8,128)(2,1)} %copy-done.35, ...), custom_call_target="tpu_custom_call" | custom-call | flops 188743680 | bytes 8000000 | tf_op jit(solution)/shard_map/cross_l/pallas_call | solution.py:979
  125.0 13.8 %cross_s.1 = (bf16[8,192]{1,0:T(8,128)(2,1)}, bf16[8,384]{1,0:T(8,128)(2,1)}, f32[1664,384]{1,0:T(8,128)}, f32[2,384]{1,0:T(2,128)}, f32[384,384]{1,0:T(8,128)},...) custom-call(bf16[8,384]{1,0:T(8,128)(2,1)} %copy-done.34, ...), custom_call_target="tpu_custom_call" | custom-call | flops 981467136 | bytes 8000000 | tf_op jit(solution)/shard_map/cross_s/pallas_call | solution.py:979
  140.9 27.1 %mlp_back_l.1 = (bf16[1,8,197,384]{3,2,1,0:T(8,128)(2,1)}, f32[1664,384]{1,0:T(8,128)}, f32[8,192]{1,0:T(8,128)}, f32[2,384]{1,0:T(2,128)}, f32[384,1536]{1,0:T(...) custom-call(s32[1]{0:T(128)} %bitcast.15.live_ref, ...), custom_call_target="tpu_custom_call" | custom-call | flops 62813896704 | bytes 20000000 | tf_op jit(solution)/shard_map/mlp_back_l/pallas_call | solution.py:1207
  168.0 5.9 %flatten2.1 = (bf16[8,416,128]{2,1,0:T(8,128)(2,1)}, bf16[8,416,128]{2,1,0:T(8,128)(2,1)}, bf16[16,416,128]{2,1,0:T(8,128)(2,1)}) custom-call(s32[2]{0:T(128)} %pad_add_fusion.core_ref.where_ref, s32[32]{0:T(128)} %constant.54.clone.base_ref, f32[1,1536]{1,0:T(1,128)} %get-tuple-element.270.refs_0_.refs_6_, f32[1536,384]{1,0:T(8,128)} %get-tuple-element.271.refs_1_, ...), custom_call_target="tpu_custom_call" | custom-call | flops 1000000 | bytes 10000000 | tf_op jit(solution)/shard_map/flatten2/pallas_call | solution.py:538
  174.2 24.6 %attention_back_l.1 = (bf16[1,8,197,384]{3,2,1,0:T(8,128)(2,1)}, f32[2,384]{1,0:T(2,128)}, f32[384,1152]{1,0:T(8,128)}, f32[1,1152]{1,0:T(1,128)}, f32[384,384]{1,0:T(8,128)}, /*index=5*/f32[1,384]{1,0:T(1,128)}) custom-call(f32[1664,384]{1,0:T(8,128)} %get-tuple-element.302.gmid_ref, bf16[8,208,384]{2,1,0:T(8,128)(2,1)} %pad.20.tok_ref.refs_0_, ...), custom_call_target="tpu_custom_call" | custom-call | flops 31406948352 | bytes 20000000 | tf_op jit(solution)/shard_map/attention_back_l/pallas_call | solution.py:1236
  198.8 4.0 %flatten1.1 = (bf16[4,416,128]{2,1,0:T(8,128)(2,1)}, bf16[4,416,128]{2,1,0:T(8,128)(2,1)}, bf16[8,416,128]{2,1,0:T(8,128)(2,1)}) custom-call(s32[2]{0:T(128)} %pad_add_fusion.core_ref.where_ref, s32[32]{0:T(128)} %constant.54.clone.base_ref, f32[384,1152]{1,0:T(8,128)} %get-tuple-element.310.refs_0_.refs_11_, f32[1,1152]{1,0:T(1,128)} %get-tuple-element.311.refs_1_, ...), custom_call_target="tpu_custom_call" | custom-call | flops 1000000 | bytes 10000000 | tf_op jit(solution)/shard_map/flatten1/pallas_call | solution.py:538
  208.4 21.7 %block_back_s.1 = (bf16[1,8,145,192]{3,2,1,0:T(8,128)(2,1)}, bf16[1,8,145,192]{3,2,1,0:T(8,128)(2,1)}, f32[2,192]{1,0:T(2,128)}, f32[192,768]{1,0:T(8,128)}, f32...) custom-call(s32[1]{0:T(128)} %bitcast.2.live_ref, ...), custom_call_target="tpu_custom_call" | custom-call | flops 18119393280 | bytes 20000000 | tf_op jit(solution)/shard_map/block_back_s/pallas_call | solution.py:1267
  230.9 4.3 %flatten0.1 = (bf16[4,416,128]{2,1,0:T(8,128)(2,1)}, bf16[4,416,128]{2,1,0:T(8,128)(2,1)}, bf16[8,416,128]{2,1,0:T(8,128)(2,1)}) custom-call(s32[2]{0:T(128)} %pad_add_fusion.core_ref.where_ref, s32[32]{0:T(128)} %constant.54.clone.base_ref, f32[2,192]{1,0:T(2,128)} %get-tuple-element.326.refs_0_, f32[192,576]{1,0:T(8,128)} %get-tuple-element.327.refs_1_, ...), custom_call_target="tpu_custom_call" | custom-call | flops 1000000 | bytes 10000000 | tf_op jit(solution)/shard_map/flatten0/pallas_call | solution.py:538
  243.4 8.0 %collective-permute-done.32.refs_3_ = bf16[4,416,128]{2,1,0:T(8,128)(2,1)S(1)} collective-permute-done((bf16[4,416,128]{2,1,0:T(8,128)(2,1)S(1)}, bf16[4,416,128]{2,1,0:T(8,128)(2,1)S(1)}, u32[]{:S(2)}, u32[]{:S(2)}) %collective-permute-start.32) | collective-permute-done | bytes 426016 | tf_op jit(solution)/shard_map/ppermute | solution.py:1314
  264.8 2.3 collective-permute-start.34
  267.2 1.8 fusion.1
  269.0 3.0 collective-permute-start.31
  273.6 2.6 collective-permute-done.31.last_ref
  276.9 2.5 settle.1
  283.7 2.6 unalign.1
  287.4 2.5 collective-permute-done.38
  290.0 3.6 %collective-permute-done.39 = f32[8,128]{1,0:T(8,128)S(1)} collective-permute-done((f32[8,128]{1,0:T(8,128)S(1)}, f32[8,128]{1,0:T(8,128)S(1)}, u32[]{:S(2)}, u32[]{:S(2)}) %collective-permute-start.39) | collective-permute-done | bytes 4128 | tf_op jit(solution)/shard_map/ppermute | solution.py:1305
  295.3 2.8 collective-permute-done.40
  299.4 2.3 fusion.5
  (203 shorter events, 70.6 us)
Async XLA Ops:
  10.2 9.6 %collective-permute-start.1 = (bf16[1,416,128]{2,1,0:T(8,128)(2,1)S(1)}, bf16[1,416,128]{2,1,0:T(8,128)(2,1)S(1)}, u32[]{:S(2)}, u32[]{:S(2)}) collective-permute-start(bf16[1,416,128]{2,1,0:T(8,128)(2,1)S(1)} %get-tuple-element.370), channel_id=1, source_target_pairs={{0,8},{1,9},{2,10},{3,11},{4,12},{5,13},{6,14},{7,15},{8,0},{9,1},... | collective-permute-start | bytes 319496 | tf_op jit(solution)/shard_map/ppermute | solution.py:1305
  19.8 7.2 %collective-permute-start.2 = (bf16[2,416,128]{2,1,0:T(8,128)(2,1)S(1)}, bf16[2,416,128]{2,1,0:T(8,128)(2,1)S(1)}, u32[]{:S(2)}, u32[]{:S(2)}) collective-permute-start(bf16[2,416,128]{2,1,0:T(8,128)(2,1)S(1)} %pad_maximum_fusion.2), channel_id=1, source_target_pairs={{0,4},{1,5},{2,6},{3,7},{4,0},{5,1},{6,2},{7,3},{8,12},{9,13},{10,... | collective-permute-start | bytes 638984 | tf_op jit(solution)/shard_map/ppermute | solution.py:1305
  27.0 9.4 %collective-permute-start.5 = (bf16[4,416,128]{2,1,0:T(8,128)(2,1)S(1)}, bf16[4,416,128]{2,1,0:T(8,128)(2,1)S(1)}, u32[]{:S(2)}, u32[]{:S(2)}) collective-permute-start(bf16[4,416,128]{2,1,0:T(8,128)(2,1)S(1)} %pad_maximum_fusion.1), channel_id=1, source_target_pairs={{0,2},{1,3},{2,0},{3,1},{4,6},{5,7},{6,4},{7,5},{8,10},{9,11},{10,... | collective-permute-start | bytes 1277960 | tf_op jit(solution)/shard_map/ppermute | solution.py:1314
  28.4 7.3 %collective-permute-start.3 = (bf16[1,416,128]{2,1,0:T(8,128)(2,1)S(1)}, bf16[1,416,128]{2,1,0:T(8,128)(2,1)S(1)}, u32[]{:S(2)}, u32[]{:S(2)}) collective-permute-start(bf16[1,416,128]{2,1,0:T(8,128)(2,1)S(1)} %get-tuple-element.194), channel_id=1, source_target_pairs={{0,8},{1,9},{2,10},{3,11},{4,12},{5,13},{6,14},{7,15},{8,0},{9,1},... | collective-permute-start | bytes 319496 | tf_op jit(solution)/shard_map/ppermute | solution.py:1305
  36.5 12.8 %collective-permute-start.6 = (bf16[8,416,128]{2,1,0:T(8,128)(2,1)S(1)}, bf16[8,416,128]{2,1,0:T(8,128)(2,1)S(1)}, u32[]{:S(2)}, u32[]{:S(2)}) collective-permute-start(bf16[8,416,128]{2,1,0:T(8,128)(2,1)S(1)} %pad_maximum_fusion.refs_0_), channel_id=1, source_target_pairs={{0,1},{1,0},{2,3},{3,2},{4,5},{5,4},{6,7},{7,6},{8,9},{9,8},{10,11... | collective-permute-start | bytes 2555912 | tf_op jit(solution)/shard_map/ppermute | solution.py:1314
  37.5 6.7 %collective-permute-start.4 = (bf16[2,416,128]{2,1,0:T(8,128)(2,1)S(1)}, bf16[2,416,128]{2,1,0:T(8,128)(2,1)S(1)}, u32[]{:S(2)}, u32[]{:S(2)}) collective-permute-start(bf16[2,416,128]{2,1,0:T(8,128)(2,1)S(1)} %get-tuple-element.371), channel_id=1, source_target_pairs={{0,4},{1,5},{2,6},{3,7},{4,0},{5,1},{6,2},{7,3},{8,12},{9,13},{10,... | collective-permute-start | bytes 638984 | tf_op jit(solution)/shard_map/ppermute | solution.py:1305
  44.9 7.0 %collective-permute-start.8 = (bf16[8,416,128]{2,1,0:T(8,128)(2,1)S(1)}, bf16[8,416,128]{2,1,0:T(8,128)(2,1)S(1)}, u32[]{:S(2)}, u32[]{:S(2)}) collective-permute-start(bf16[8,416,128]{2,1,0:T(8,128)(2,1)S(1)} %pad_maximum_fusion.refs_0_), channel_id=1, source_target_pairs={{0,16},{16,0},{1,17},{17,1},{2,18},{18,2},{3,19},{19,3},{4,20},{20... | collective-permute-start | bytes 2555912 | tf_op jit(solution)/shard_map/ppermute | solution.py:1300
  49.3 8.4 %collective-permute-start.7 = (bf16[4,416,128]{2,1,0:T(8,128)(2,1)}, bf16[4,416,128]{2,1,0:T(8,128)(2,1)}, u32[]{:S(2)}, u32[]{:S(2)}) collective-permute-start(bf16[4,416,128]{2,1,0:T(8,128)(2,1)} %constant_dynamic-update-slice_fusion.2), channel_id=1, source_target_pairs={{0,2},{1,3},{2,0},{3,1},{4,6},{5,7},{6,4},{7,5},{8,10},{9,11},{10,... | collective-permute-start | bytes 1277960 | tf_op jit(solution)/shard_map/ppermute | solution.py:1314
  58.8 16.1 %collective-permute-start.10 = (bf16[8,416,128]{2,1,0:T(8,128)(2,1)S(1)}, bf16[8,416,128]{2,1,0:T(8,128)(2,1)S(1)}, u32[]{:S(2)}, u32[]{:S(2)}) collective-permute-start(bf16[8,416,128]{2,1,0:T(8,128)(2,1)S(1)} %constant_dynamic-update-slice_fusion.5.refs_0_), channel_id=1, source_target_pairs={{0,1},{1,0},{2,3},{3,2},{4,5},{5,4},{6,7},{7,6},{8,9},{9,8},{10,11... | collective-permute-start | bytes 2555912 | tf_op jit(solution)/shard_map/ppermute | solution.py:1314
  59.8 52.4 %collective-permute-start.14 = (bf16[8,384]{1,0:T(8,128)(2,1)S(1)}, bf16[8,384]{1,0:T(8,128)(2,1)S(1)}, u32[]{:S(2)}, u32[]{:S(2)}) collective-permute-start(bf16[8,384]{1,0:T(8,128)(2,1)S(1)} %bitcast_select_fusion), channel_id=1, source_target_pairs={{0,16},{16,0},{1,17},{17,1},{2,18},{18,2},{3,19},{19,3},{4,20},{20... | collective-permute-start | bytes 18440 | tf_op jit(solution)/shard_map/ppermute | solution.py:1300
  59.8 29.4 %collective-permute-start.11 = (bf16[8,416,128]{2,1,0:T(8,128)(2,1)S(1)}, bf16[8,416,128]{2,1,0:T(8,128)(2,1)S(1)}, u32[]{:S(2)}, u32[]{:S(2)}) collective-permute-start(bf16[8,416,128]{2,1,0:T(8,128)(2,1)S(1)} %constant_dynamic-update-slice_fusion.5.refs_0_), channel_id=1, source_target_pairs={{0,16},{16,0},{1,17},{17,1},{2,18},{18,2},{3,19},{19,3},{4,20},{20... | collective-permute-start | bytes 2555912 | tf_op jit(solution)/shard_map/ppermute | solution.py:1300
  74.9 14.3 %collective-permute-start.12 = (bf16[8,416,128]{2,1,0:T(8,128)(2,1)S(1)}, bf16[8,416,128]{2,1,0:T(8,128)(2,1)S(1)}, u32[]{:S(2)}, u32[]{:S(2)}) collective-permute-start(bf16[8,416,128]{2,1,0:T(8,128)(2,1)S(1)} %collective-permute-done.10.refs_1_), channel_id=1, source_target_pairs={{0,16},{16,0},{1,17},{17,1},{2,18},{18,2},{3,19},{19,3},{4,20},{20... | collective-permute-start | bytes 2555912 | tf_op jit(solution)/shard_map/ppermute | solution.py:1300
  111.6 12.7 %collective-permute-start.16 = (bf16[8,192]{1,0:T(8,128)(2,1)S(1)}, bf16[8,192]{1,0:T(8,128)(2,1)S(1)}, u32[]{:S(2)}, u32[]{:S(2)}) collective-permute-start(bf16[8,192]{1,0:T(8,128)(2,1)S(1)} %bitcast_select_fusion.1), channel_id=1, source_target_pairs={{0,16},{16,0},{1,17},{17,1},{2,18},{18,2},{3,19},{19,3},{4,20},{20... | collective-permute-start | bytes 9224 | tf_op jit(solution)/shard_map/ppermute | solution.py:1300
  111.9 12.5 %collective-permute-start.15 = (bf16[8,384]{1,0:T(8,128)(2,1)}, bf16[8,384]{1,0:T(8,128)(2,1)S(1)}, u32[]{:S(2)}, u32[]{:S(2)}) collective-permute-start(bf16[8,384]{1,0:T(8,128)(2,1)} %get-tuple-element.250), channel_id=1, source_target_pairs={{0,16},{16,0},{1,17},{17,1},{2,18},{18,2},{3,19},{19,3},{4,20},{20... | collective-permute-start | bytes 18440 | tf_op jit(solution)/shard_map/ppermute | solution.py:1300
  124.0 16.3 %collective-permute-start.17 = (bf16[8,384]{1,0:T(8,128)(2,1)}, bf16[8,384]{1,0:T(8,128)(2,1)S(1)}, u32[]{:S(2)}, u32[]{:S(2)}) collective-permute-start(bf16[8,384]{1,0:T(8,128)(2,1)} %get-tuple-element.265), channel_id=1, source_target_pairs={{0,16},{16,0},{1,17},{17,1},{2,18},{18,2},{3,19},{19,3},{4,20},{20... | collective-permute-start | bytes 18440 | tf_op jit(solution)/shard_map/ppermute | solution.py:1300
  173.9 29.5 %collective-permute-start.20 = (bf16[16,416,128]{2,1,0:T(8,128)(2,1)}, bf16[16,416,128]{2,1,0:T(8,128)(2,1)S(1)}, u32[]{:S(2)}, u32[]{:S(2)}) collective-permute-start(bf16[16,416,128]{2,1,0:T(8,128)(2,1)} %get-tuple-element.308), channel_id=1, source_target_pairs={{0,16},{16,0},{1,17},{17,1},{2,18},{18,2},{3,19},{19,3},{4,20},{20... | collective-permute-start | bytes 5111816 | tf_op jit(solution)/shard_map/ppermute | solution.py:1300
  203.1 4.7 %collective-permute-start.22 = (bf16[8,192]{1,0:T(8,128)(2,1)S(1)}, bf16[8,192]{1,0:T(8,128)(2,1)S(1)}, u32[]{:S(2)}, u32[]{:S(2)}) collective-permute-start(bf16[8,192]{1,0:T(8,128)(2,1)S(1)} %copy-done.41), channel_id=1, source_target_pairs={{0,16},{16,0},{1,17},{17,1},{2,18},{18,2},{3,19},{19,3},{4,20},{20... | collective-permute-start | bytes 9224 | tf_op jit(solution)/shard_map/ppermute | solution.py:1300
  204.7 25.5 %collective-permute-start.23 = (bf16[8,416,128]{2,1,0:T(8,128)(2,1)}, bf16[8,416,128]{2,1,0:T(8,128)(2,1)S(1)}, u32[]{:S(2)}, u32[]{:S(2)}) collective-permute-start(bf16[8,416,128]{2,1,0:T(8,128)(2,1)} %add_convert_fusion), channel_id=1, source_target_pairs={{0,1},{1,0},{2,3},{3,2},{4,5},{5,4},{6,7},{7,6},{8,9},{9,8},{10,11... | collective-permute-start | bytes 2555912 | tf_op jit(solution)/shard_map/ppermute | solution.py:1314
  206.9 23.3 %collective-permute-start.24 = (bf16[4,416,128]{2,1,0:T(8,128)(2,1)S(1)}, bf16[4,416,128]{2,1,0:T(8,128)(2,1)S(1)}, u32[]{:S(2)}, u32[]{:S(2)}) collective-permute-start(bf16[4,416,128]{2,1,0:T(8,128)(2,1)S(1)} %add_convert_fusion.3), channel_id=1, source_target_pairs={{0,1},{1,0},{2,3},{3,2},{4,5},{5,4},{6,7},{7,6},{8,9},{9,8},{10,11... | collective-permute-start | bytes 1277960 | tf_op jit(solution)/shard_map/ppermute | solution.py:1314
  235.2 3.7 %collective-permute-start.25 = (bf16[8,416,128]{2,1,0:T(8,128)(2,1)}, bf16[8,416,128]{2,1,0:T(8,128)(2,1)}, u32[]{:S(2)}, u32[]{:S(2)}) collective-permute-start(bf16[8,416,128]{2,1,0:T(8,128)(2,1)} %get-tuple-element.338), channel_id=1, source_target_pairs={{0,16},{16,0},{1,17},{17,1},{2,18},{18,2},{3,19},{19,3},{4,20},{20... | collective-permute-start | bytes 2555912 | tf_op jit(solution)/shard_map/ppermute | solution.py:1300
  236.6 5.9 %collective-permute-start.28 = (bf16[2,416,128]{2,1,0:T(8,128)(2,1)S(1)}, bf16[2,416,128]{2,1,0:T(8,128)(2,1)S(1)}, u32[]{:S(2)}, u32[]{:S(2)}) collective-permute-start(bf16[2,416,128]{2,1,0:T(8,128)(2,1)S(1)} %add_convert_fusion.5), channel_id=1, source_target_pairs={{0,2},{1,3},{2,0},{3,1},{4,6},{5,7},{6,4},{7,5},{8,10},{9,11},{10,... | collective-permute-start | bytes 638984 | tf_op jit(solution)/shard_map/ppermute | solution.py:1314
  238.2 13.3 %collective-permute-start.32 = (bf16[4,416,128]{2,1,0:T(8,128)(2,1)S(1)}, bf16[4,416,128]{2,1,0:T(8,128)(2,1)S(1)}, u32[]{:S(2)}, u32[]{:S(2)}) collective-permute-start(bf16[4,416,128]{2,1,0:T(8,128)(2,1)S(1)} %add_convert_fusion.1), channel_id=1, source_target_pairs={{0,2},{1,3},{2,0},{3,1},{4,6},{5,7},{6,4},{7,5},{8,10},{9,11},{10,... | collective-permute-start | bytes 1277960 | tf_op jit(solution)/shard_map/ppermute | solution.py:1314
  240.0 14.0 %collective-permute-start.26 = (bf16[4,416,128]{2,1,0:T(8,128)(2,1)S(1)}, bf16[4,416,128]{2,1,0:T(8,128)(2,1)S(1)}, u32[]{:S(2)}, u32[]{:S(2)}) collective-permute-start(bf16[4,416,128]{2,1,0:T(8,128)(2,1)S(1)} %add_convert_fusion.2), channel_id=1, source_target_pairs={{0,1},{1,0},{2,3},{3,2},{4,5},{5,4},{6,7},{7,6},{8,9},{9,8},{10,11... | collective-permute-start | bytes 1277960 | tf_op jit(solution)/shard_map/ppermute | solution.py:1314
  251.4 15.7 %collective-permute-start.29 = (bf16[1,416,128]{2,1,0:T(8,128)(2,1)S(1)}, bf16[1,416,128]{2,1,0:T(8,128)(2,1)S(1)}, u32[]{:S(2)}, u32[]{:S(2)}) collective-permute-start(bf16[1,416,128]{2,1,0:T(8,128)(2,1)S(1)} %add_convert_fusion.9), channel_id=1, source_target_pairs={{0,4},{1,5},{2,6},{3,7},{4,0},{5,1},{6,2},{7,3},{8,12},{9,13},{10,... | collective-permute-start | bytes 319496 | tf_op jit(solution)/shard_map/ppermute | solution.py:1305
  255.1 5.9 %collective-permute-start.27 = (bf16[2,416,128]{2,1,0:T(8,128)(2,1)S(1)}, bf16[2,416,128]{2,1,0:T(8,128)(2,1)S(1)}, u32[]{:S(2)}, u32[]{:S(2)}) collective-permute-start(bf16[2,416,128]{2,1,0:T(8,128)(2,1)S(1)} %add_convert_fusion.6), channel_id=1, source_target_pairs={{0,2},{1,3},{2,0},{3,1},{4,6},{5,7},{6,4},{7,5},{8,10},{9,11},{10,... | collective-permute-start | bytes 638984 | tf_op jit(solution)/shard_map/ppermute | solution.py:1314
  256.6 8.2 %collective-permute-start.33 = (bf16[2,416,128]{2,1,0:T(8,128)(2,1)S(1)}, bf16[2,416,128]{2,1,0:T(8,128)(2,1)S(1)}, u32[]{:S(2)}, u32[]{:S(2)}) collective-permute-start(bf16[2,416,128]{2,1,0:T(8,128)(2,1)S(1)} %add_convert_fusion.4), channel_id=1, source_target_pairs={{0,4},{1,5},{2,6},{3,7},{4,0},{5,1},{6,2},{7,3},{8,12},{9,13},{10,... | collective-permute-start | bytes 638984 | tf_op jit(solution)/shard_map/ppermute | solution.py:1305
  262.0 5.2 %collective-permute-start.30 = (bf16[1,416,128]{2,1,0:T(8,128)(2,1)S(1)}, bf16[1,416,128]{2,1,0:T(8,128)(2,1)S(1)}, u32[]{:S(2)}, u32[]{:S(2)}) collective-permute-start(bf16[1,416,128]{2,1,0:T(8,128)(2,1)S(1)} %add_convert_fusion.8), channel_id=1, source_target_pairs={{0,4},{1,5},{2,6},{3,7},{4,0},{5,1},{6,2},{7,3},{8,12},{9,13},{10,... | collective-permute-start | bytes 319496 | tf_op jit(solution)/shard_map/ppermute | solution.py:1305
  264.8 8.8 %collective-permute-start.34 = (bf16[1,416,128]{2,1,0:T(8,128)(2,1)S(1)}, bf16[1,416,128]{2,1,0:T(8,128)(2,1)S(1)}, u32[]{:S(2)}, u32[]{:S(2)}) collective-permute-start(bf16[1,416,128]{2,1,0:T(8,128)(2,1)S(1)} %add_convert_fusion.7), channel_id=1, source_target_pairs={{0,8},{1,9},{2,10},{3,11},{4,12},{5,13},{6,14},{7,15},{8,0},{9,1},... | collective-permute-start | bytes 319496 | tf_op jit(solution)/shard_map/ppermute | solution.py:1305
  269.0 7.3 %collective-permute-start.31 = (bf16[416,128]{1,0:T(8,128)(2,1)S(1)}, bf16[416,128]{1,0:T(8,128)(2,1)S(1)}, u32[]{:S(2)}, u32[]{:S(2)}) collective-permute-start(bf16[416,128]{1,0:T(8,128)(2,1)S(1)} %get-tuple-element.367), channel_id=1, source_target_pairs={{0,8},{1,9},{2,10},{3,11},{4,12},{5,13},{6,14},{7,15},{8,0},{9,1},... | collective-permute-start | bytes 319496 | tf_op jit(solution)/shard_map/ppermute | solution.py:1305
  281.7 4.6 %collective-permute-start.36 = (f32[8,128]{1,0:T(8,128)S(1)}, f32[8,128]{1,0:T(8,128)S(1)}, u32[]{:S(2)}, u32[]{:S(2)}) collective-permute-start(f32[8,128]{1,0:T(8,128)S(1)} %add.204), channel_id=1, source_target_pairs={{0,1},{1,0},{2,3},{3,2},{4,5},{5,4},{6,7},{7,6},{8,9},{9,8},{10,11... | collective-permute-start | bytes 12296 | tf_op jit(solution)/shard_map/ppermute | solution.py:1305
  286.3 3.7 %collective-permute-start.38 = (f32[8,128]{1,0:T(8,128)S(1)}, f32[8,128]{1,0:T(8,128)S(1)}, u32[]{:S(2)}, u32[]{:S(2)}) collective-permute-start(f32[8,128]{1,0:T(8,128)S(1)} %add.205), channel_id=1, source_target_pairs={{0,2},{1,3},{2,0},{3,1},{4,6},{5,7},{6,4},{7,5},{8,10},{9,11},{10,... | collective-permute-start | bytes 12296 | tf_op jit(solution)/shard_map/ppermute | solution.py:1305
  293.6 4.5 %collective-permute-start.40 = (f32[8,128]{1,0:T(8,128)S(1)}, f32[8,128]{1,0:T(8,128)S(1)}, u32[]{:S(2)}, u32[]{:S(2)}) collective-permute-start(f32[8,128]{1,0:T(8,128)S(1)} %add.207), channel_id=1, source_target_pairs={{0,8},{1,9},{2,10},{3,11},{4,12},{5,13},{6,14},{7,15},{8,0},{9,1},... | collective-permute-start | bytes 12296 | tf_op jit(solution)/shard_map/ppermute | solution.py:1305
  (54 other events, 408.4 us)

commit v2 on v1

--- a/solution.py
+++ b/solution.py
@@ -1045,17 +1045,14 @@
         part = mm_t(gu, fc1_w[:, cols])
         gnormed[...] = part if first else gnormed[...] + part
 
-    def two(number, carry):
-        one(2 * number, False)
-        one(2 * number + 1, False)
+    def looped(number, carry):
+        one(number, False)
         return carry
 
     chunks = fc1_w.shape[1] // chunk
-    if chunks > 2:
+    if fc1_w.shape[1] > 1024:
         gnormed[...] = jnp.zeros_like(gnormed)
-        lax.fori_loop(0, chunks // 2, two, 0)
-        for number in range(chunks // 2 * 2, chunks):
-            one(number, False)
+        lax.fori_loop(0, chunks, looped, 0)
     else:
         for number in range(chunks):
             one(number, number == 0)
@@ -1205,7 +1202,7 @@
     outs += grad_outs(params, label, GRAD_MLP)
     outs += grad_outs(params, label, TO) + grad_outs(params, other, TO)
     values = pl.pallas_call(
-        functools.partial(mlp_back_kernel, pair, tall, 384),
+        functools.partial(mlp_back_kernel, pair, tall, 768),
         grid=(crops // pair,),
         out_shape=[shape for spec, shape in outs],
         in_specs=[smem, pl.BlockSpec((pair, tall, width), lambda i: (i, 0, 0))]

time: 304 us -> 301 us (level)
  no operation moved by 1% of the time
where the time goes in v2:
time: 301 us; the launch traced here: 300 us
  Pallas kernels  172 us (57%)
  waiting for transfers between devices  46.8 us (16%)
  starting transfers between devices  36.8 us (12%)
  local copies, waits for them, and re-layouts  26.4 us (9%)
  other arithmetic  15.8 us (5%)
    ppermute x13, waiting for transfers between devices, partner(): return lax.ppermute(value, 'dp', [(i, i ^ bit) for i in range(count)])  29.4 us
    pallas_call x1, Pallas kernels, mlp_back(): pl.pallas_call(functools.partial(mlp_back_kernel, pair, tall, 768), grid=...  24.6 us
    pallas_call x1, Pallas kernels, attention_back(): pl.pallas_call(functools.partial(attention_back_kernel, pair, tall), grid...  24.6 us
    pallas_call x2, Pallas kernels, cross(): pl.pallas_call(functools.partial(cross_kernel, length, tall, crops), out_...  24.5 us
    pallas_call x1, Pallas kernels, block_back(): pl.pallas_call(functools.partial(block_back_kernel, pair, tall, 384), gri...  21.7 us
    ppermute x13, starting transfers between devices, partner(): return lax.ppermute(value, 'dp', [(i, i ^ bit) for i in range(count)])  20.9 us
    pallas_call x1, Pallas kernels, mlp_only(): pl.pallas_call(functools.partial(mlp_kernel, pair, tall, 384), grid=(crop...  15.5 us
    ppermute x10, waiting for transfers between devices, side_partner(): return lax.ppermute(value, ('branch', 'dp'), pairs)  14.7 us
  transfers between devices with their start and end apart: 41, of which 17 were waited for; matrix products, arithmetic and copies ran while one was open for 9% of the time, Pallas kernels for 44%

profile of v2, /device:TPU:0, one launch (start us, length us, event | category | flops | bytes accessed | tf_op | source)
XLA Modules:
  0.0 300.3 jit_solution(15799094220840428228)
XLA Ops:
  0.7 1.9 pad_bitcast_fusion.shard_ref
  4.5 2.3 align.1
  10.2 3.6 %collective-permute-start.1 = (bf16[1,416,128]{2,1,0:T(8,128)(2,1)S(1)}, bf16[1,416,128]{2,1,0:T(8,128)(2,1)S(1)}, u32[]{:S(2)}, u32[]{:S(2)}) collective-permute-start(bf16[1,416,128]{2,1,0:T(8,128)(2,1)S(1)} %get-tuple-element.370), channel_id=1, source_target_pairs={{0,8},{1,9},{2,10},{3,11},{4,12},{5,13},{6,14},{7,15},{8,0},{9,1},... | collective-permute-start | bytes 319496 | tf_op jit(solution)/shard_map/ppermute | solution.py:1302
  23.3 3.7 %collective-permute-done.2 = bf16[2,416,128]{2,1,0:T(8,128)(2,1)S(1)} collective-permute-done((bf16[2,416,128]{2,1,0:T(8,128)(2,1)S(1)}, bf16[2,416,128]{2,1,0:T(8,128)(2,1)S(1)}, u32[]{:S(2)}, u32[]{:S(2)}) %collective-permute-start.2) | collective-permute-done | bytes 213024 | tf_op jit(solution)/shard_map/ppermute | solution.py:1302
  28.4 2.7 collective-permute-start.3
  31.8 3.9 %collective-permute-done.3 = bf16[1,416,128]{2,1,0:T(8,128)(2,1)S(1)} collective-permute-done((bf16[1,416,128]{2,1,0:T(8,128)(2,1)S(1)}, bf16[1,416,128]{2,1,0:T(8,128)(2,1)S(1)}, u32[]{:S(2)}, u32[]{:S(2)}) %collective-permute-start.3) | collective-permute-done | bytes 106528 | tf_op jit(solution)/shard_map/ppermute | solution.py:1302
  38.3 5.9 %collective-permute-done.4 = bf16[2,416,128]{2,1,0:T(8,128)(2,1)S(1)} collective-permute-done((bf16[2,416,128]{2,1,0:T(8,128)(2,1)S(1)}, bf16[2,416,128]{2,1,0:T(8,128)(2,1)S(1)}, u32[]{:S(2)}, u32[]{:S(2)}) %collective-permute-start.4) | collective-permute-done | bytes 213024 | tf_op jit(solution)/shard_map/ppermute | solution.py:1302
  44.9 4.4 %collective-permute-done.6.refs_1_ = bf16[8,416,128]{2,1,0:T(8,128)(2,1)S(1)} collective-permute-done((bf16[8,416,128]{2,1,0:T(8,128)(2,1)S(1)}, bf16[8,416,128]{2,1,0:T(8,128)(2,1)S(1)}, u32[]{:S(2)}, u32[]{:S(2)}) %collective-permute-start.6) | collective-permute-done | bytes 852000 | tf_op jit(solution)/shard_map/ppermute | solution.py:1311
  52.8 4.9 %unflatten0.1 = (f32[2,192]{1,0:T(2,128)}, bf16[192,576]{1,0:T(8,128)(2,1)}, f32[1,576]{1,0:T(1,128)}, bf16[192,192]{1,0:T(8,128)(2,1)}, f32[1,192]{1,0:T(1,128)...) custom-call(s32[2]{0:T(128)} %pad_add_fusion.core_ref.where_ref, ...), custom_call_target="tpu_custom_call" | custom-call | flops 1000000 | bytes 8000000 | tf_op jit(solution)/shard_map/unflatten0/pallas_call | solution.py:484
  60.3 14.6 %block_s.1 = (bf16[1280,192]{1,0:T(8,128)(2,1)}, bf16[1280,576]{1,0:T(8,128)(2,1)}, bf16[8,6,160,160]{3,2,1,0:T(8,128)(2,1)}, bf16[1280,192]{1,0:T(8,128)(2,1)},...) custom-call(bf16[8,160,192]{2,1,0:T(8,128)(2,1)} %pad.19.tok_ref.ref, ...), custom_call_target="tpu_custom_call" | custom-call | flops 9059696640 | bytes 10000000 | tf_op jit(solution)/shard_map/block_s/pallas_call | solution.py:743
  74.9 14.2 %attention_l.1 = (bf16[1664,384]{1,0:T(8,128)(2,1)}, bf16[1664,1152]{1,0:T(8,128)(2,1)}, bf16[8,6,208,208]{3,2,1,0:T(8,128)(2,1)}, bf16[1664,384]{1,0:T(8,128)(2...) custom-call(bf16[8,208,384]{2,1,0:T(8,128)(2,1)} %pad.20.tok_ref.refs_0_, ...), custom_call_target="tpu_custom_call" | custom-call | flops 15703474176 | bytes 20000000 | tf_op jit(solution)/shard_map/attention_l/pallas_call | solution.py:760
  90.4 5.3 %unflatten1.1 = (f32[1,1536]{1,0:T(1,128)}, bf16[1536,384]{1,0:T(8,128)(2,1)}, f32[1,384]{1,0:T(1,128)}, f32[2,192]{1,0:T(2,128)}, bf16[192,384]{1,0:T(8,128)(2,...) custom-call(s32[2]{0:T(128)} %pad_add_fusion.core_ref.where_ref, ...), custom_call_target="tpu_custom_call" | custom-call | flops 1000000 | bytes 8000000 | tf_op jit(solution)/shard_map/unflatten1/pallas_call | solution.py:484
  95.7 15.5 %mlp_l.1 = (bf16[1664,1536]{1,0:T(8,128)(2,1)}, bf16[1664,1536]{1,0:T(8,128)(2,1)}, f32[1664,384]{1,0:T(8,128)}, f32[8,384]{1,0:T(8,128)}, bf16[8,192]{1,0:T(8,128)(2,1)}, /*index=5*/bf16[8,384]{1,0:T(8,128)(2,1)}) custom-call(f32[1664,384]{1,0:T(8,128)} %get-tuple-element.218.mid_ref.refs_3_, bf16[1664,384]{1,0:T(8,128)(2,1)} %get-tuple-element.219.n2_ref.refs_4_, ...), custom_call_target="tpu_custom_call" | custom-call | flops 31406948352 | bytes 20000000 | tf_op jit(solution)/shard_map/mlp_l/pallas_call | solution.py:784
  113.3 10.7 %cross_l.1 = (bf16[8,384]{1,0:T(8,128)(2,1)}, bf16[8,192]{1,0:T(8,128)(2,1)}, f32[1280,192]{1,0:T(8,128)}, f32[2,192]{1,0:T(2,128)}, f32[192,192]{1,0:T(8,128)},...) custom-call(bf16[8,192]{1,0:T(8,128)(2,1)} %copy-done.35, ...), custom_call_target="tpu_custom_call" | custom-call | flops 188743680 | bytes 8000000 | tf_op jit(solution)/shard_map/cross_l/pallas_call | solution.py:979
  125.0 13.8 %cross_s.1 = (bf16[8,192]{1,0:T(8,128)(2,1)}, bf16[8,384]{1,0:T(8,128)(2,1)}, f32[1664,384]{1,0:T(8,128)}, f32[2,384]{1,0:T(2,128)}, f32[384,384]{1,0:T(8,128)},...) custom-call(bf16[8,384]{1,0:T(8,128)(2,1)} %copy-done.34, ...), custom_call_target="tpu_custom_call" | custom-call | flops 981467136 | bytes 8000000 | tf_op jit(solution)/shard_map/cross_s/pallas_call | solution.py:979
  140.9 24.6 %mlp_back_l.1 = (bf16[1,8,197,384]{3,2,1,0:T(8,128)(2,1)}, f32[1664,384]{1,0:T(8,128)}, f32[8,192]{1,0:T(8,128)}, f32[2,384]{1,0:T(2,128)}, f32[384,1536]{1,0:T(...) custom-call(s32[1]{0:T(128)} %bitcast.15.live_ref, ...), custom_call_target="tpu_custom_call" | custom-call | flops 62813896704 | bytes 20000000 | tf_op jit(solution)/shard_map/mlp_back_l/pallas_call | solution.py:1204
  165.4 5.9 %flatten2.1 = (bf16[8,416,128]{2,1,0:T(8,128)(2,1)}, bf16[8,416,128]{2,1,0:T(8,128)(2,1)}, bf16[16,416,128]{2,1,0:T(8,128)(2,1)}) custom-call(s32[2]{0:T(128)} %pad_add_fusion.core_ref.where_ref, s32[32]{0:T(128)} %constant.54.clone.base_ref, f32[1,1536]{1,0:T(1,128)} %get-tuple-element.270.refs_0_.refs_6_, f32[1536,384]{1,0:T(8,128)} %get-tuple-element.271.refs_1_, ...), custom_call_target="tpu_custom_call" | custom-call | flops 1000000 | bytes 10000000 | tf_op jit(solution)/shard_map/flatten2/pallas_call | solution.py:538
  171.7 24.6 %attention_back_l.1 = (bf16[1,8,197,384]{3,2,1,0:T(8,128)(2,1)}, f32[2,384]{1,0:T(2,128)}, f32[384,1152]{1,0:T(8,128)}, f32[1,1152]{1,0:T(1,128)}, f32[384,384]{1,0:T(8,128)}, /*index=5*/f32[1,384]{1,0:T(1,128)}) custom-call(f32[1664,384]{1,0:T(8,128)} %get-tuple-element.302.gmid_ref, bf16[8,208,384]{2,1,0:T(8,128)(2,1)} %pad.20.tok_ref.refs_0_, ...), custom_call_target="tpu_custom_call" | custom-call | flops 31406948352 | bytes 20000000 | tf_op jit(solution)/shard_map/attention_back_l/pallas_call | solution.py:1233
  196.3 4.0 %flatten1.1 = (bf16[4,416,128]{2,1,0:T(8,128)(2,1)}, bf16[4,416,128]{2,1,0:T(8,128)(2,1)}, bf16[8,416,128]{2,1,0:T(8,128)(2,1)}) custom-call(s32[2]{0:T(128)} %pad_add_fusion.core_ref.where_ref, s32[32]{0:T(128)} %constant.54.clone.base_ref, f32[384,1152]{1,0:T(8,128)} %get-tuple-element.310.refs_0_.refs_11_, f32[1,1152]{1,0:T(1,128)} %get-tuple-element.311.refs_1_, ...), custom_call_target="tpu_custom_call" | custom-call | flops 1000000 | bytes 10000000 | tf_op jit(solution)/shard_map/flatten1/pallas_call | solution.py:538
  205.9 21.7 %block_back_s.1 = (bf16[1,8,145,192]{3,2,1,0:T(8,128)(2,1)}, bf16[1,8,145,192]{3,2,1,0:T(8,128)(2,1)}, f32[2,192]{1,0:T(2,128)}, f32[192,768]{1,0:T(8,128)}, f32...) custom-call(s32[1]{0:T(128)} %bitcast.2.live_ref, ...), custom_call_target="tpu_custom_call" | custom-call | flops 18119393280 | bytes 20000000 | tf_op jit(solution)/shard_map/block_back_s/pallas_call | solution.py:1264
  228.4 4.3 %flatten0.1 = (bf16[4,416,128]{2,1,0:T(8,128)(2,1)}, bf16[4,416,128]{2,1,0:T(8,128)(2,1)}, bf16[8,416,128]{2,1,0:T(8,128)(2,1)}) custom-call(s32[2]{0:T(128)} %pad_add_fusion.core_ref.where_ref, s32[32]{0:T(128)} %constant.54.clone.base_ref, f32[2,192]{1,0:T(2,128)} %get-tuple-element.326.refs_0_, f32[192,576]{1,0:T(8,128)} %get-tuple-element.327.refs_1_, ...), custom_call_target="tpu_custom_call" | custom-call | flops 1000000 | bytes 10000000 | tf_op jit(solution)/shard_map/flatten0/pallas_call | solution.py:538
  240.9 8.0 %collective-permute-done.32.refs_3_ = bf16[4,416,128]{2,1,0:T(8,128)(2,1)S(1)} collective-permute-done((bf16[4,416,128]{2,1,0:T(8,128)(2,1)S(1)}, bf16[4,416,128]{2,1,0:T(8,128)(2,1)S(1)}, u32[]{:S(2)}, u32[]{:S(2)}) %collective-permute-start.32) | collective-permute-done | bytes 426016 | tf_op jit(solution)/shard_map/ppermute | solution.py:1311
  262.3 2.3 collective-permute-start.34
  264.7 1.8 fusion.1
  266.4 3.0 collective-permute-start.31
  271.1 2.6 collective-permute-done.31.last_ref
  274.4 2.5 settle.1
  281.2 2.6 unalign.1
  284.9 2.5 collective-permute-done.38
  287.5 3.6 %collective-permute-done.39 = f32[8,128]{1,0:T(8,128)S(1)} collective-permute-done((f32[8,128]{1,0:T(8,128)S(1)}, f32[8,128]{1,0:T(8,128)S(1)}, u32[]{:S(2)}, u32[]{:S(2)}) %collective-permute-start.39) | collective-permute-done | bytes 4128 | tf_op jit(solution)/shard_map/ppermute | solution.py:1302
  292.8 2.8 collective-permute-done.40
  296.9 2.3 fusion.5
  (203 shorter events, 70.6 us)
Async XLA Ops:
  10.2 9.6 %collective-permute-start.1 = (bf16[1,416,128]{2,1,0:T(8,128)(2,1)S(1)}, bf16[1,416,128]{2,1,0:T(8,128)(2,1)S(1)}, u32[]{:S(2)}, u32[]{:S(2)}) collective-permute-start(bf16[1,416,128]{2,1,0:T(8,128)(2,1)S(1)} %get-tuple-element.370), channel_id=1, source_target_pairs={{0,8},{1,9},{2,10},{3,11},{4,12},{5,13},{6,14},{7,15},{8,0},{9,1},... | collective-permute-start | bytes 319496 | tf_op jit(solution)/shard_map/ppermute | solution.py:1302
  19.8 7.2 %collective-permute-start.2 = (bf16[2,416,128]{2,1,0:T(8,128)(2,1)S(1)}, bf16[2,416,128]{2,1,0:T(8,128)(2,1)S(1)}, u32[]{:S(2)}, u32[]{:S(2)}) collective-permute-start(bf16[2,416,128]{2,1,0:T(8,128)(2,1)S(1)} %pad_maximum_fusion.2), channel_id=1, source_target_pairs={{0,4},{1,5},{2,6},{3,7},{4,0},{5,1},{6,2},{7,3},{8,12},{9,13},{10,... | collective-permute-start | bytes 638984 | tf_op jit(solution)/shard_map/ppermute | solution.py:1302
  27.0 9.4 %collective-permute-start.5 = (bf16[4,416,128]{2,1,0:T(8,128)(2,1)S(1)}, bf16[4,416,128]{2,1,0:T(8,128)(2,1)S(1)}, u32[]{:S(2)}, u32[]{:S(2)}) collective-permute-start(bf16[4,416,128]{2,1,0:T(8,128)(2,1)S(1)} %pad_maximum_fusion.1), channel_id=1, source_target_pairs={{0,2},{1,3},{2,0},{3,1},{4,6},{5,7},{6,4},{7,5},{8,10},{9,11},{10,... | collective-permute-start | bytes 1277960 | tf_op jit(solution)/shard_map/ppermute | solution.py:1311
  28.4 7.3 %collective-permute-start.3 = (bf16[1,416,128]{2,1,0:T(8,128)(2,1)S(1)}, bf16[1,416,128]{2,1,0:T(8,128)(2,1)S(1)}, u32[]{:S(2)}, u32[]{:S(2)}) collective-permute-start(bf16[1,416,128]{2,1,0:T(8,128)(2,1)S(1)} %get-tuple-element.194), channel_id=1, source_target_pairs={{0,8},{1,9},{2,10},{3,11},{4,12},{5,13},{6,14},{7,15},{8,0},{9,1},... | collective-permute-start | bytes 319496 | tf_op jit(solution)/shard_map/ppermute | solution.py:1302
  36.5 12.8 %collective-permute-start.6 = (bf16[8,416,128]{2,1,0:T(8,128)(2,1)S(1)}, bf16[8,416,128]{2,1,0:T(8,128)(2,1)S(1)}, u32[]{:S(2)}, u32[]{:S(2)}) collective-permute-start(bf16[8,416,128]{2,1,0:T(8,128)(2,1)S(1)} %pad_maximum_fusion.refs_0_), channel_id=1, source_target_pairs={{0,1},{1,0},{2,3},{3,2},{4,5},{5,4},{6,7},{7,6},{8,9},{9,8},{10,11... | collective-permute-start | bytes 2555912 | tf_op jit(solution)/shard_map/ppermute | solution.py:1311
  37.5 6.7 %collective-permute-start.4 = (bf16[2,416,128]{2,1,0:T(8,128)(2,1)S(1)}, bf16[2,416,128]{2,1,0:T(8,128)(2,1)S(1)}, u32[]{:S(2)}, u32[]{:S(2)}) collective-permute-start(bf16[2,416,128]{2,1,0:T(8,128)(2,1)S(1)} %get-tuple-element.371), channel_id=1, source_target_pairs={{0,4},{1,5},{2,6},{3,7},{4,0},{5,1},{6,2},{7,3},{8,12},{9,13},{10,... | collective-permute-start | bytes 638984 | tf_op jit(solution)/shard_map/ppermute | solution.py:1302
  44.9 7.0 %collective-permute-start.8 = (bf16[8,416,128]{2,1,0:T(8,128)(2,1)S(1)}, bf16[8,416,128]{2,1,0:T(8,128)(2,1)S(1)}, u32[]{:S(2)}, u32[]{:S(2)}) collective-permute-start(bf16[8,416,128]{2,1,0:T(8,128)(2,1)S(1)} %pad_maximum_fusion.refs_0_), channel_id=1, source_target_pairs={{0,16},{16,0},{1,17},{17,1},{2,18},{18,2},{3,19},{19,3},{4,20},{20... | collective-permute-start | bytes 2555912 | tf_op jit(solution)/shard_map/ppermute | solution.py:1297
  49.3 8.4 %collective-permute-start.7 = (bf16[4,416,128]{2,1,0:T(8,128)(2,1)}, bf16[4,416,128]{2,1,0:T(8,128)(2,1)}, u32[]{:S(2)}, u32[]{:S(2)}) collective-permute-start(bf16[4,416,128]{2,1,0:T(8,128)(2,1)} %constant_dynamic-update-slice_fusion.2), channel_id=1, source_target_pairs={{0,2},{1,3},{2,0},{3,1},{4,6},{5,7},{6,4},{7,5},{8,10},{9,11},{10,... | collective-permute-start | bytes 1277960 | tf_op jit(solution)/shard_map/ppermute | solution.py:1311
  58.8 16.1 %collective-permute-start.10 = (bf16[8,416,128]{2,1,0:T(8,128)(2,1)S(1)}, bf16[8,416,128]{2,1,0:T(8,128)(2,1)S(1)}, u32[]{:S(2)}, u32[]{:S(2)}) collective-permute-start(bf16[8,416,128]{2,1,0:T(8,128)(2,1)S(1)} %constant_dynamic-update-slice_fusion.5.refs_0_), channel_id=1, source_target_pairs={{0,1},{1,0},{2,3},{3,2},{4,5},{5,4},{6,7},{7,6},{8,9},{9,8},{10,11... | collective-permute-start | bytes 2555912 | tf_op jit(solution)/shard_map/ppermute | solution.py:1311
  59.8 52.4 %collective-permute-start.14 = (bf16[8,384]{1,0:T(8,128)(2,1)S(1)}, bf16[8,384]{1,0:T(8,128)(2,1)S(1)}, u32[]{:S(2)}, u32[]{:S(2)}) collective-permute-start(bf16[8,384]{1,0:T(8,128)(2,1)S(1)} %bitcast_select_fusion), channel_id=1, source_target_pairs={{0,16},{16,0},{1,17},{17,1},{2,18},{18,2},{3,19},{19,3},{4,20},{20... | collective-permute-start | bytes 18440 | tf_op jit(solution)/shard_map/ppermute | solution.py:1297
  59.8 29.4 %collective-permute-start.11 = (bf16[8,416,128]{2,1,0:T(8,128)(2,1)S(1)}, bf16[8,416,128]{2,1,0:T(8,128)(2,1)S(1)}, u32[]{:S(2)}, u32[]{:S(2)}) collective-permute-start(bf16[8,416,128]{2,1,0:T(8,128)(2,1)S(1)} %constant_dynamic-update-slice_fusion.5.refs_0_), channel_id=1, source_target_pairs={{0,16},{16,0},{1,17},{17,1},{2,18},{18,2},{3,19},{19,3},{4,20},{20... | collective-permute-start | bytes 2555912 | tf_op jit(solution)/shard_map/ppermute | solution.py:1297
  74.9 14.3 %collective-permute-start.12 = (bf16[8,416,128]{2,1,0:T(8,128)(2,1)S(1)}, bf16[8,416,128]{2,1,0:T(8,128)(2,1)S(1)}, u32[]{:S(2)}, u32[]{:S(2)}) collective-permute-start(bf16[8,416,128]{2,1,0:T(8,128)(2,1)S(1)} %collective-permute-done.10.refs_1_), channel_id=1, source_target_pairs={{0,16},{16,0},{1,17},{17,1},{2,18},{18,2},{3,19},{19,3},{4,20},{20... | collective-permute-start | bytes 2555912 | tf_op jit(solution)/shard_map/ppermute | solution.py:1297
  111.6 12.7 %collective-permute-start.16 = (bf16[8,192]{1,0:T(8,128)(2,1)S(1)}, bf16[8,192]{1,0:T(8,128)(2,1)S(1)}, u32[]{:S(2)}, u32[]{:S(2)}) collective-permute-start(bf16[8,192]{1,0:T(8,128)(2,1)S(1)} %bitcast_select_fusion.1), channel_id=1, source_target_pairs={{0,16},{16,0},{1,17},{17,1},{2,18},{18,2},{3,19},{19,3},{4,20},{20... | collective-permute-start | bytes 9224 | tf_op jit(solution)/shard_map/ppermute | solution.py:1297
  111.9 12.5 %collective-permute-start.15 = (bf16[8,384]{1,0:T(8,128)(2,1)}, bf16[8,384]{1,0:T(8,128)(2,1)S(1)}, u32[]{:S(2)}, u32[]{:S(2)}) collective-permute-start(bf16[8,384]{1,0:T(8,128)(2,1)} %get-tuple-element.250), channel_id=1, source_target_pairs={{0,16},{16,0},{1,17},{17,1},{2,18},{18,2},{3,19},{19,3},{4,20},{20... | collective-permute-start | bytes 18440 | tf_op jit(solution)/shard_map/ppermute | solution.py:1297
  124.0 16.3 %collective-permute-start.17 = (bf16[8,384]{1,0:T(8,128)(2,1)}, bf16[8,384]{1,0:T(8,128)(2,1)S(1)}, u32[]{:S(2)}, u32[]{:S(2)}) collective-permute-start(bf16[8,384]{1,0:T(8,128)(2,1)} %get-tuple-element.265), channel_id=1, source_target_pairs={{0,16},{16,0},{1,17},{17,1},{2,18},{18,2},{3,19},{19,3},{4,20},{20... | collective-permute-start | bytes 18440 | tf_op jit(solution)/shard_map/ppermute | solution.py:1297
  171.4 29.5 %collective-permute-start.20 = (bf16[16,416,128]{2,1,0:T(8,128)(2,1)}, bf16[16,416,128]{2,1,0:T(8,128)(2,1)S(1)}, u32[]{:S(2)}, u32[]{:S(2)}) collective-permute-start(bf16[16,416,128]{2,1,0:T(8,128)(2,1)} %get-tuple-element.308), channel_id=1, source_target_pairs={{0,16},{16,0},{1,17},{17,1},{2,18},{18,2},{3,19},{19,3},{4,20},{20... | collective-permute-start | bytes 5111816 | tf_op jit(solution)/shard_map/ppermute | solution.py:1297
  200.6 4.7 %collective-permute-start.22 = (bf16[8,192]{1,0:T(8,128)(2,1)S(1)}, bf16[8,192]{1,0:T(8,128)(2,1)S(1)}, u32[]{:S(2)}, u32[]{:S(2)}) collective-permute-start(bf16[8,192]{1,0:T(8,128)(2,1)S(1)} %copy-done.41), channel_id=1, source_target_pairs={{0,16},{16,0},{1,17},{17,1},{2,18},{18,2},{3,19},{19,3},{4,20},{20... | collective-permute-start | bytes 9224 | tf_op jit(solution)/shard_map/ppermute | solution.py:1297
  202.2 25.5 %collective-permute-start.23 = (bf16[8,416,128]{2,1,0:T(8,128)(2,1)}, bf16[8,416,128]{2,1,0:T(8,128)(2,1)S(1)}, u32[]{:S(2)}, u32[]{:S(2)}) collective-permute-start(bf16[8,416,128]{2,1,0:T(8,128)(2,1)} %add_convert_fusion), channel_id=1, source_target_pairs={{0,1},{1,0},{2,3},{3,2},{4,5},{5,4},{6,7},{7,6},{8,9},{9,8},{10,11... | collective-permute-start | bytes 2555912 | tf_op jit(solution)/shard_map/ppermute | solution.py:1311
  204.3 23.3 %collective-permute-start.24 = (bf16[4,416,128]{2,1,0:T(8,128)(2,1)S(1)}, bf16[4,416,128]{2,1,0:T(8,128)(2,1)S(1)}, u32[]{:S(2)}, u32[]{:S(2)}) collective-permute-start(bf16[4,416,128]{2,1,0:T(8,128)(2,1)S(1)} %add_convert_fusion.3), channel_id=1, source_target_pairs={{0,1},{1,0},{2,3},{3,2},{4,5},{5,4},{6,7},{7,6},{8,9},{9,8},{10,11... | collective-permute-start | bytes 1277960 | tf_op jit(solution)/shard_map/ppermute | solution.py:1311
  232.7 3.7 %collective-permute-start.25 = (bf16[8,416,128]{2,1,0:T(8,128)(2,1)}, bf16[8,416,128]{2,1,0:T(8,128)(2,1)}, u32[]{:S(2)}, u32[]{:S(2)}) collective-permute-start(bf16[8,416,128]{2,1,0:T(8,128)(2,1)} %get-tuple-element.338), channel_id=1, source_target_pairs={{0,16},{16,0},{1,17},{17,1},{2,18},{18,2},{3,19},{19,3},{4,20},{20... | collective-permute-start | bytes 2555912 | tf_op jit(solution)/shard_map/ppermute | solution.py:1297
  234.0 5.9 %collective-permute-start.28 = (bf16[2,416,128]{2,1,0:T(8,128)(2,1)S(1)}, bf16[2,416,128]{2,1,0:T(8,128)(2,1)S(1)}, u32[]{:S(2)}, u32[]{:S(2)}) collective-permute-start(bf16[2,416,128]{2,1,0:T(8,128)(2,1)S(1)} %add_convert_fusion.5), channel_id=1, source_target_pairs={{0,2},{1,3},{2,0},{3,1},{4,6},{5,7},{6,4},{7,5},{8,10},{9,11},{10,... | collective-permute-start | bytes 638984 | tf_op jit(solution)/shard_map/ppermute | solution.py:1311
  235.6 13.3 %collective-permute-start.32 = (bf16[4,416,128]{2,1,0:T(8,128)(2,1)S(1)}, bf16[4,416,128]{2,1,0:T(8,128)(2,1)S(1)}, u32[]{:S(2)}, u32[]{:S(2)}) collective-permute-start(bf16[4,416,128]{2,1,0:T(8,128)(2,1)S(1)} %add_convert_fusion.1), channel_id=1, source_target_pairs={{0,2},{1,3},{2,0},{3,1},{4,6},{5,7},{6,4},{7,5},{8,10},{9,11},{10,... | collective-permute-start | bytes 1277960 | tf_op jit(solution)/shard_map/ppermute | solution.py:1311
  237.5 14.0 %collective-permute-start.26 = (bf16[4,416,128]{2,1,0:T(8,128)(2,1)S(1)}, bf16[4,416,128]{2,1,0:T(8,128)(2,1)S(1)}, u32[]{:S(2)}, u32[]{:S(2)}) collective-permute-start(bf16[4,416,128]{2,1,0:T(8,128)(2,1)S(1)} %add_convert_fusion.2), channel_id=1, source_target_pairs={{0,1},{1,0},{2,3},{3,2},{4,5},{5,4},{6,7},{7,6},{8,9},{9,8},{10,11... | collective-permute-start | bytes 1277960 | tf_op jit(solution)/shard_map/ppermute | solution.py:1311
  248.9 15.7 %collective-permute-start.29 = (bf16[1,416,128]{2,1,0:T(8,128)(2,1)S(1)}, bf16[1,416,128]{2,1,0:T(8,128)(2,1)S(1)}, u32[]{:S(2)}, u32[]{:S(2)}) collective-permute-start(bf16[1,416,128]{2,1,0:T(8,128)(2,1)S(1)} %add_convert_fusion.9), channel_id=1, source_target_pairs={{0,4},{1,5},{2,6},{3,7},{4,0},{5,1},{6,2},{7,3},{8,12},{9,13},{10,... | collective-permute-start | bytes 319496 | tf_op jit(solution)/shard_map/ppermute | solution.py:1302
  252.6 5.9 %collective-permute-start.27 = (bf16[2,416,128]{2,1,0:T(8,128)(2,1)S(1)}, bf16[2,416,128]{2,1,0:T(8,128)(2,1)S(1)}, u32[]{:S(2)}, u32[]{:S(2)}) collective-permute-start(bf16[2,416,128]{2,1,0:T(8,128)(2,1)S(1)} %add_convert_fusion.6), channel_id=1, source_target_pairs={{0,2},{1,3},{2,0},{3,1},{4,6},{5,7},{6,4},{7,5},{8,10},{9,11},{10,... | collective-permute-start | bytes 638984 | tf_op jit(solution)/shard_map/ppermute | solution.py:1311
  254.0 8.2 %collective-permute-start.33 = (bf16[2,416,128]{2,1,0:T(8,128)(2,1)S(1)}, bf16[2,416,128]{2,1,0:T(8,128)(2,1)S(1)}, u32[]{:S(2)}, u32[]{:S(2)}) collective-permute-start(bf16[2,416,128]{2,1,0:T(8,128)(2,1)S(1)} %add_convert_fusion.4), channel_id=1, source_target_pairs={{0,4},{1,5},{2,6},{3,7},{4,0},{5,1},{6,2},{7,3},{8,12},{9,13},{10,... | collective-permute-start | bytes 638984 | tf_op jit(solution)/shard_map/ppermute | solution.py:1302
  259.5 5.2 %collective-permute-start.30 = (bf16[1,416,128]{2,1,0:T(8,128)(2,1)S(1)}, bf16[1,416,128]{2,1,0:T(8,128)(2,1)S(1)}, u32[]{:S(2)}, u32[]{:S(2)}) collective-permute-start(bf16[1,416,128]{2,1,0:T(8,128)(2,1)S(1)} %add_convert_fusion.8), channel_id=1, source_target_pairs={{0,4},{1,5},{2,6},{3,7},{4,0},{5,1},{6,2},{7,3},{8,12},{9,13},{10,... | collective-permute-start | bytes 319496 | tf_op jit(solution)/shard_map/ppermute | solution.py:1302
  262.3 8.8 %collective-permute-start.34 = (bf16[1,416,128]{2,1,0:T(8,128)(2,1)S(1)}, bf16[1,416,128]{2,1,0:T(8,128)(2,1)S(1)}, u32[]{:S(2)}, u32[]{:S(2)}) collective-permute-start(bf16[1,416,128]{2,1,0:T(8,128)(2,1)S(1)} %add_convert_fusion.7), channel_id=1, source_target_pairs={{0,8},{1,9},{2,10},{3,11},{4,12},{5,13},{6,14},{7,15},{8,0},{9,1},... | collective-permute-start | bytes 319496 | tf_op jit(solution)/shard_map/ppermute | solution.py:1302
  266.4 7.3 %collective-permute-start.31 = (bf16[416,128]{1,0:T(8,128)(2,1)S(1)}, bf16[416,128]{1,0:T(8,128)(2,1)S(1)}, u32[]{:S(2)}, u32[]{:S(2)}) collective-permute-start(bf16[416,128]{1,0:T(8,128)(2,1)S(1)} %get-tuple-element.367), channel_id=1, source_target_pairs={{0,8},{1,9},{2,10},{3,11},{4,12},{5,13},{6,14},{7,15},{8,0},{9,1},... | collective-permute-start | bytes 319496 | tf_op jit(solution)/shard_map/ppermute | solution.py:1302
  279.2 4.6 %collective-permute-start.36 = (f32[8,128]{1,0:T(8,128)S(1)}, f32[8,128]{1,0:T(8,128)S(1)}, u32[]{:S(2)}, u32[]{:S(2)}) collective-permute-start(f32[8,128]{1,0:T(8,128)S(1)} %add.204), channel_id=1, source_target_pairs={{0,1},{1,0},{2,3},{3,2},{4,5},{5,4},{6,7},{7,6},{8,9},{9,8},{10,11... | collective-permute-start | bytes 12296 | tf_op jit(solution)/shard_map/ppermute | solution.py:1302
  283.8 3.7 %collective-permute-start.38 = (f32[8,128]{1,0:T(8,128)S(1)}, f32[8,128]{1,0:T(8,128)S(1)}, u32[]{:S(2)}, u32[]{:S(2)}) collective-permute-start(f32[8,128]{1,0:T(8,128)S(1)} %add.205), channel_id=1, source_target_pairs={{0,2},{1,3},{2,0},{3,1},{4,6},{5,7},{6,4},{7,5},{8,10},{9,11},{10,... | collective-permute-start | bytes 12296 | tf_op jit(solution)/shard_map/ppermute | solution.py:1302
  291.1 4.5 %collective-permute-start.40 = (f32[8,128]{1,0:T(8,128)S(1)}, f32[8,128]{1,0:T(8,128)S(1)}, u32[]{:S(2)}, u32[]{:S(2)}) collective-permute-start(f32[8,128]{1,0:T(8,128)S(1)} %add.207), channel_id=1, source_target_pairs={{0,8},{1,9},{2,10},{3,11},{4,12},{5,13},{6,14},{7,15},{8,0},{9,1},... | collective-permute-start | bytes 12296 | tf_op jit(solution)/shard_map/ppermute | solution.py:1302
  (54 other events, 408.4 us)

commit v3 on v2

--- a/solution.py
+++ b/solution.py
@@ -741,7 +741,7 @@
     outs = attention + mlp
     flops = 2 * crops * tall * (4 * width * width + 2 * width * hidden)
     return pl.pallas_call(
-        functools.partial(block_kernel, pair, length, tall, 384),
+        functools.partial(block_kernel, pair, length, tall, 768),
         grid=(crops // pair,),
         out_shape=[shape for spec, shape in outs],
         in_specs=[pl.BlockSpec((pair, tall, width), lambda i: (i, 0, 0))]
@@ -782,7 +782,7 @@
         outs.append((fixed_spec(shape), jax.ShapeDtypeStruct(shape, bf16)))
     flops = 2 * flat * 2 * width * hidden
     return pl.pallas_call(
-        functools.partial(mlp_kernel, pair, tall, 384),
+        functools.partial(mlp_kernel, pair, tall, 768),
         grid=(crops // pair,),
         out_shape=[shape for spec, shape in outs],
         in_specs=[row_spec(rows, width), row_spec(rows, width)]
@@ -1262,7 +1262,7 @@
     outs = [token_out(crops, length, width, pair)] * 2
     outs += grad_outs(params, label, GRAD_MLP) + grad_outs(params, label, GRAD_ATTENTION)
     values = pl.pallas_call(
-        functools.partial(block_back_kernel, pair, tall, 384),
+        functools.partial(block_back_kernel, pair, tall, 768),
         grid=(crops // pair,),
         out_shape=[shape for spec, shape in outs],
         in_specs=[smem, token_spec]

time: 301 us -> 296 us (0.983)
  Pallas kernels: 172 us -> 167 us
    pallas_call x3, Pallas kernels: 51.8 us -> 47 us  [the longest x1 20.8 us: block_back(): pl.pallas_call(functools.partial(block_back_kernel, pair, tall, 768), gri...]
  transfers between devices with their start and end apart: 41 -> 41, of which waited for: 17 -> 17; matrix products, arithmetic and copies ran while one was open for 9% -> 9% of each run, Pallas kernels for 44% -> 43%
where the time goes in v3:
time: 296 us; the launch traced here: 295 us
  Pallas kernels  167 us (56%)
  waiting for transfers between devices  46.8 us (16%)
  starting transfers between devices  36.8 us (12%)
  local copies, waits for them, and re-layouts  26.4 us (9%)
  other arithmetic  15.8 us (5%)
  between operations  2.99 us (1%)
    ppermute x13, waiting for transfers between devices, partner(): return lax.ppermute(value, 'dp', [(i, i ^ bit) for i in range(count)])  29.4 us
    pallas_call x1, Pallas kernels, mlp_back(): pl.pallas_call(functools.partial(mlp_back_kernel, pair, tall, 768), grid=...  24.6 us
    pallas_call x1, Pallas kernels, attention_back(): pl.pallas_call(functools.partial(attention_back_kernel, pair, tall), grid...  24.6 us
    pallas_call x2, Pallas kernels, cross(): pl.pallas_call(functools.partial(cross_kernel, length, tall, crops), out_...  24.5 us
    pallas_call x1, Pallas kernels, block_back(): pl.pallas_call(functools.partial(block_back_kernel, pair, tall, 768), gri...  20.8 us
    ppermute x13, starting transfers between devices, partner(): return lax.ppermute(value, 'dp', [(i, i ^ bit) for i in range(count)])  20.8 us
    ppermute x10, waiting for transfers between devices, side_partner(): return lax.ppermute(value, ('branch', 'dp'), pairs)  14.7 us
    pallas_call x3, Pallas kernels, flatten(): pl.pallas_call(functools.partial(flatten_kernel, plan, group, owners.bit_...  14.3 us
  transfers between devices with their start and end apart: 41, of which 17 were waited for; matrix products, arithmetic and copies ran while one was open for 9% of the time, Pallas kernels for 43%

profile of v3, /device:TPU:0, one launch (start us, length us, event | category | flops | bytes accessed | tf_op | source)
XLA Modules:
  0.0 295.4 jit_solution(5287892496355903102)
XLA Ops:
  0.7 1.9 pad_bitcast_fusion.shard_ref
  4.5 2.3 align.1
  10.2 3.6 %collective-permute-start.1 = (bf16[1,416,128]{2,1,0:T(8,128)(2,1)S(1)}, bf16[1,416,128]{2,1,0:T(8,128)(2,1)S(1)}, u32[]{:S(2)}, u32[]{:S(2)}) collective-permute-start(bf16[1,416,128]{2,1,0:T(8,128)(2,1)S(1)} %get-tuple-element.370), channel_id=1, source_target_pairs={{0,8},{1,9},{2,10},{3,11},{4,12},{5,13},{6,14},{7,15},{8,0},{9,1},... | collective-permute-start | bytes 319496 | tf_op jit(solution)/shard_map/ppermute | solution.py:1302
  23.3 3.7 %collective-permute-done.2 = bf16[2,416,128]{2,1,0:T(8,128)(2,1)S(1)} collective-permute-done((bf16[2,416,128]{2,1,0:T(8,128)(2,1)S(1)}, bf16[2,416,128]{2,1,0:T(8,128)(2,1)S(1)}, u32[]{:S(2)}, u32[]{:S(2)}) %collective-permute-start.2) | collective-permute-done | bytes 213024 | tf_op jit(solution)/shard_map/ppermute | solution.py:1302
  28.4 2.7 collective-permute-start.3
  31.8 3.9 %collective-permute-done.3 = bf16[1,416,128]{2,1,0:T(8,128)(2,1)S(1)} collective-permute-done((bf16[1,416,128]{2,1,0:T(8,128)(2,1)S(1)}, bf16[1,416,128]{2,1,0:T(8,128)(2,1)S(1)}, u32[]{:S(2)}, u32[]{:S(2)}) %collective-permute-start.3) | collective-permute-done | bytes 106528 | tf_op jit(solution)/shard_map/ppermute | solution.py:1302
  38.3 5.9 %collective-permute-done.4 = bf16[2,416,128]{2,1,0:T(8,128)(2,1)S(1)} collective-permute-done((bf16[2,416,128]{2,1,0:T(8,128)(2,1)S(1)}, bf16[2,416,128]{2,1,0:T(8,128)(2,1)S(1)}, u32[]{:S(2)}, u32[]{:S(2)}) %collective-permute-start.4) | collective-permute-done | bytes 213024 | tf_op jit(solution)/shard_map/ppermute | solution.py:1302
  44.9 4.4 %collective-permute-done.6.refs_1_ = bf16[8,416,128]{2,1,0:T(8,128)(2,1)S(1)} collective-permute-done((bf16[8,416,128]{2,1,0:T(8,128)(2,1)S(1)}, bf16[8,416,128]{2,1,0:T(8,128)(2,1)S(1)}, u32[]{:S(2)}, u32[]{:S(2)}) %collective-permute-start.6) | collective-permute-done | bytes 852000 | tf_op jit(solution)/shard_map/ppermute | solution.py:1311
  52.8 4.9 %unflatten0.1 = (f32[2,192]{1,0:T(2,128)}, bf16[192,576]{1,0:T(8,128)(2,1)}, f32[1,576]{1,0:T(1,128)}, bf16[192,192]{1,0:T(8,128)(2,1)}, f32[1,192]{1,0:T(1,128)...) custom-call(s32[2]{0:T(128)} %pad_add_fusion.core_ref.where_ref, ...), custom_call_target="tpu_custom_call" | custom-call | flops 1000000 | bytes 8000000 | tf_op jit(solution)/shard_map/unflatten0/pallas_call | solution.py:484
  60.3 13.8 %block_s.1 = (bf16[1280,192]{1,0:T(8,128)(2,1)}, bf16[1280,576]{1,0:T(8,128)(2,1)}, bf16[8,6,160,160]{3,2,1,0:T(8,128)(2,1)}, bf16[1280,192]{1,0:T(8,128)(2,1)},...) custom-call(bf16[8,160,192]{2,1,0:T(8,128)(2,1)} %pad.19.tok_ref.ref, ...), custom_call_target="tpu_custom_call" | custom-call | flops 9059696640 | bytes 10000000 | tf_op jit(solution)/shard_map/block_s/pallas_call | solution.py:743
  74.2 14.2 %attention_l.1 = (bf16[1664,384]{1,0:T(8,128)(2,1)}, bf16[1664,1152]{1,0:T(8,128)(2,1)}, bf16[8,6,208,208]{3,2,1,0:T(8,128)(2,1)}, bf16[1664,384]{1,0:T(8,128)(2...) custom-call(bf16[8,208,384]{2,1,0:T(8,128)(2,1)} %pad.20.tok_ref.refs_0_, ...), custom_call_target="tpu_custom_call" | custom-call | flops 15703474176 | bytes 20000000 | tf_op jit(solution)/shard_map/attention_l/pallas_call | solution.py:760
  89.6 5.3 %unflatten1.1 = (f32[1,1536]{1,0:T(1,128)}, bf16[1536,384]{1,0:T(8,128)(2,1)}, f32[1,384]{1,0:T(1,128)}, f32[2,192]{1,0:T(2,128)}, bf16[192,384]{1,0:T(8,128)(2,...) custom-call(s32[2]{0:T(128)} %pad_add_fusion.core_ref.where_ref, ...), custom_call_target="tpu_custom_call" | custom-call | flops 1000000 | bytes 8000000 | tf_op jit(solution)/shard_map/unflatten1/pallas_call | solution.py:484
  94.9 12.4 %mlp_l.1 = (bf16[1664,1536]{1,0:T(8,128)(2,1)}, bf16[1664,1536]{1,0:T(8,128)(2,1)}, f32[1664,384]{1,0:T(8,128)}, f32[8,384]{1,0:T(8,128)}, bf16[8,192]{1,0:T(8,128)(2,1)}, /*index=5*/bf16[8,384]{1,0:T(8,128)(2,1)}) custom-call(f32[1664,384]{1,0:T(8,128)} %get-tuple-element.218.mid_ref.refs_3_, bf16[1664,384]{1,0:T(8,128)(2,1)} %get-tuple-element.219.n2_ref.refs_4_, ...), custom_call_target="tpu_custom_call" | custom-call | flops 31406948352 | bytes 20000000 | tf_op jit(solution)/shard_map/mlp_l/pallas_call | solution.py:784
  109.4 10.7 %cross_l.1 = (bf16[8,384]{1,0:T(8,128)(2,1)}, bf16[8,192]{1,0:T(8,128)(2,1)}, f32[1280,192]{1,0:T(8,128)}, f32[2,192]{1,0:T(2,128)}, f32[192,192]{1,0:T(8,128)},...) custom-call(bf16[8,192]{1,0:T(8,128)(2,1)} %copy-done.35, ...), custom_call_target="tpu_custom_call" | custom-call | flops 188743680 | bytes 8000000 | tf_op jit(solution)/shard_map/cross_l/pallas_call | solution.py:979
  121.0 13.8 %cross_s.1 = (bf16[8,192]{1,0:T(8,128)(2,1)}, bf16[8,384]{1,0:T(8,128)(2,1)}, f32[1664,384]{1,0:T(8,128)}, f32[2,384]{1,0:T(2,128)}, f32[384,384]{1,0:T(8,128)},...) custom-call(bf16[8,384]{1,0:T(8,128)(2,1)} %copy-done.34, ...), custom_call_target="tpu_custom_call" | custom-call | flops 981467136 | bytes 8000000 | tf_op jit(solution)/shard_map/cross_s/pallas_call | solution.py:979
  137.0 24.6 %mlp_back_l.1 = (bf16[1,8,197,384]{3,2,1,0:T(8,128)(2,1)}, f32[1664,384]{1,0:T(8,128)}, f32[8,192]{1,0:T(8,128)}, f32[2,384]{1,0:T(2,128)}, f32[384,1536]{1,0:T(...) custom-call(s32[1]{0:T(128)} %bitcast.15.live_ref, ...), custom_call_target="tpu_custom_call" | custom-call | flops 62813896704 | bytes 20000000 | tf_op jit(solution)/shard_map/mlp_back_l/pallas_call | solution.py:1204
  161.5 5.9 %flatten2.1 = (bf16[8,416,128]{2,1,0:T(8,128)(2,1)}, bf16[8,416,128]{2,1,0:T(8,128)(2,1)}, bf16[16,416,128]{2,1,0:T(8,128)(2,1)}) custom-call(s32[2]{0:T(128)} %pad_add_fusion.core_ref.where_ref, s32[32]{0:T(128)} %constant.54.clone.base_ref, f32[1,1536]{1,0:T(1,128)} %get-tuple-element.270.refs_0_.refs_6_, f32[1536,384]{1,0:T(8,128)} %get-tuple-element.271.refs_1_, ...), custom_call_target="tpu_custom_call" | custom-call | flops 1000000 | bytes 10000000 | tf_op jit(solution)/shard_map/flatten2/pallas_call | solution.py:538
  167.8 24.6 %attention_back_l.1 = (bf16[1,8,197,384]{3,2,1,0:T(8,128)(2,1)}, f32[2,384]{1,0:T(2,128)}, f32[384,1152]{1,0:T(8,128)}, f32[1,1152]{1,0:T(1,128)}, f32[384,384]{1,0:T(8,128)}, /*index=5*/f32[1,384]{1,0:T(1,128)}) custom-call(f32[1664,384]{1,0:T(8,128)} %get-tuple-element.302.gmid_ref, bf16[8,208,384]{2,1,0:T(8,128)(2,1)} %pad.20.tok_ref.refs_0_, ...), custom_call_target="tpu_custom_call" | custom-call | flops 31406948352 | bytes 20000000 | tf_op jit(solution)/shard_map/attention_back_l/pallas_call | solution.py:1233
  192.3 4.0 %flatten1.1 = (bf16[4,416,128]{2,1,0:T(8,128)(2,1)}, bf16[4,416,128]{2,1,0:T(8,128)(2,1)}, bf16[8,416,128]{2,1,0:T(8,128)(2,1)}) custom-call(s32[2]{0:T(128)} %pad_add_fusion.core_ref.where_ref, s32[32]{0:T(128)} %constant.54.clone.base_ref, f32[384,1152]{1,0:T(8,128)} %get-tuple-element.310.refs_0_.refs_11_, f32[1,1152]{1,0:T(1,128)} %get-tuple-element.311.refs_1_, ...), custom_call_target="tpu_custom_call" | custom-call | flops 1000000 | bytes 10000000 | tf_op jit(solution)/shard_map/flatten1/pallas_call | solution.py:538
  202.0 20.8 %block_back_s.1 = (bf16[1,8,145,192]{3,2,1,0:T(8,128)(2,1)}, bf16[1,8,145,192]{3,2,1,0:T(8,128)(2,1)}, f32[2,192]{1,0:T(2,128)}, f32[192,768]{1,0:T(8,128)}, f32...) custom-call(s32[1]{0:T(128)} %bitcast.2.live_ref, ...), custom_call_target="tpu_custom_call" | custom-call | flops 18119393280 | bytes 20000000 | tf_op jit(solution)/shard_map/block_back_s/pallas_call | solution.py:1264
  223.6 4.3 %flatten0.1 = (bf16[4,416,128]{2,1,0:T(8,128)(2,1)}, bf16[4,416,128]{2,1,0:T(8,128)(2,1)}, bf16[8,416,128]{2,1,0:T(8,128)(2,1)}) custom-call(s32[2]{0:T(128)} %pad_add_fusion.core_ref.where_ref, s32[32]{0:T(128)} %constant.54.clone.base_ref, f32[2,192]{1,0:T(2,128)} %get-tuple-element.326.refs_0_, f32[192,576]{1,0:T(8,128)} %get-tuple-element.327.refs_1_, ...), custom_call_target="tpu_custom_call" | custom-call | flops 1000000 | bytes 10000000 | tf_op jit(solution)/shard_map/flatten0/pallas_call | solution.py:538
  236.1 8.0 %collective-permute-done.32.refs_3_ = bf16[4,416,128]{2,1,0:T(8,128)(2,1)S(1)} collective-permute-done((bf16[4,416,128]{2,1,0:T(8,128)(2,1)S(1)}, bf16[4,416,128]{2,1,0:T(8,128)(2,1)S(1)}, u32[]{:S(2)}, u32[]{:S(2)}) %collective-permute-start.32) | collective-permute-done | bytes 426016 | tf_op jit(solution)/shard_map/ppermute | solution.py:1311
  257.6 2.2 collective-permute-start.34
  259.8 1.8 fusion.1
  261.5 3.1 %collective-permute-start.31 = (bf16[416,128]{1,0:T(8,128)(2,1)S(1)}, bf16[416,128]{1,0:T(8,128)(2,1)S(1)}, u32[]{:S(2)}, u32[]{:S(2)}) collective-permute-start(bf16[416,128]{1,0:T(8,128)(2,1)S(1)} %get-tuple-element.367), channel_id=1, source_target_pairs={{0,8},{1,9},{2,10},{3,11},{4,12},{5,13},{6,14},{7,15},{8,0},{9,1},... | collective-permute-start | bytes 319496 | tf_op jit(solution)/shard_map/ppermute | solution.py:1302
  266.3 2.6 collective-permute-done.31.last_ref
  269.6 2.5 settle.1
  276.3 2.6 unalign.1
  280.1 2.5 collective-permute-done.38
  282.6 3.6 %collective-permute-done.39 = f32[8,128]{1,0:T(8,128)S(1)} collective-permute-done((f32[8,128]{1,0:T(8,128)S(1)}, f32[8,128]{1,0:T(8,128)S(1)}, u32[]{:S(2)}, u32[]{:S(2)}) %collective-permute-start.39) | collective-permute-done | bytes 4128 | tf_op jit(solution)/shard_map/ppermute | solution.py:1302
  287.9 2.8 collective-permute-done.40
  292.0 2.3 fusion.5
  (203 shorter events, 70.7 us)
Async XLA Ops:
  10.2 9.6 %collective-permute-start.1 = (bf16[1,416,128]{2,1,0:T(8,128)(2,1)S(1)}, bf16[1,416,128]{2,1,0:T(8,128)(2,1)S(1)}, u32[]{:S(2)}, u32[]{:S(2)}) collective-permute-start(bf16[1,416,128]{2,1,0:T(8,128)(2,1)S(1)} %get-tuple-element.370), channel_id=1, source_target_pairs={{0,8},{1,9},{2,10},{3,11},{4,12},{5,13},{6,14},{7,15},{8,0},{9,1},... | collective-permute-start | bytes 319496 | tf_op jit(solution)/shard_map/ppermute | solution.py:1302
  19.8 7.2 %collective-permute-start.2 = (bf16[2,416,128]{2,1,0:T(8,128)(2,1)S(1)}, bf16[2,416,128]{2,1,0:T(8,128)(2,1)S(1)}, u32[]{:S(2)}, u32[]{:S(2)}) collective-permute-start(bf16[2,416,128]{2,1,0:T(8,128)(2,1)S(1)} %pad_maximum_fusion.2), channel_id=1, source_target_pairs={{0,4},{1,5},{2,6},{3,7},{4,0},{5,1},{6,2},{7,3},{8,12},{9,13},{10,... | collective-permute-start | bytes 638984 | tf_op jit(solution)/shard_map/ppermute | solution.py:1302
  27.0 9.4 %collective-permute-start.5 = (bf16[4,416,128]{2,1,0:T(8,128)(2,1)S(1)}, bf16[4,416,128]{2,1,0:T(8,128)(2,1)S(1)}, u32[]{:S(2)}, u32[]{:S(2)}) collective-permute-start(bf16[4,416,128]{2,1,0:T(8,128)(2,1)S(1)} %pad_maximum_fusion.1), channel_id=1, source_target_pairs={{0,2},{1,3},{2,0},{3,1},{4,6},{5,7},{6,4},{7,5},{8,10},{9,11},{10,... | collective-permute-start | bytes 1277960 | tf_op jit(solution)/shard_map/ppermute | solution.py:1311
  28.4 7.3 %collective-permute-start.3 = (bf16[1,416,128]{2,1,0:T(8,128)(2,1)S(1)}, bf16[1,416,128]{2,1,0:T(8,128)(2,1)S(1)}, u32[]{:S(2)}, u32[]{:S(2)}) collective-permute-start(bf16[1,416,128]{2,1,0:T(8,128)(2,1)S(1)} %get-tuple-element.194), channel_id=1, source_target_pairs={{0,8},{1,9},{2,10},{3,11},{4,12},{5,13},{6,14},{7,15},{8,0},{9,1},... | collective-permute-start | bytes 319496 | tf_op jit(solution)/shard_map/ppermute | solution.py:1302
  36.5 12.8 %collective-permute-start.6 = (bf16[8,416,128]{2,1,0:T(8,128)(2,1)S(1)}, bf16[8,416,128]{2,1,0:T(8,128)(2,1)S(1)}, u32[]{:S(2)}, u32[]{:S(2)}) collective-permute-start(bf16[8,416,128]{2,1,0:T(8,128)(2,1)S(1)} %pad_maximum_fusion.refs_0_), channel_id=1, source_target_pairs={{0,1},{1,0},{2,3},{3,2},{4,5},{5,4},{6,7},{7,6},{8,9},{9,8},{10,11... | collective-permute-start | bytes 2555912 | tf_op jit(solution)/shard_map/ppermute | solution.py:1311
  37.5 6.7 %collective-permute-start.4 = (bf16[2,416,128]{2,1,0:T(8,128)(2,1)S(1)}, bf16[2,416,128]{2,1,0:T(8,128)(2,1)S(1)}, u32[]{:S(2)}, u32[]{:S(2)}) collective-permute-start(bf16[2,416,128]{2,1,0:T(8,128)(2,1)S(1)} %get-tuple-element.371), channel_id=1, source_target_pairs={{0,4},{1,5},{2,6},{3,7},{4,0},{5,1},{6,2},{7,3},{8,12},{9,13},{10,... | collective-permute-start | bytes 638984 | tf_op jit(solution)/shard_map/ppermute | solution.py:1302
  44.9 7.0 %collective-permute-start.8 = (bf16[8,416,128]{2,1,0:T(8,128)(2,1)S(1)}, bf16[8,416,128]{2,1,0:T(8,128)(2,1)S(1)}, u32[]{:S(2)}, u32[]{:S(2)}) collective-permute-start(bf16[8,416,128]{2,1,0:T(8,128)(2,1)S(1)} %pad_maximum_fusion.refs_0_), channel_id=1, source_target_pairs={{0,16},{16,0},{1,17},{17,1},{2,18},{18,2},{3,19},{19,3},{4,20},{20... | collective-permute-start | bytes 2555912 | tf_op jit(solution)/shard_map/ppermute | solution.py:1297
  49.3 8.4 %collective-permute-start.7 = (bf16[4,416,128]{2,1,0:T(8,128)(2,1)}, bf16[4,416,128]{2,1,0:T(8,128)(2,1)}, u32[]{:S(2)}, u32[]{:S(2)}) collective-permute-start(bf16[4,416,128]{2,1,0:T(8,128)(2,1)} %constant_dynamic-update-slice_fusion.2), channel_id=1, source_target_pairs={{0,2},{1,3},{2,0},{3,1},{4,6},{5,7},{6,4},{7,5},{8,10},{9,11},{10,... | collective-permute-start | bytes 1277960 | tf_op jit(solution)/shard_map/ppermute | solution.py:1311
  58.8 15.3 %collective-permute-start.10 = (bf16[8,416,128]{2,1,0:T(8,128)(2,1)S(1)}, bf16[8,416,128]{2,1,0:T(8,128)(2,1)S(1)}, u32[]{:S(2)}, u32[]{:S(2)}) collective-permute-start(bf16[8,416,128]{2,1,0:T(8,128)(2,1)S(1)} %constant_dynamic-update-slice_fusion.5.refs_0_), channel_id=1, source_target_pairs={{0,1},{1,0},{2,3},{3,2},{4,5},{5,4},{6,7},{7,6},{8,9},{9,8},{10,11... | collective-permute-start | bytes 2555912 | tf_op jit(solution)/shard_map/ppermute | solution.py:1311
  59.8 48.5 %collective-permute-start.14 = (bf16[8,384]{1,0:T(8,128)(2,1)S(1)}, bf16[8,384]{1,0:T(8,128)(2,1)S(1)}, u32[]{:S(2)}, u32[]{:S(2)}) collective-permute-start(bf16[8,384]{1,0:T(8,128)(2,1)S(1)} %bitcast_select_fusion), channel_id=1, source_target_pairs={{0,16},{16,0},{1,17},{17,1},{2,18},{18,2},{3,19},{19,3},{4,20},{20... | collective-permute-start | bytes 18440 | tf_op jit(solution)/shard_map/ppermute | solution.py:1297
  59.8 28.6 %collective-permute-start.11 = (bf16[8,416,128]{2,1,0:T(8,128)(2,1)S(1)}, bf16[8,416,128]{2,1,0:T(8,128)(2,1)S(1)}, u32[]{:S(2)}, u32[]{:S(2)}) collective-permute-start(bf16[8,416,128]{2,1,0:T(8,128)(2,1)S(1)} %constant_dynamic-update-slice_fusion.5.refs_0_), channel_id=1, source_target_pairs={{0,16},{16,0},{1,17},{17,1},{2,18},{18,2},{3,19},{19,3},{4,20},{20... | collective-permute-start | bytes 2555912 | tf_op jit(solution)/shard_map/ppermute | solution.py:1297
  74.1 14.4 %collective-permute-start.12 = (bf16[8,416,128]{2,1,0:T(8,128)(2,1)S(1)}, bf16[8,416,128]{2,1,0:T(8,128)(2,1)S(1)}, u32[]{:S(2)}, u32[]{:S(2)}) collective-permute-start(bf16[8,416,128]{2,1,0:T(8,128)(2,1)S(1)} %collective-permute-done.10.refs_1_), channel_id=1, source_target_pairs={{0,16},{16,0},{1,17},{17,1},{2,18},{18,2},{3,19},{19,3},{4,20},{20... | collective-permute-start | bytes 2555912 | tf_op jit(solution)/shard_map/ppermute | solution.py:1297
  107.7 12.7 %collective-permute-start.16 = (bf16[8,192]{1,0:T(8,128)(2,1)S(1)}, bf16[8,192]{1,0:T(8,128)(2,1)S(1)}, u32[]{:S(2)}, u32[]{:S(2)}) collective-permute-start(bf16[8,192]{1,0:T(8,128)(2,1)S(1)} %bitcast_select_fusion.1), channel_id=1, source_target_pairs={{0,16},{16,0},{1,17},{17,1},{2,18},{18,2},{3,19},{19,3},{4,20},{20... | collective-permute-start | bytes 9224 | tf_op jit(solution)/shard_map/ppermute | solution.py:1297
  107.9 12.5 %collective-permute-start.15 = (bf16[8,384]{1,0:T(8,128)(2,1)}, bf16[8,384]{1,0:T(8,128)(2,1)S(1)}, u32[]{:S(2)}, u32[]{:S(2)}) collective-permute-start(bf16[8,384]{1,0:T(8,128)(2,1)} %get-tuple-element.250), channel_id=1, source_target_pairs={{0,16},{16,0},{1,17},{17,1},{2,18},{18,2},{3,19},{19,3},{4,20},{20... | collective-permute-start | bytes 18440 | tf_op jit(solution)/shard_map/ppermute | solution.py:1297
  120.1 16.3 %collective-permute-start.17 = (bf16[8,384]{1,0:T(8,128)(2,1)}, bf16[8,384]{1,0:T(8,128)(2,1)S(1)}, u32[]{:S(2)}, u32[]{:S(2)}) collective-permute-start(bf16[8,384]{1,0:T(8,128)(2,1)} %get-tuple-element.265), channel_id=1, source_target_pairs={{0,16},{16,0},{1,17},{17,1},{2,18},{18,2},{3,19},{19,3},{4,20},{20... | collective-permute-start | bytes 18440 | tf_op jit(solution)/shard_map/ppermute | solution.py:1297
  167.4 29.5 %collective-permute-start.20 = (bf16[16,416,128]{2,1,0:T(8,128)(2,1)}, bf16[16,416,128]{2,1,0:T(8,128)(2,1)S(1)}, u32[]{:S(2)}, u32[]{:S(2)}) collective-permute-start(bf16[16,416,128]{2,1,0:T(8,128)(2,1)} %get-tuple-element.308), channel_id=1, source_target_pairs={{0,16},{16,0},{1,17},{17,1},{2,18},{18,2},{3,19},{19,3},{4,20},{20... | collective-permute-start | bytes 5111816 | tf_op jit(solution)/shard_map/ppermute | solution.py:1297
  196.6 4.7 %collective-permute-start.22 = (bf16[8,192]{1,0:T(8,128)(2,1)S(1)}, bf16[8,192]{1,0:T(8,128)(2,1)S(1)}, u32[]{:S(2)}, u32[]{:S(2)}) collective-permute-start(bf16[8,192]{1,0:T(8,128)(2,1)S(1)} %copy-done.41), channel_id=1, source_target_pairs={{0,16},{16,0},{1,17},{17,1},{2,18},{18,2},{3,19},{19,3},{4,20},{20... | collective-permute-start | bytes 9224 | tf_op jit(solution)/shard_map/ppermute | solution.py:1297
  198.2 24.6 %collective-permute-start.23 = (bf16[8,416,128]{2,1,0:T(8,128)(2,1)}, bf16[8,416,128]{2,1,0:T(8,128)(2,1)S(1)}, u32[]{:S(2)}, u32[]{:S(2)}) collective-permute-start(bf16[8,416,128]{2,1,0:T(8,128)(2,1)} %add_convert_fusion), channel_id=1, source_target_pairs={{0,1},{1,0},{2,3},{3,2},{4,5},{5,4},{6,7},{7,6},{8,9},{9,8},{10,11... | collective-permute-start | bytes 2555912 | tf_op jit(solution)/shard_map/ppermute | solution.py:1311
  200.4 22.3 %collective-permute-start.24 = (bf16[4,416,128]{2,1,0:T(8,128)(2,1)S(1)}, bf16[4,416,128]{2,1,0:T(8,128)(2,1)S(1)}, u32[]{:S(2)}, u32[]{:S(2)}) collective-permute-start(bf16[4,416,128]{2,1,0:T(8,128)(2,1)S(1)} %add_convert_fusion.3), channel_id=1, source_target_pairs={{0,1},{1,0},{2,3},{3,2},{4,5},{5,4},{6,7},{7,6},{8,9},{9,8},{10,11... | collective-permute-start | bytes 1277960 | tf_op jit(solution)/shard_map/ppermute | solution.py:1311
  227.9 3.7 %collective-permute-start.25 = (bf16[8,416,128]{2,1,0:T(8,128)(2,1)}, bf16[8,416,128]{2,1,0:T(8,128)(2,1)}, u32[]{:S(2)}, u32[]{:S(2)}) collective-permute-start(bf16[8,416,128]{2,1,0:T(8,128)(2,1)} %get-tuple-element.338), channel_id=1, source_target_pairs={{0,16},{16,0},{1,17},{17,1},{2,18},{18,2},{3,19},{19,3},{4,20},{20... | collective-permute-start | bytes 2555912 | tf_op jit(solution)/shard_map/ppermute | solution.py:1297
  229.2 5.9 %collective-permute-start.28 = (bf16[2,416,128]{2,1,0:T(8,128)(2,1)S(1)}, bf16[2,416,128]{2,1,0:T(8,128)(2,1)S(1)}, u32[]{:S(2)}, u32[]{:S(2)}) collective-permute-start(bf16[2,416,128]{2,1,0:T(8,128)(2,1)S(1)} %add_convert_fusion.5), channel_id=1, source_target_pairs={{0,2},{1,3},{2,0},{3,1},{4,6},{5,7},{6,4},{7,5},{8,10},{9,11},{10,... | collective-permute-start | bytes 638984 | tf_op jit(solution)/shard_map/ppermute | solution.py:1311
  230.8 13.3 %collective-permute-start.32 = (bf16[4,416,128]{2,1,0:T(8,128)(2,1)S(1)}, bf16[4,416,128]{2,1,0:T(8,128)(2,1)S(1)}, u32[]{:S(2)}, u32[]{:S(2)}) collective-permute-start(bf16[4,416,128]{2,1,0:T(8,128)(2,1)S(1)} %add_convert_fusion.1), channel_id=1, source_target_pairs={{0,2},{1,3},{2,0},{3,1},{4,6},{5,7},{6,4},{7,5},{8,10},{9,11},{10,... | collective-permute-start | bytes 1277960 | tf_op jit(solution)/shard_map/ppermute | solution.py:1311
  232.7 14.0 %collective-permute-start.26 = (bf16[4,416,128]{2,1,0:T(8,128)(2,1)S(1)}, bf16[4,416,128]{2,1,0:T(8,128)(2,1)S(1)}, u32[]{:S(2)}, u32[]{:S(2)}) collective-permute-start(bf16[4,416,128]{2,1,0:T(8,128)(2,1)S(1)} %add_convert_fusion.2), channel_id=1, source_target_pairs={{0,1},{1,0},{2,3},{3,2},{4,5},{5,4},{6,7},{7,6},{8,9},{9,8},{10,11... | collective-permute-start | bytes 1277960 | tf_op jit(solution)/shard_map/ppermute | solution.py:1311
  244.1 15.7 %collective-permute-start.29 = (bf16[1,416,128]{2,1,0:T(8,128)(2,1)S(1)}, bf16[1,416,128]{2,1,0:T(8,128)(2,1)S(1)}, u32[]{:S(2)}, u32[]{:S(2)}) collective-permute-start(bf16[1,416,128]{2,1,0:T(8,128)(2,1)S(1)} %add_convert_fusion.9), channel_id=1, source_target_pairs={{0,4},{1,5},{2,6},{3,7},{4,0},{5,1},{6,2},{7,3},{8,12},{9,13},{10,... | collective-permute-start | bytes 319496 | tf_op jit(solution)/shard_map/ppermute | solution.py:1302
  247.8 5.9 %collective-permute-start.27 = (bf16[2,416,128]{2,1,0:T(8,128)(2,1)S(1)}, bf16[2,416,128]{2,1,0:T(8,128)(2,1)S(1)}, u32[]{:S(2)}, u32[]{:S(2)}) collective-permute-start(bf16[2,416,128]{2,1,0:T(8,128)(2,1)S(1)} %add_convert_fusion.6), channel_id=1, source_target_pairs={{0,2},{1,3},{2,0},{3,1},{4,6},{5,7},{6,4},{7,5},{8,10},{9,11},{10,... | collective-permute-start | bytes 638984 | tf_op jit(solution)/shard_map/ppermute | solution.py:1311
  249.3 8.2 %collective-permute-start.33 = (bf16[2,416,128]{2,1,0:T(8,128)(2,1)S(1)}, bf16[2,416,128]{2,1,0:T(8,128)(2,1)S(1)}, u32[]{:S(2)}, u32[]{:S(2)}) collective-permute-start(bf16[2,416,128]{2,1,0:T(8,128)(2,1)S(1)} %add_convert_fusion.4), channel_id=1, source_target_pairs={{0,4},{1,5},{2,6},{3,7},{4,0},{5,1},{6,2},{7,3},{8,12},{9,13},{10,... | collective-permute-start | bytes 638984 | tf_op jit(solution)/shard_map/ppermute | solution.py:1302
  254.7 5.1 %collective-permute-start.30 = (bf16[1,416,128]{2,1,0:T(8,128)(2,1)S(1)}, bf16[1,416,128]{2,1,0:T(8,128)(2,1)S(1)}, u32[]{:S(2)}, u32[]{:S(2)}) collective-permute-start(bf16[1,416,128]{2,1,0:T(8,128)(2,1)S(1)} %add_convert_fusion.8), channel_id=1, source_target_pairs={{0,4},{1,5},{2,6},{3,7},{4,0},{5,1},{6,2},{7,3},{8,12},{9,13},{10,... | collective-permute-start | bytes 319496 | tf_op jit(solution)/shard_map/ppermute | solution.py:1302
  257.6 8.8 %collective-permute-start.34 = (bf16[1,416,128]{2,1,0:T(8,128)(2,1)S(1)}, bf16[1,416,128]{2,1,0:T(8,128)(2,1)S(1)}, u32[]{:S(2)}, u32[]{:S(2)}) collective-permute-start(bf16[1,416,128]{2,1,0:T(8,128)(2,1)S(1)} %add_convert_fusion.7), channel_id=1, source_target_pairs={{0,8},{1,9},{2,10},{3,11},{4,12},{5,13},{6,14},{7,15},{8,0},{9,1},... | collective-permute-start | bytes 319496 | tf_op jit(solution)/shard_map/ppermute | solution.py:1302
  261.5 7.4 %collective-permute-start.31 = (bf16[416,128]{1,0:T(8,128)(2,1)S(1)}, bf16[416,128]{1,0:T(8,128)(2,1)S(1)}, u32[]{:S(2)}, u32[]{:S(2)}) collective-permute-start(bf16[416,128]{1,0:T(8,128)(2,1)S(1)} %get-tuple-element.367), channel_id=1, source_target_pairs={{0,8},{1,9},{2,10},{3,11},{4,12},{5,13},{6,14},{7,15},{8,0},{9,1},... | collective-permute-start | bytes 319496 | tf_op jit(solution)/shard_map/ppermute | solution.py:1302
  274.4 4.5 %collective-permute-start.36 = (f32[8,128]{1,0:T(8,128)S(1)}, f32[8,128]{1,0:T(8,128)S(1)}, u32[]{:S(2)}, u32[]{:S(2)}) collective-permute-start(f32[8,128]{1,0:T(8,128)S(1)} %add.204), channel_id=1, source_target_pairs={{0,1},{1,0},{2,3},{3,2},{4,5},{5,4},{6,7},{7,6},{8,9},{9,8},{10,11... | collective-permute-start | bytes 12296 | tf_op jit(solution)/shard_map/ppermute | solution.py:1302
  278.9 3.7 %collective-permute-start.38 = (f32[8,128]{1,0:T(8,128)S(1)}, f32[8,128]{1,0:T(8,128)S(1)}, u32[]{:S(2)}, u32[]{:S(2)}) collective-permute-start(f32[8,128]{1,0:T(8,128)S(1)} %add.205), channel_id=1, source_target_pairs={{0,2},{1,3},{2,0},{3,1},{4,6},{5,7},{6,4},{7,5},{8,10},{9,11},{10,... | collective-permute-start | bytes 12296 | tf_op jit(solution)/shard_map/ppermute | solution.py:1302
  286.2 4.5 %collective-permute-start.40 = (f32[8,128]{1,0:T(8,128)S(1)}, f32[8,128]{1,0:T(8,128)S(1)}, u32[]{:S(2)}, u32[]{:S(2)}) collective-permute-start(f32[8,128]{1,0:T(8,128)S(1)} %add.207), channel_id=1, source_target_pairs={{0,8},{1,9},{2,10},{3,11},{4,12},{5,13},{6,14},{7,15},{8,0},{9,1},... | collective-permute-start | bytes 12296 | tf_op jit(solution)/shard_map/ppermute | solution.py:1302
  (54 other events, 406.6 us)
